TPU v7x, 32 devices: a whole 2x2x4 slice. The times are simulated.
32 devices in a mesh: wide: 8 (over z, y), narrow: 4 (over x, core).
Axes of the slice: x: 2, y: 2, z: 4, core: 2. Of those that a mesh axis runs over, the one named last changes fastest.
Arguments:
- images: bfloat16 [1088, 50, 512], P(('wide', 'narrow')), may hold values from -6 to 6
- cotangent: bfloat16 [1088, 50, 512], P(('wide', 'narrow')), may hold values from -24 to 24
- counts: int32 [32], P(('wide', 'narrow')), may hold values from 1 to 34, as said below
- in_mats: float32 [512, 4096], P(('wide', 'narrow')), may hold values from -0.25 to 0.25
- in_mats_m: float32 [512, 4096], P(('wide', 'narrow')), may hold values from -0.00036621094 to 0.00036621094
- in_mats_v: float32 [512, 4096], P(('wide', 'narrow')), may hold values from 3.1789144e-10 to 1.2715657e-09
- out_mat: float32 [2048, 512], P(('wide', 'narrow')), may hold values from -0.125 to 0.125
- out_mat_m: float32 [2048, 512], P(('wide', 'narrow')), may hold values from -0.00036621094 to 0.00036621094
- out_mat_v: float32 [2048, 512], P(('wide', 'narrow')), may hold values from 3.1789144e-10 to 1.2715657e-09
- kernels: float32 [58, 512], P(None, ('wide', 'narrow')), may hold values from -1 to 1
- kernels_m: float32 [58, 512], P(None, ('wide', 'narrow')), may hold values from -0.0009765625 to 0.0009765625
- kernels_v: float32 [58, 512], P(None, ('wide', 'narrow')), may hold values from 2.861023e-09 to 1.1444092e-08
- gains: float32 [2, 512], P(None, ('wide', 'narrow')), may hold values from 0.8 to 5, as said below
- gains_m: float32 [2, 512], P(None, ('wide', 'narrow')), may hold values from -0.0009765625 to 0.0009765625
- gains_v: float32 [2, 512], P(None, ('wide', 'narrow')), may hold values from 2.861023e-09 to 1.1444092e-08
- biases: float32 [12, 512], P(None, ('wide', 'narrow')), may hold values from -1.25 to 1.25
- biases_m: float32 [12, 512], P(None, ('wide', 'narrow')), may hold values from -0.0009765625 to 0.0009765625
- biases_v: float32 [12, 512], P(None, ('wide', 'narrow')), may hold values from 2.861023e-09 to 1.1444092e-08
Outputs:
- block_out: bfloat16 [1088, 50, 512], P(('wide', 'narrow'))
- input_grad: float32 [1088, 50, 512], P(('wide', 'narrow'))
- grad_norm: float32 [], replicated
- in_mats_new: float32 [512, 4096], P(('wide', 'narrow'))
- in_mats_m_new: float32 [512, 4096], P(('wide', 'narrow'))
- in_mats_v_new: float32 [512, 4096], P(('wide', 'narrow'))
- in_mats_low: bfloat16 [512, 4096], P(('wide', 'narrow'))
- out_mat_new: float32 [2048, 512], P(('wide', 'narrow'))
- out_mat_m_new: float32 [2048, 512], P(('wide', 'narrow'))
- out_mat_v_new: float32 [2048, 512], P(('wide', 'narrow'))
- out_mat_low: bfloat16 [2048, 512], P(('wide', 'narrow'))
- kernels_new: float32 [58, 512], P(None, ('wide', 'narrow'))
- kernels_m_new: float32 [58, 512], P(None, ('wide', 'narrow'))
- kernels_v_new: float32 [58, 512], P(None, ('wide', 'narrow'))
- kernels_low: bfloat16 [58, 512], P(None, ('wide', 'narrow'))
- gains_new: float32 [2, 512], P(None, ('wide', 'narrow'))
- gains_m_new: float32 [2, 512], P(None, ('wide', 'narrow'))
- gains_v_new: float32 [2, 512], P(None, ('wide', 'narrow'))
- gains_low: bfloat16 [2, 512], P(None, ('wide', 'narrow'))
- biases_new: float32 [12, 512], P(None, ('wide', 'narrow'))
- biases_m_new: float32 [12, 512], P(None, ('wide', 'narrow'))
- biases_v_new: float32 [12, 512], P(None, ('wide', 'narrow'))
- biases_low: bfloat16 [12, 512], P(None, ('wide', 'narrow'))
Inputs may be any that keep to these rules, and one draw needn't show every extreme that they name: Each device holds counts[d] live images in its first slots; some device is full. `gains`: gains are positive.
All inputs are finite; a program needn't handle non-finite values.
Results may differ from a plain program's by a relative error of at most 0.012.
Values may be sent and summed in bfloat16 or wider, within the bound.
A program may use at most 512 MiB of HBM per device.

v0:
```python
import jax
import jax.numpy as jnp
from jax import lax
from jax.sharding import PartitionSpec as P

D = 512
HEADS = 8
MLP_WIDTH = 2048
GRID = 7
STEP = 10
BROWS = 12


NORM_EPS = 1e-06
BETA_ONE = 0.9
BETA_TWO = 0.999
ADAM_EPS = 1e-08
HIGHEST = lax.Precision.HIGHEST
RATES = (0.04, 0.02, 0.1, 0.8, 0.25)
DECAYS = (0.05, 0.05, 0.05, 0.0, 0.0)


def layer_norm(values, gain_row, shift_row):
    centred = values - jnp.mean(values, axis=-1, keepdims=True)
    variance = jnp.mean(centred * centred, axis=-1, keepdims=True)
    return centred * lax.rsqrt(variance + NORM_EPS) * gain_row + shift_row


def depthwise(patch_grid, taps, kernel_width):
    margin = kernel_width // 2
    padded = jnp.pad(patch_grid, ((0, 0), (margin, margin), (margin, margin), (0, 0)))
    summed_taps = jnp.zeros_like(patch_grid)
    for row_tap in range(kernel_width):
        for col_tap in range(kernel_width):
            window = padded[:, row_tap : row_tap + GRID, col_tap : col_tap + GRID, :]
            summed_taps = summed_taps + window * taps[row_tap * kernel_width + col_tap]
    return summed_taps


def tap_mask(channels):
    head_width = channels // HEADS
    channel_ids = jnp.arange(channels, dtype=jnp.int32)
    reach_cells = jnp.where(
        channel_ids < 2 * head_width, 1, jnp.where(channel_ids < 5 * head_width, 2, 3)
    )
    tap_ids = jnp.arange(49, dtype=jnp.int32)
    row_offset = jnp.abs(tap_ids // 7 - 3)
    col_offset = jnp.abs(tap_ids % 7 - 3)
    inside = (row_offset[:, None] <= reach_cells[None, :]) & (
        col_offset[:, None] <= reach_cells[None, :]
    )
    return inside.astype(jnp.float32)


def pre_block(inputs, cpe_taps, cpe_shift, gain_row, shift_row):
    num_images, num_tokens, channels = inputs.shape
    patches = inputs[:, 1:].reshape(num_images, GRID, GRID, channels)
    mixed = patches + depthwise(patches, cpe_taps, 3) + cpe_shift
    after_cpe = jnp.concatenate(
        [inputs[:, :1], mixed.reshape(num_images, GRID * GRID, channels)], axis=1
    )
    return (after_cpe, layer_norm(after_cpe, gain_row, shift_row))


def attend(qkv_rows, crpe_taps, crpe_shift):
    num_images, num_tokens, triple = qkv_rows.shape
    channels = triple // 3
    head_width = channels // HEADS
    queries = qkv_rows[..., :channels]
    key_rows = qkv_rows[..., channels : 2 * channels]
    values = qkv_rows[..., 2 * channels :]
    weights = jax.nn.softmax(key_rows, axis=1)
    shape_heads = (num_images, num_tokens, HEADS, head_width)
    context = jnp.einsum(
        "bnhd,bnhe->bhde",
        weights.reshape(shape_heads),
        values.reshape(shape_heads),
        precision=HIGHEST,
    )
    factor = jnp.einsum("bnhd,bhde->bnhe", queries.reshape(shape_heads), context, precision=HIGHEST)
    factor = factor.reshape(num_images, num_tokens, channels)
    grid_values = values[:, 1:].reshape(num_images, GRID, GRID, channels)
    conv_values = depthwise(grid_values, crpe_taps * tap_mask(channels), 7) + crpe_shift
    relative = queries[:, 1:] * conv_values.reshape(num_images, GRID * GRID, channels)
    relative = jnp.concatenate(
        [jnp.zeros((num_images, 1, channels), jnp.float32), relative], axis=1
    )
    return factor * head_width ** (-0.5) + relative


def gelu_exact(values):
    return jax.nn.gelu(values, approximate=False)


def cross_rows(left, right):
    return lax.dot_general(
        left, right, (((0,), (0,)), ((), ())), preferred_element_type=jnp.float32
    )


def transposed(gradient, weight):
    return lax.dot_general(
        gradient, weight, (((1,), (1,)), ((), ())), preferred_element_type=jnp.float32
    )


def column_sums(rounded):
    return jnp.sum(rounded.astype(jnp.float32), axis=0)


def adamw_update(master, first_moment, second_moment, gradient, clip_factor, rate, decay):
    clipped = gradient * clip_factor
    first_new = BETA_ONE * first_moment + (1.0 - BETA_ONE) * clipped
    second_new = BETA_TWO * second_moment + (1.0 - BETA_TWO) * clipped * clipped
    first_hat = first_new / (1.0 - BETA_ONE**STEP)
    second_hat = second_new / (1.0 - BETA_TWO**STEP)
    master_new = master - rate * (first_hat / (jnp.sqrt(second_hat) + ADAM_EPS) + decay * master)
    return (master_new, first_new, second_new, master_new.astype(jnp.bfloat16))


def local(
    images,
    cotangent,
    counts,
    in_mats,
    in_mats_m,
    in_mats_v,
    out_mat,
    out_mat_m,
    out_mat_v,
    kernels,
    kernels_m,
    kernels_v,
    gains,
    gains_m,
    gains_v,
    biases,
    biases_m,
    biases_v,
):
    in_copy = in_mats.astype(jnp.bfloat16)
    out_copy = out_mat.astype(jnp.bfloat16)
    kern_copy = kernels.astype(jnp.bfloat16)
    gain_copy = gains.astype(jnp.bfloat16)
    bias_copy = biases.astype(jnp.bfloat16)
    gathered = (
        lax.all_gather(in_copy, ("wide", "narrow"), axis=0, tiled=True),
        lax.all_gather(out_copy, ("wide", "narrow"), axis=0, tiled=True),
        lax.all_gather(kern_copy, ("wide", "narrow"), axis=1, tiled=True),
        lax.all_gather(gain_copy, ("wide", "narrow"), axis=1, tiled=True),
        lax.all_gather(bias_copy, ("wide", "narrow"), axis=1, tiled=True),
    )
    wide_in = gathered[0]
    wide_out = gathered[1]
    kern_all = gathered[2].astype(jnp.float32)
    gain_all = gathered[3].astype(jnp.float32)
    bias_all = gathered[4].astype(jnp.float32)
    inputs = images.astype(jnp.float32)
    num_images, num_tokens, channels = inputs.shape
    flat_rows = num_images * num_tokens
    hidden_rows = MLP_WIDTH // D
    live = (jnp.arange(num_images, dtype=jnp.int32) < counts[0]).astype(jnp.float32)
    local_tokens = counts[0].astype(jnp.float32) * num_tokens
    scale_factor = 1.0 / lax.psum(local_tokens, ("wide", "narrow"))
    (after_cpe, normed), pre_back = jax.vjp(
        pre_block, inputs, kern_all[:9], bias_all[BROWS - 2], gain_all[0], bias_all[0]
    )
    normed_low = normed.astype(jnp.bfloat16).reshape(flat_rows, channels)
    qkv_bias = jnp.concatenate([bias_all[2], jnp.zeros_like(bias_all[2]), bias_all[3]])
    qkv_rows = (
        jnp.dot(normed_low, wide_in[:, : 3 * channels], preferred_element_type=jnp.float32)
        + qkv_bias
    )
    qkv_shaped = qkv_rows.reshape(num_images, num_tokens, 3 * channels)
    attended, attend_back = jax.vjp(attend, qkv_shaped, kern_all[9:], bias_all[BROWS - 1])
    attended_low = attended.astype(jnp.bfloat16).reshape(flat_rows, channels)
    projected = (
        jnp.dot(
            attended_low,
            wide_in[:, 3 * channels : 4 * channels],
            preferred_element_type=jnp.float32,
        )
        + bias_all[4]
    )
    second = after_cpe.reshape(flat_rows, channels) + projected
    normed_two, norm_back = jax.vjp(layer_norm, second, gain_all[1], bias_all[1])
    normed_two_low = normed_two.astype(jnp.bfloat16)
    fc_bias = bias_all[5 : 5 + hidden_rows].reshape(-1)
    hidden_pre = (
        jnp.dot(normed_two_low, wide_in[:, 4 * channels :], preferred_element_type=jnp.float32)
        + fc_bias
    )
    activated, gelu_back = jax.vjp(gelu_exact, hidden_pre)
    activated_low = activated.astype(jnp.bfloat16)
    branch_out = (
        jnp.dot(activated_low, wide_out, preferred_element_type=jnp.float32) + bias_all[BROWS - 3]
    )
    block_out = (second + branch_out).reshape(num_images, num_tokens, channels).astype(jnp.bfloat16)
    regathered = (
        lax.all_gather(in_copy, ("wide", "narrow"), axis=0, tiled=True),
        lax.all_gather(out_copy, ("wide", "narrow"), axis=0, tiled=True),
        lax.all_gather(kern_copy, ("wide", "narrow"), axis=1, tiled=True),
        lax.all_gather(gain_copy, ("wide", "narrow"), axis=1, tiled=True),
        lax.all_gather(bias_copy, ("wide", "narrow"), axis=1, tiled=True),
    )
    back_in = regathered[0]
    back_out = regathered[1]
    out_grad = (cotangent.astype(jnp.float32) * live[:, None, None]).reshape(flat_rows, channels)
    out_grad_low = out_grad.astype(jnp.bfloat16)
    grad_fc2 = cross_rows(activated_low, out_grad_low)
    grad_fc2_bias = column_sums(out_grad_low)
    grad_act = transposed(out_grad_low, back_out)
    grad_hidden = gelu_back(grad_act)[0].astype(jnp.bfloat16)
    grad_fc1 = cross_rows(normed_two_low, grad_hidden)
    grad_fc1_bias = column_sums(grad_hidden).reshape(hidden_rows, channels)
    grad_normed_two = transposed(grad_hidden, back_in[:, 4 * channels :])
    grad_second_norm, grad_gain_two, grad_shift_two = norm_back(grad_normed_two)
    grad_second = out_grad + grad_second_norm
    grad_second_low = grad_second.astype(jnp.bfloat16)
    grad_proj = cross_rows(attended_low, grad_second_low)
    grad_proj_bias = column_sums(grad_second_low)
    grad_attended = transposed(grad_second_low, back_in[:, 3 * channels : 4 * channels])
    grad_qkv, grad_crpe_taps, grad_crpe_shift = attend_back(
        grad_attended.reshape(num_images, num_tokens, channels)
    )
    grad_qkv_low = grad_qkv.reshape(flat_rows, 3 * channels).astype(jnp.bfloat16)
    grad_qkv_mat = cross_rows(normed_low, grad_qkv_low)
    qkv_sums = column_sums(grad_qkv_low)
    grad_normed = transposed(grad_qkv_low, back_in[:, : 3 * channels])
    input_grad, grad_cpe_taps, grad_cpe_shift, grad_gain_one, grad_shift_one = pre_back(
        (
            grad_second.reshape(num_images, num_tokens, channels),
            grad_normed.reshape(num_images, num_tokens, channels),
        )
    )
    grad_kern = jnp.concatenate([grad_cpe_taps, grad_crpe_taps], axis=0)
    grad_gain = jnp.stack([grad_gain_one, grad_gain_two])
    grad_bias = jnp.concatenate(
        [
            grad_shift_one[None],
            grad_shift_two[None],
            qkv_sums[None, :channels],
            qkv_sums[None, 2 * channels :],
            grad_proj_bias[None],
            grad_fc1_bias,
            grad_fc2_bias[None],
            grad_cpe_shift[None],
            grad_crpe_shift[None],
        ],
        axis=0,
    )
    grad_in = jnp.concatenate([grad_qkv_mat, grad_proj, grad_fc1], axis=1)
    summed = (
        lax.psum_scatter(
            grad_in * scale_factor, ("wide", "narrow"), scatter_dimension=0, tiled=True
        ),
        lax.psum_scatter(
            grad_fc2 * scale_factor, ("wide", "narrow"), scatter_dimension=0, tiled=True
        ),
        lax.psum_scatter(
            grad_kern * scale_factor, ("wide", "narrow"), scatter_dimension=1, tiled=True
        ),
        lax.psum_scatter(
            grad_gain * scale_factor, ("wide", "narrow"), scatter_dimension=1, tiled=True
        ),
        lax.psum_scatter(
            grad_bias * scale_factor, ("wide", "narrow"), scatter_dimension=1, tiled=True
        ),
    )
    local_squares = (
        jnp.sum(summed[0] * summed[0])
        + jnp.sum(summed[1] * summed[1])
        + jnp.sum(summed[2] * summed[2])
        + jnp.sum(summed[3] * summed[3])
        + jnp.sum(summed[4] * summed[4])
    )
    grad_norm = jnp.sqrt(lax.psum(local_squares, ("wide", "narrow")))
    clip_factor = jnp.minimum(1.0, 1.0 / (grad_norm + 1e-06))
    in_new = adamw_update(
        in_mats, in_mats_m, in_mats_v, summed[0], clip_factor, RATES[0], DECAYS[0]
    )
    out_new = adamw_update(
        out_mat, out_mat_m, out_mat_v, summed[1], clip_factor, RATES[1], DECAYS[1]
    )
    kern_new = adamw_update(
        kernels, kernels_m, kernels_v, summed[2], clip_factor, RATES[2], DECAYS[2]
    )
    gain_new = adamw_update(gains, gains_m, gains_v, summed[3], clip_factor, RATES[3], DECAYS[3])
    bias_new = adamw_update(biases, biases_m, biases_v, summed[4], clip_factor, RATES[4], DECAYS[4])
    return (
        block_out,
        input_grad,
        grad_norm,
        in_new[0],
        in_new[1],
        in_new[2],
        in_new[3],
        out_new[0],
        out_new[1],
        out_new[2],
        out_new[3],
        kern_new[0],
        kern_new[1],
        kern_new[2],
        kern_new[3],
        gain_new[0],
        gain_new[1],
        gain_new[2],
        gain_new[3],
        bias_new[0],
        bias_new[1],
        bias_new[2],
        bias_new[3],
    )


def solution(mesh):
    placed = (
        P(("wide", "narrow"), None, None),
        P(("wide", "narrow"), None, None),
        P(("wide", "narrow")),
        P(("wide", "narrow"), None),
        P(("wide", "narrow"), None),
        P(("wide", "narrow"), None),
        P(("wide", "narrow"), None),
        P(("wide", "narrow"), None),
        P(("wide", "narrow"), None),
        P(None, ("wide", "narrow")),
        P(None, ("wide", "narrow")),
        P(None, ("wide", "narrow")),
        P(None, ("wide", "narrow")),
        P(None, ("wide", "narrow")),
        P(None, ("wide", "narrow")),
        P(None, ("wide", "narrow")),
        P(None, ("wide", "narrow")),
        P(None, ("wide", "narrow")),
    )
    return jax.shard_map(
        local,
        mesh=mesh,
        in_specs=placed,
        out_specs=(
            P(("wide", "narrow"), None, None),
            P(("wide", "narrow"), None, None),
            P(),
            P(("wide", "narrow"), None),
            P(("wide", "narrow"), None),
            P(("wide", "narrow"), None),
            P(("wide", "narrow"), None),
            P(("wide", "narrow"), None),
            P(("wide", "narrow"), None),
            P(("wide", "narrow"), None),
            P(("wide", "narrow"), None),
            P(None, ("wide", "narrow")),
            P(None, ("wide", "narrow")),
            P(None, ("wide", "narrow")),
            P(None, ("wide", "narrow")),
            P(None, ("wide", "narrow")),
            P(None, ("wide", "narrow")),
            P(None, ("wide", "narrow")),
            P(None, ("wide", "narrow")),
            P(None, ("wide", "narrow")),
            P(None, ("wide", "narrow")),
            P(None, ("wide", "narrow")),
            P(None, ("wide", "narrow")),
        ),
        check_vma=False,
    )
```

profile of v0, /device:TPU:0, one launch (start us, length us, event | category | flops | bytes accessed | tf_op | source)
XLA Modules:
  0.0 1639.4 jit_solution(16979127948002462279)
XLA Ops:
  11.5 43.7 %all_gather.17 = bf16[58,512]{0,1:T(8,128)(2,1)S(1)} all-gather(bf16[58,16]{0,1:T(8,128)(2,1)S(1)} %convert_element_type.115), channel_id=1, replica_groups=mesh['wide'=8,'narrow'=4] {'wide','narrow'}, dimensions={1}, use_global_device_ids=true | all-gather | bytes 61248 | tf_op jit(solution)/shard_map/all_gather | solution.py:149
  58.3 37.4 %all_gather.18 = bf16[12,512]{0,1:T(8,128)(2,1)S(1)} all-gather(bf16[12,16]{0,1:T(8,128)(2,1)S(1)} %copy.115), channel_id=1, replica_groups=mesh['wide'=8,'narrow'=4] {'wide','narrow'}, dimensions={1}, use_global_device_ids=true | all-gather | bytes 12672 | tf_op jit(solution)/shard_map/all_gather | solution.py:151
  106.7 15.8 add_add_fusion.4
  143.6 37.0 %psum.14 = f32[]{:T(128)} all-reduce(f32[]{:T(128)S(6)} %mul.1878), channel_id=1, replica_groups=mesh['wide'=8,'narrow'=4] {'wide','narrow'}, use_global_device_ids=true, to_apply=%region_11.12 | all-reduce | flops 1 | bytes 8 | tf_op jit(solution)/shard_map/psum | solution.py:164
  181.1 41.6 %all-gather = bf16[32,16,2]{1,2,0:T(2,128)(2,1)S(1)} all-gather(bf16[1,16,2]{1,2,0:T(2,128)(2,1)S(1)} %convert_bitcast_fusion), channel_id=1, replica_groups=mesh['wide'=8,'narrow'=4] {'wide','narrow'}, dimensions={0}, use_global_device_ids=true | all-gather | bytes 2112 | tf_op jit(solution)/shard_map/all_gather | solution.py:150
  237.8 7.3 convolution_add_fusion
  245.1 11.3 reshape.579
  271.2 74.6 %add_add_fusion.3 = f32[34,7,7,512]{3,2,1,0:T(8,128)} fusion(f32[34,7,7,512]{3,2,1,0:T(8,128)} %reshape.583, f32[512]{0:T(512)} %get-tuple-element.162, f32[512]{0:T(512)S(1)} %bitcast.259, f32[512]{0:T(512)S(1)} %bitcast.277, f32[512]{0:T(512)S(1)} %bitcast.307, f32[512]{0:T(512)S(1)} %bitcast.309, f32[512]{0:T(512)S(1)} %bitcast.311, f32[512]{0:T(512)} %bitcast.313, ...), kind=kLoop, calls=%fused_computation.184 | loop fusion | flops 83593216 | bytes 6926336 | tf_op jit(solution)/shard_map/jvp()/add | solution.py:83
  357.0 10.7 fusion.87
  367.8 7.0 reshape.582
  392.5 23.3 %fusion.18 = f32[34,8,64,64]{3,2,1,0:T(8,128)S(1)} fusion(f32[34,50,8,64]{3,2,1,0:T(8,128)} %reshape.581, f32[34,50,8,64]{3,2,1,0:T(8,128)} %reshape.580), kind=kOutput, calls=%fused_computation.93 | convolution fusion | flops 668467200 | bytes 11419648 | tf_op jit(solution)/shard_map/jvp(bnhd,bnhe->bhde)/dot_general | solution.py:74
  415.8 15.5 multiply_bitcast_fusion
  431.3 7.4 copy.121
  438.7 7.3 mul.1625
  456.8 37.4 %multiply_convert_fusion = (bf16[1700,2048]{1,0:T(8,128)(2,1)}, f32[1700,2048]{1,0:T(8,128)}, f32[1700,2048]{1,0:T(8,128)}) fusion(f32[2048]{0:T(1024)S(1)} %bitcast.392, bf16[512,4096]{1,0:T(8,128)(2,1)S(1)} %copy-done.36, f32[1700,512]{1,0:T(8,128)S(1)} %get-tuple-element.328, f32[512]{0:T(512)S(1)} %copy-done.220, f32[512]{0:T(512)S(1)} %bitcast.398, ...), kind=kOutput, calls=%fused_computation.62 | convolution fusion | flops 3799296000 | bytes 40431616 | tf_op jit(solution)/shard_map/dot_general | solution.py:190
  494.9 19.2 %convert_reduce_fusion = (f32[2048]{0:T(1024)S(1)}, bf16[1700,2048]{1,0:T(8,128)(2,1)}) fusion(f32[1700,2048]{1,0:T(8,128)} %get-tuple-element.195, bf16[2048,512]{1,0:T(8,128)(2,1)} %all-gather.6.cloned.1.call-done, f32[1700,512]{1,0:T(8,128)} %reshape.586, f32[1700,2048]{1,0:T(8,128)} %get-tuple-element.329, f32[2048]{0:T(1024)S(1)} %bitcast.393), kind=kOutput, calls=%fused_computation.60 | convolution fusion | flops 3625213952 | bytes 40411136 | tf_op jit(solution)/shard_map/dot_general | solution.py:102
  514.0 8.9 multiply_reduce_fusion.62
  540.3 21.3 %fusion.33 = f32[34,50,8,64]{3,1,2,0:T(8,128)} fusion(f32[34,8,64,64]{3,2,1,0:T(8,128)} %copy-done.4, f32[34,50,8,64]{3,2,1,0:T(8,128)} %mul.1851), kind=kOutput, calls=%fused_computation.206 | convolution fusion | flops 668467200 | bytes 11419648 | tf_op jit(solution)/shard_map/transpose(jvp(bnhd,bhde->bnhe))/dot_general | solution.py:80
  561.6 20.4 %fusion.9 = f32[34,8,64,64]{3,2,1,0:T(8,128)S(1)} fusion(f32[34,50,8,64]{3,2,1,0:T(8,128)} %mul.1851, f32[34,50,8,64]{3,2,1,0:T(8,128)S(1)} %bitcast.199), kind=kOutput, calls=%fused_computation.83 | convolution fusion | flops 668467200 | bytes 11419648 | tf_op jit(solution)/shard_map/transpose(jvp(bnhd,bhde->bnhe))/dot_general | solution.py:80
  582.0 18.4 %fusion.28 = f32[34,50,8,64]{3,1,2,0:T(8,128)} fusion(f32[34,8,64,64]{3,2,1,0:T(8,128)S(1)} %fusion.9, f32[34,50,8,64]{3,2,1,0:T(8,128)} %reshape.581), kind=kOutput, calls=%fused_computation.205 | convolution fusion | flops 668467200 | bytes 11419648 | tf_op jit(solution)/shard_map/transpose(jvp(bnhd,bnhe->bhde))/dot_general | solution.py:74
  600.4 17.4 %fusion.25 = f32[34,50,8,64]{3,1,2,0:T(8,128)} fusion(f32[34,8,64,64]{3,2,1,0:T(8,128)S(1)} %fusion.9, f32[34,50,8,64]{3,2,1,0:T(8,128)S(1)} %bitcast.195), kind=kOutput, calls=%fused_computation.204 | convolution fusion | flops 668467200 | bytes 11419648 | tf_op jit(solution)/shard_map/transpose(jvp(bnhd,bnhe->bhde))/dot_general | solution.py:74
  620.2 12.6 fusion.73
  637.9 31.8 %multiply_reduce_fusion.48 = (f32[512]{0:T(512)}, f32[512]{0:T(512)}, f32[512]{0:T(512)}, f32[512]{0:T(512)}, f32[512]{0:T(512)}, /*index=5*/f32[512]{0:T(512)},...) fusion(f32[34,7,7,512]{3,2,1,0:T(8,128)} %reshape.589, ...), kind=kLoop, calls=%fused_computation.163 | loop fusion | flops 30698496 | bytes 6860800 | tf_op jit(solution)/shard_map/transpose(jvp())/reduce_sum | solution.py:36
  669.7 9.9 multiply_reduce_fusion.49
  679.7 10.1 multiply_reduce_fusion.47
  690.1 9.3 broadcast_multiply_fusion.2
  699.7 22.3 %broadcast_multiply_fusion.1 = (f32[34,7,7,512]{3,2,1,0:T(8,128)}, f32[34,7,7,512]{3,2,1,0:T(8,128)}, f32[34,7,7,512]{3,2,1,0:T(8,128)}, f32[34,7,7,512]{3,2,1,0...) fusion(f32[34,7,7,512]{3,2,1,0:T(8,128)S(1)} %copy-done, ...), kind=kLoop, calls=%fused_computation.211 | loop fusion | flops 15353856 | bytes 64864256 | tf_op jit(solution)/shard_map/transpose(jvp())/mul | solution.py:36
  722.2 22.7 %broadcast_multiply_fusion = (f32[34,7,7,512]{3,2,1,0:T(8,128)}, f32[34,7,7,512]{3,2,1,0:T(8,128)}, f32[34,7,7,512]{3,2,1,0:T(8,128)}, f32[34,7,7,512]{3,2,1,0:T...) fusion(f32[34,7,7,512]{3,2,1,0:T(8,128)S(1)} %copy-done, ...), kind=kLoop, calls=%fused_computation.210 | loop fusion | flops 15353856 | bytes 64864256 | tf_op jit(solution)/shard_map/transpose(jvp())/mul | solution.py:36
  744.9 7.4 copy.129
  752.3 7.3 reshape.593
  759.6 7.4 copy.126
  766.9 7.3 reshape.591
  774.2 7.4 copy.128
  781.6 7.3 reshape.592
  797.5 59.0 %pad_add_fusion = f32[34,13,13,512]{3,2,1,0:T(8,128)} fusion(f32[34,7,7,512]{3,2,1,0:T(8,128)} %get-tuple-element.220, f32[34,7,7,512]{3,2,1,0:T(8,128)} %get-tuple-element.221, f32[34,7,7,512]{3,2,1,0:T(8,128)} %get-tuple-element.222, f32[34,7,7,512]{3,2,1,0:T(8,128)} %get-tuple-element.223, f32[34,7,7,512]{3,2,1,0:T(8,128)} %get-tuple-element.224, ...), kind=kLoop, calls=%fused_computation.58 | loop fusion | flops 123561984 | bytes 158482432 | tf_op jit(solution)/shard_map/transpose(jvp())/add_any | solution.py:35
  856.5 10.9 pad_add_fusion.8
  906.0 13.2 broadcast_multiply_fusion.49
  920.3 10.7 pad_add_fusion.1
  931.4 14.2 multiply_reduce_fusion.58
  948.2 10.0 convolution_multiply_fusion
  962.2 7.7 fusion.72
  989.1 8.3 add_convert_fusion.4
  997.5 26.3 %reduce-scatter.18.cloned.1.call-done = f32[16,2]{1,0:T(8,128)} async-done(((f32[512,2]{1,0:T(8,128)}), f32[16,2]{1,0:T(8,128)}) %reduce-scatter.18.cloned.1.call-update) | async-done | bytes 144
  1025.2 132.8 %reduce-scatter.20.cloned.1.call-done = f32[16,12]{1,0:T(8,128)} async-done(((f32[512,12]{1,0:T(8,128)}), f32[16,12]{1,0:T(8,128)}) %reduce-scatter.20.cloned.1.call-update) | async-done | bytes 784
  1159.4 132.8 %reduce-scatter.16.cloned.1.call-done = f32[16,58]{1,0:T(8,128)} async-done(((f32[512,58]{1,0:T(8,128)}), f32[16,58]{1,0:T(8,128)}) %reduce-scatter.16.cloned.1.call-update) | async-done | bytes 3728
  1293.6 139.1 %reduce-scatter.14.cloned.1.call-done = f32[64,512]{1,0:T(8,128)} async-done(((f32[2048,512]{1,0:T(8,128)}), f32[64,512]{1,0:T(8,128)}) %reduce-scatter.14.cloned.1.call-update) | async-done | bytes 131088 | tf_op jit(solution)/shard_map/reduce_scatter | solution.py:257
  1434.4 146.7 %reduce-scatter.12.cloned.1.call-done = f32[16,4096]{1,0:T(8,128)} async-done(((f32[512,4096]{1,0:T(8,128)}), f32[16,4096]{1,0:T(8,128)}) %reduce-scatter.12.cloned.1.call-update) | async-done | bytes 262160 | tf_op jit(solution)/shard_map/reduce_scatter | solution.py:254
  1589.6 36.8 %psum.15 = f32[]{:T(128)} all-reduce(f32[]{:T(128)S(6)} %add.770), channel_id=1, replica_groups=mesh['wide'=8,'narrow'=4] {'wide','narrow'}, use_global_device_ids=true, to_apply=%region_90.91 | all-reduce | flops 1 | bytes 8 | tf_op jit(solution)/shard_map/psum | solution.py:277
  (598 shorter events, 221.3 us)
Async XLA Ops:
  7.2 90.3 %copy-start.13 = (bf16[34,50,512]{2,1,0:T(8,128)(2,1)S(1)}, bf16[34,50,512]{2,1,0:T(8,128)(2,1)}, u32[]{:S(2)}) copy-start(bf16[34,50,512]{2,1,0:T(8,128)(2,1)} %param.18) | copy-start | bytes 5222404
  7.2 230.5 %all-gather.4.cloned.1.call-start = ((), (), s32[]{:S(2)}) async-start(), calls=%async_computation.5 | async-start | bytes 4325376 | tf_op jit(solution)/shard_map/all_gather | solution.py:147
  9.0 485.9 %all-gather.6.cloned.1.call-start = ((), (), s32[]{:S(2)}) async-start(), calls=%async_computation.6 | async-start | bytes 2162688 | tf_op jit(solution)/shard_map/all_gather | solution.py:148
  10.6 1013.2 %reduce-scatter.18.cloned.1.call-start = ((), (), s32[]{:S(2)}) async-start(), calls=%async_computation.10 | async-start | bytes 270336
  10.7 89.3 %copy-start.214 = (s32[49]{0:T(128)}, s32[49]{0:T(128)S(1)}, u32[]{:S(2)}) copy-start(s32[49]{0:T(128)S(1)} %get-tuple-element.336) | copy-start | bytes 592
  10.7 89.3 %copy-start.215 = (s32[49]{0:T(128)}, s32[49]{0:T(128)S(1)}, u32[]{:S(2)}) copy-start(s32[49]{0:T(128)S(1)} %get-tuple-element.337) | copy-start | bytes 592
  10.7 89.3 %copy-start.159 = (s32[512]{0:T(512)}, s32[512]{0:T(512)S(1)}, u32[]{:S(2)}) copy-start(s32[512]{0:T(512)S(1)} %select_select_fusion) | copy-start | bytes 6148
  55.3 51.3 %copy-start.48 = (f32[1,512]{1,0:T(1,128)}, f32[1,512]{1,0:T(1,128)S(1)}, u32[]{:S(2)}) copy-start(f32[1,512]{1,0:T(1,128)S(1)} %get-tuple-element.314) | copy-start | bytes 6148
  55.3 51.3 %copy-start.50 = (f32[1,512]{1,0:T(1,128)}, f32[1,512]{1,0:T(1,128)S(1)}, u32[]{:S(2)}) copy-start(f32[1,512]{1,0:T(1,128)S(1)} %get-tuple-element.315) | copy-start | bytes 6148
  55.4 51.3 %copy-start.52 = (f32[1,512]{1,0:T(1,128)}, f32[1,512]{1,0:T(1,128)S(1)}, u32[]{:S(2)}) copy-start(f32[1,512]{1,0:T(1,128)S(1)} %get-tuple-element.316) | copy-start | bytes 6148
  55.4 51.3 %copy-start.54 = (f32[1,512]{1,0:T(1,128)}, f32[1,512]{1,0:T(1,128)S(1)}, u32[]{:S(2)}) copy-start(f32[1,512]{1,0:T(1,128)S(1)} %get-tuple-element.317) | copy-start | bytes 6148
  55.4 51.3 %copy-start.56 = (f32[1,512]{1,0:T(1,128)}, f32[1,512]{1,0:T(1,128)S(1)}, u32[]{:S(2)}) copy-start(f32[1,512]{1,0:T(1,128)S(1)} %get-tuple-element.318) | copy-start | bytes 6148
  55.4 51.3 %copy-start.58 = (f32[1,512]{1,0:T(1,128)}, f32[1,512]{1,0:T(1,128)S(1)}, u32[]{:S(2)}) copy-start(f32[1,512]{1,0:T(1,128)S(1)} %get-tuple-element.319) | copy-start | bytes 6148
  55.4 51.3 %copy-start.60 = (f32[1,512]{1,0:T(1,128)}, f32[1,512]{1,0:T(1,128)S(1)}, u32[]{:S(2)}) copy-start(f32[1,512]{1,0:T(1,128)S(1)} %get-tuple-element.320) | copy-start | bytes 6148
  55.4 51.3 %copy-start.62 = (f32[1,512]{1,0:T(1,128)}, f32[1,512]{1,0:T(1,128)S(1)}, u32[]{:S(2)}) copy-start(f32[1,512]{1,0:T(1,128)S(1)} %get-tuple-element.321) | copy-start | bytes 6148
  55.4 51.3 %copy-start.64 = (f32[1,512]{1,0:T(1,128)}, f32[1,512]{1,0:T(1,128)S(1)}, u32[]{:S(2)}) copy-start(f32[1,512]{1,0:T(1,128)S(1)} %get-tuple-element.322) | copy-start | bytes 6148
  56.2 214.6 %copy-start.66 = (f32[1,512]{1,0:T(1,128)}, f32[1,512]{1,0:T(1,128)S(1)}, u32[]{:S(2)}) copy-start(f32[1,512]{1,0:T(1,128)S(1)} %get-tuple-element.304) | copy-start | bytes 6148
  56.2 214.6 %copy-start.68 = (f32[1,512]{1,0:T(1,128)}, f32[1,512]{1,0:T(1,128)S(1)}, u32[]{:S(2)}) copy-start(f32[1,512]{1,0:T(1,128)S(1)} %get-tuple-element.305) | copy-start | bytes 6148
  56.2 214.6 %copy-start.70 = (f32[1,512]{1,0:T(1,128)}, f32[1,512]{1,0:T(1,128)S(1)}, u32[]{:S(2)}) copy-start(f32[1,512]{1,0:T(1,128)S(1)} %get-tuple-element.306) | copy-start | bytes 6148
  56.2 214.6 %copy-start.72 = (f32[1,512]{1,0:T(1,128)}, f32[1,512]{1,0:T(1,128)S(1)}, u32[]{:S(2)}) copy-start(f32[1,512]{1,0:T(1,128)S(1)} %get-tuple-element.307) | copy-start | bytes 6148
  135.4 91.1 %copy-start.37 = (f32[34,50]{1,0:T(8,128)}, f32[34,50]{1,0:T(8,128)S(1)}, u32[]{:S(2)}) copy-start(f32[34,50]{1,0:T(8,128)S(1)} %multiply_reduce_fusion.61) | copy-start | bytes 20404
  138.4 99.4 %copy-start.12 = (f32[1700,512]{1,0:T(8,128)}, f32[1700,512]{1,0:T(8,128)S(1)}, u32[]{:S(2)}) copy-start(f32[1700,512]{1,0:T(8,128)S(1)} %reshape.578) | copy-start | bytes 10444804
  138.4 42.7 %copy-start.221 = (f32[2,16]{1,0:T(2,128)S(1)}, f32[2,16]{1,0:T(2,128)}, u32[]{:S(2)}) copy-start(f32[2,16]{1,0:T(2,128)} %param.30) | copy-start | bytes 388
  456.0 67.0 %copy-start.6 = (f32[1700,512]{1,0:T(8,128)}, f32[1700,512]{1,0:T(8,128)S(1)}, u32[]{:S(2)}) copy-start(f32[1700,512]{1,0:T(8,128)S(1)} %get-tuple-element.328) | copy-start | bytes 10444804
  456.0 66.9 %copy-start.41 = (f32[1700]{0:T(1024)}, f32[1700]{0:T(1024)S(1)}, u32[]{:S(2)}) copy-start(f32[1700]{0:T(1024)S(1)} %broadcast_multiply_fusion.61) | copy-start | bytes 20404
  456.7 66.3 %copy-start.46 = (f32[1700]{0:T(1024)}, f32[1700]{0:T(1024)S(1)}, u32[]{:S(2)}) copy-start(f32[1700]{0:T(1024)S(1)} %fusion.63) | copy-start | bytes 20404
  891.9 266.0 %reduce-scatter.20.cloned.1.call-start = ((), (), s32[]{:S(2)}) async-start(), calls=%async_computation.11 | async-start | bytes 270336
  920.2 371.9 %reduce-scatter.16.cloned.1.call-start = ((), (), s32[]{:S(2)}) async-start(), calls=%async_computation.9 | async-start | bytes 270336
  947.9 484.8 %reduce-scatter.14.cloned.1.call-start = ((), (), s32[]{:S(2)}) async-start(), calls=%async_computation.8 | async-start | bytes 4325376 | tf_op jit(solution)/shard_map/reduce_scatter | solution.py:257
  958.3 622.8 %reduce-scatter.12.cloned.1.call-start = ((), (), s32[]{:S(2)}) async-start(), calls=%async_computation.7 | async-start | bytes 8650752 | tf_op jit(solution)/shard_map/reduce_scatter | solution.py:254
  997.3 629.8 %copy-start.222 = (f32[2,16]{1,0:T(2,128)S(1)}, f32[2,16]{1,0:T(2,128)}, u32[]{:S(2)}) copy-start(f32[2,16]{1,0:T(2,128)} %param.30) | copy-start | bytes 388
  997.3 629.8 %copy-start.223 = (f32[2,16]{1,0:T(2,128)S(1)}, f32[2,16]{1,0:T(2,128)}, u32[]{:S(2)}) copy-start(f32[2,16]{1,0:T(2,128)} %param.31) | copy-start | bytes 388
  997.3 629.8 %copy-start.224 = (f32[2,16]{1,0:T(2,128)S(1)}, f32[2,16]{1,0:T(2,128)}, u32[]{:S(2)}) copy-start(f32[2,16]{1,0:T(2,128)} %param.32) | copy-start | bytes 388
  997.3 630.4 %copy-start.44 = (f32[12,16]{1,0:T(8,128)S(1)}, f32[12,16]{1,0:T(8,128)}, u32[]{:S(2)}) copy-start(f32[12,16]{1,0:T(8,128)} %param.33) | copy-start | bytes 2308
  997.4 630.4 %copy-start.205 = (f32[12,16]{1,0:T(8,128)S(1)}, f32[12,16]{1,0:T(8,128)}, u32[]{:S(2)}) copy-start(f32[12,16]{1,0:T(8,128)} %param.34) | copy-start | bytes 2308
  997.4 630.4 %copy-start.206 = (f32[12,16]{1,0:T(8,128)S(1)}, f32[12,16]{1,0:T(8,128)}, u32[]{:S(2)}) copy-start(f32[12,16]{1,0:T(8,128)} %param.35) | copy-start | bytes 2308
  997.4 631.0 %copy-start.45 = (f32[58,16]{0,1:T(8,128)S(1)}, f32[58,16]{0,1:T(8,128)}, u32[]{:S(2)}) copy-start(f32[58,16]{0,1:T(8,128)} %param.27) | copy-start | bytes 11140
  997.4 631.0 %copy-start.207 = (f32[58,16]{0,1:T(8,128)S(1)}, f32[58,16]{0,1:T(8,128)}, u32[]{:S(2)}) copy-start(f32[58,16]{0,1:T(8,128)} %param.28) | copy-start | bytes 11140
  997.4 631.0 %copy-start.208 = (f32[58,16]{0,1:T(8,128)S(1)}, f32[58,16]{0,1:T(8,128)}, u32[]{:S(2)}) copy-start(f32[58,16]{0,1:T(8,128)} %param.29) | copy-start | bytes 11140
  997.4 631.7 %copy-start.27 = (f32[64,512]{1,0:T(8,128)S(1)}, f32[64,512]{1,0:T(8,128)}, u32[]{:S(2)}) copy-start(f32[64,512]{1,0:T(8,128)} %param.24) | copy-start | bytes 393220
  997.4 631.6 %copy-start.39 = (f32[64,512]{1,0:T(8,128)S(1)}, f32[64,512]{1,0:T(8,128)}, u32[]{:S(2)}) copy-start(f32[64,512]{1,0:T(8,128)} %param.25) | copy-start | bytes 393220
  997.4 631.6 %copy-start.40 = (f32[64,512]{1,0:T(8,128)S(1)}, f32[64,512]{1,0:T(8,128)}, u32[]{:S(2)}) copy-start(f32[64,512]{1,0:T(8,128)} %param.26) | copy-start | bytes 393220
  997.4 632.5 %copy-start.25 = (f32[16,4096]{1,0:T(8,128)S(1)}, f32[16,4096]{1,0:T(8,128)}, u32[]{:S(2)}) copy-start(f32[16,4096]{1,0:T(8,128)} %param.21) | copy-start | bytes 786436
  997.5 632.5 %copy-start.34 = (f32[16,4096]{1,0:T(8,128)S(1)}, f32[16,4096]{1,0:T(8,128)}, u32[]{:S(2)}) copy-start(f32[16,4096]{1,0:T(8,128)} %param.22) | copy-start | bytes 786436
  997.5 632.4 %copy-start.35 = (f32[16,4096]{1,0:T(8,128)S(1)}, f32[16,4096]{1,0:T(8,128)}, u32[]{:S(2)}) copy-start(f32[16,4096]{1,0:T(8,128)} %param.23) | copy-start | bytes 786436
  1292.1 336.3 %copy-start.43 = (f32[16,58]{1,0:T(8,128)S(1)}, f32[16,58]{1,0:T(8,128)}, u32[]{:S(2)}) copy-start(f32[16,58]{1,0:T(8,128)} %reduce-scatter.16.cloned.1.call-done) | copy-start | bytes 11140
  1432.7 196.3 %copy-start.28 = (f32[64,512]{1,0:T(8,128)S(1)}, f32[64,512]{1,0:T(8,128)}, u32[]{:S(2)}) copy-start(f32[64,512]{1,0:T(8,128)} %reduce-scatter.14.cloned.1.call-done) | copy-start | bytes 393220
  1581.1 48.9 %copy-start.26 = (f32[16,4096]{1,0:T(8,128)S(1)}, f32[16,4096]{1,0:T(8,128)}, u32[]{:S(2)}) copy-start(f32[16,4096]{1,0:T(8,128)} %reduce-scatter.12.cloned.1.call-done) | copy-start | bytes 786436
  (194 other events, 2115.1 us)
Sparse Core Ops, SparseCore 0:
  11.4 64.9 all-gather.3
  79.8 54.8 all-gather.5
  892.1 131.6 reduce-scatter.17
  1026.5 131.4 reduce-scatter.19
  1160.6 131.4 reduce-scatter.15
  1294.3 138.4 reduce-scatter.13
  1435.0 145.9 reduce-scatter.11
where the time goes:
time: 1650 us; the launch traced here: 1640 us
  waiting for transfers between devices  578 us (35%)
  other arithmetic  419 us (25%)
  matrix products  239 us (14%)
  blocking collectives  196 us (12%)
  local copies, waits for them, and re-layouts  182 us (11%)
  between operations  24.4 us (1%)
    unnamed x10, waiting for transfers between devices  292 us
    reduce_scatter x1, waiting for transfers between devices, local(): lax.psum_scatter(grad_in * scale_factor, ('wide', 'narrow'), scatter_dime...  147 us
    reduce_scatter x1, waiting for transfers between devices, local(): lax.psum_scatter(grad_fc2 * scale_factor, ('wide', 'narrow'), scatter_dim...  139 us
    add_any x3, other arithmetic, depthwise(): window = padded[:, row_tap:row_tap + GRID, col_tap:col_tap + GRID, :]  80.6 us
    add x1, other arithmetic, attend(): depthwise(grid_values, crpe_taps * tap_mask(channels), 7) + crpe_shift  74.6 us
    mul x4, other arithmetic, depthwise(): summed_taps = summed_taps + window * taps[row_tap * kernel_width + col_tap]  67.5 us
    reduce_sum x4, other arithmetic, depthwise(): summed_taps = summed_taps + window * taps[row_tap * kernel_width + col_tap]  65.9 us
    dot_general x3, matrix products, attend(): jnp.einsum('bnhd,bnhe->bhde', weights.reshape(shape_heads), values.reshap...  59.1 us
  transfers between devices with their start and end apart: 7, of which 5 were waited for; matrix products, arithmetic and copies ran while one was open for 26% of the time, Pallas kernels for 0%

commit v1 on v0

--- a/solution.py
+++ b/solution.py
@@ -1,6 +1,10 @@
+import functools
+
 import jax
 import jax.numpy as jnp
 from jax import lax
+from jax.experimental import pallas as pl
+from jax.experimental.pallas import tpu as pltpu
 from jax.sharding import PartitionSpec as P
 
 D = 512
@@ -18,6 +22,364 @@
 HIGHEST = lax.Precision.HIGHEST
 RATES = (0.04, 0.02, 0.1, 0.8, 0.25)
 DECAYS = (0.05, 0.05, 0.05, 0.0, 0.0)
+
+
+MESH_ID = pl.DeviceIdType.MESH
+SPLIT = 3072
+SMALL_ROWS = 16
+
+
+def place():
+    w = lax.axis_index("wide")
+    n = lax.axis_index("narrow")
+    return w // 2, w % 2, n // 2, n % 2
+
+
+def device(z, y, x, c):
+    return (z * 2 + y, x * 2 + c)
+
+
+def neighbour(at, axis, step=1):
+    z, y, x, c = at
+    if axis == 0:
+        return (lax.rem(z + step, 4), y, x, c)
+    if axis == 1:
+        return (z, 1 - y, x, c)
+    if axis == 2:
+        return (z, y, 1 - x, c)
+    return (z, y, x, 1 - c)
+
+
+def gather_kernel(wi, wo, sm, gi, go, gs, send_sem, recv_sem, own_sem):
+    at = place()
+    z, y, x, c = at
+    partners = [device(*neighbour(at, 0, s)) for s in (1, 2, 3)]
+    partners += [device(*neighbour(at, a)) for a in (1, 2, 3)]
+    barrier = pltpu.get_barrier_semaphore()
+    for partner in partners:
+        pl.semaphore_signal(barrier, inc=1, device_id=partner, device_id_type=MESH_ID)
+    pl.semaphore_wait(barrier, len(partners))
+
+    width = wi.shape[1]
+    pieces = (
+        (wi, gi, 0, pl.ds(0, SPLIT)),
+        (sm, gs, 0, pl.ds(0, 128)),
+        (wi, gi, 1, pl.ds(SPLIT, width - SPLIT)),
+        (wo, go, 1, pl.ds(0, wo.shape[1])),
+    )
+    orders = ((0, 1, 2, 3), (0, 2, 1, 3))
+
+    def slot(r):
+        zs = lax.rem(z - r[0] + 4, 4)
+        ys = 1 - y if r[1] else y
+        xs = 1 - x if r[2] else x
+        cs = 1 - c if r[3] else c
+        return ((zs * 2 + ys) * 2 + xs) * 2 + cs
+
+    def flat(r):
+        return ((r[0] * 2 + r[1]) * 2 + r[2]) * 2 + r[3]
+
+    def moved(r, axis, step):
+        r = list(r)
+        r[axis] = step
+        return tuple(r)
+
+    def transfer(p, r, axis, step):
+        own, out, color, cols = pieces[p]
+        there = out.at[slot(r), :, cols]
+        here = own.at[:, cols] if r == (0, 0, 0, 0) else there
+        to = moved(r, axis, step)
+        return pltpu.make_async_remote_copy(
+            src_ref=here,
+            dst_ref=there,
+            send_sem=send_sem.at[p, flat(to)],
+            recv_sem=recv_sem.at[p, flat(to)],
+            device_id=device(*neighbour(at, axis, step)),
+            device_id_type=MESH_ID,
+        )
+
+    def onward(p, r):
+        order = orders[pieces[p][2]]
+        last = max([i for i in range(4) if r[order[i]]], default=-1)
+        for i in range(last + 1, 4):
+            axis = order[i]
+            for step in (1, 2, 3) if axis == 0 else (1,):
+                yield axis, step
+
+    started = []
+
+    def forward(p, r):
+        for axis, step in onward(p, r):
+            copy = transfer(p, r, axis, step)
+            copy.start()
+            started.append(copy)
+
+    zero = (0, 0, 0, 0)
+    for p in range(4):
+        forward(p, zero)
+    own_copies = []
+    for p in range(4):
+        own, out, color, cols = pieces[p]
+        copy = pltpu.make_async_copy(
+            own.at[:, cols], out.at[slot(zero), :, cols], own_sem.at[p]
+        )
+        copy.start()
+        own_copies.append(copy)
+
+    def arrival(p, r):
+        order = orders[pieces[p][2]]
+        axis = [a for a in order if r[a]][-1]
+        back = moved(r, axis, 0)
+        return transfer(p, back, axis, r[axis])
+
+    offsets = [
+        (dz, dy, dx, dc) for dz in range(4) for dy in range(2) for dx in range(2) for dc in range(2)
+    ]
+    cost = {0: 0, 1: 2, 2: 4, 3: 2}
+
+    def when(r):
+        return cost[r[0]] + r[1] * 2 + r[2] * 2 + r[3]
+
+    for r in sorted(offsets[1:], key=when):
+        for p in range(4):
+            copy = arrival(p, r)
+            copy.wait_recv()
+            forward(p, r)
+    for copy in started:
+        copy.wait_send()
+    for copy in own_copies:
+        copy.wait()
+
+
+def gather_all(in_copy, out_copy, small):
+    hbm = pl.BlockSpec(memory_space=pl.ANY)
+    return pl.pallas_call(
+        gather_kernel,
+        out_shape=(
+            jax.ShapeDtypeStruct((32,) + in_copy.shape, in_copy.dtype),
+            jax.ShapeDtypeStruct((32,) + out_copy.shape, out_copy.dtype),
+            jax.ShapeDtypeStruct((32,) + small.shape, small.dtype),
+        ),
+        in_specs=[hbm] * 3,
+        out_specs=(hbm,) * 3,
+        scratch_shapes=[
+            pltpu.SemaphoreType.DMA((4, 32)),
+            pltpu.SemaphoreType.DMA((4, 32)),
+            pltpu.SemaphoreType.DMA((4,)),
+        ],
+        compiler_params=pltpu.CompilerParams(collective_id=0, has_side_effects=True),
+        name="gather_all",
+    )(in_copy, out_copy, small)
+
+
+def add_low(left, right):
+    return (left.astype(jnp.float32) + right.astype(jnp.float32)).astype(left.dtype)
+
+
+def reduce_kernel(
+    gi, go, gs, fi, fo, fs, fq,
+    ai, ao, a_s, b1, b2i, b2o, b2s, b3,
+    ri, ro, rs, r1, r2i, r2o, r2s, r3,
+    t1, t2i, t2o, t2s, u1, u2i, u2o, u2s,
+    squares_narrow, squares_wide, send_sem, recv_sem, norm_send, norm_recv,
+):
+    at = place()
+    z, y, x, c = at
+    w = z * 2 + y
+    n = x * 2 + c
+    partners = [(w, lax.rem(n + s, 4)) for s in (1, 2, 3)]
+    partners += [(lax.rem(w + s, 8), n) for s in range(1, 8)]
+    barrier = pltpu.get_barrier_semaphore()
+    for partner in partners:
+        pl.semaphore_signal(barrier, inc=1, device_id=partner, device_id_type=MESH_ID)
+    pl.semaphore_wait(barrier, len(partners))
+
+    count = [0]
+
+    def send(src, dst, axis, step=1):
+        index = count[0]
+        count[0] += 1
+        copy = pltpu.make_async_remote_copy(
+            src_ref=src,
+            dst_ref=dst,
+            send_sem=send_sem.at[index],
+            recv_sem=recv_sem.at[index],
+            device_id=device(*neighbour(at, axis, step)),
+            device_id_type=MESH_ID,
+        )
+        copy.start()
+        return copy
+
+    first = [
+        send(gi.at[:, :, :, 1 - c], ri, 3),
+        send(go.at[:, :, :, 1 - c], ro, 3),
+        send(gs.at[:, :, :, 1 - c], rs, 3),
+    ]
+    for copy in first:
+        copy.wait_recv()
+
+    def add_first(k, carry):
+        zi, yi, xi = k // 4, lax.rem(k // 2, 2), lax.rem(k, 2)
+        ai[zi, yi, xi] = add_low(gi[zi, yi, xi, c], ri[zi, yi, xi])
+        ao[zi, yi, xi] = add_low(go[zi, yi, xi, c], ro[zi, yi, xi])
+        a_s[zi, yi, xi] = add_low(gs[zi, yi, xi, c], rs[zi, yi, xi])
+        return carry
+
+    lax.fori_loop(0, 16, add_first, 0)
+    width = gi.shape[-1]
+    left, right = pl.ds(0, SPLIT), pl.ds(SPLIT, width - SPLIT)
+    second = [
+        send(ai.at[:, :, 1 - x, :, left], r1, 2),
+        send(ai.at[:, 1 - y, :, :, right], r2i, 1),
+        send(ao.at[:, 1 - y], r2o, 1),
+        send(a_s.at[:, 1 - y], r2s, 1),
+    ]
+    for copy in second:
+        copy.wait_recv()
+
+    def add_second(k, carry):
+        zi, j = k // 2, lax.rem(k, 2)
+        b1[zi, j] = add_low(ai[zi, j, x, :, left], r1[zi, j])
+        b2i[zi, j] = add_low(ai[zi, y, j, :, right], r2i[zi, j])
+        b2o[zi, j] = add_low(ao[zi, y, j], r2o[zi, j])
+        b2s[zi, j] = add_low(a_s[zi, y, j], r2s[zi, j])
+        return carry
+
+    lax.fori_loop(0, 8, add_second, 0)
+    third = [
+        send(b1.at[:, 1 - y], r3, 1),
+        send(b2i.at[:, 1 - x], t2i, 2),
+        send(b2o.at[:, 1 - x], t2o, 2),
+        send(b2s.at[:, 1 - x], t2s, 2),
+    ]
+    for copy in third:
+        copy.wait_recv()
+
+    def add_third(k, carry):
+        b3[k] = add_low(b1[k, y], r3[k])
+        r2i[k, 0] = add_low(b2i[k, x], t2i[k])
+        r2o[k, 0] = add_low(b2o[k, x], t2o[k])
+        r2s[k, 0] = add_low(b2s[k, x], t2s[k])
+        return carry
+
+    lax.fori_loop(0, 4, add_third, 0)
+    fourth = []
+    for step in (1, 2, 3):
+        to = lax.rem(z + step, 4)
+        fourth += [
+            send(b3.at[to], u1.at[step - 1], 0, step),
+            send(r2i.at[to, 0], u2i.at[step - 1], 0, step),
+            send(r2o.at[to, 0], u2o.at[step - 1], 0, step),
+            send(r2s.at[to, 0], u2s.at[step - 1], 0, step),
+        ]
+    for copy in fourth:
+        copy.wait_recv()
+
+    def total(own, others):
+        value = own.astype(jnp.float32)
+        for k in range(3):
+            value = value + others[k].astype(jnp.float32)
+        return value
+
+    squares = jnp.zeros((8, 128), jnp.float32)
+
+    def tile_squares(value, squares):
+        rows, cols = value.shape
+        for i in range(rows // 8):
+            for j in range(cols // 128):
+                part = value[i * 8 : i * 8 + 8, j * 128 : j * 128 + 128]
+                squares = squares + part * part
+        return squares
+
+    for own, others, out, cols in (
+        (b3[z], u1, fi, left),
+        (r2i[z, 0], u2i, fi, right),
+        (r2o[z, 0], u2o, fo, pl.ds(0, fo.shape[1])),
+        (r2s[z, 0], u2s, fs, pl.ds(0, 128)),
+    ):
+        value = total(own, others)
+        out[:, cols] = value
+        squares = tile_squares(value, squares)
+
+    def exchange(buffer, mine, size, axis, base):
+        copies = []
+        for step in range(1, size):
+            to = lax.rem(mine + step, size)
+            copy = pltpu.make_async_remote_copy(
+                src_ref=buffer.at[mine],
+                dst_ref=buffer.at[mine],
+                send_sem=norm_send.at[base + step],
+                recv_sem=norm_recv.at[base + step],
+                device_id=(to, n) if axis == 0 else (w, to),
+                device_id_type=MESH_ID,
+            )
+            copy.start()
+            copies.append(copy)
+        for copy in copies:
+            copy.wait()
+        value = buffer[0]
+        for k in range(1, size):
+            value = value + buffer[k]
+        return value
+
+    squares_narrow[n] = squares
+    squares = exchange(squares_narrow, n, 4, 1, 0)
+    squares_wide[w] = squares
+    fq[...] = exchange(squares_wide, w, 8, 0, 4)
+    for copy in first + second + third + fourth:
+        copy.wait_send()
+
+
+def reduce_all(grad_in, grad_out, small):
+    low = jnp.bfloat16
+    rows_in, width = grad_in.shape[0] // 32, grad_in.shape[1]
+    rows_out, cols_out = grad_out.shape[0] // 32, grad_out.shape[1]
+    gi = grad_in.reshape(4, 2, 2, 2, rows_in, width)
+    go = grad_out.reshape(4, 2, 2, 2, rows_out, cols_out)
+    gs = small.reshape(4, 2, 2, 2, SMALL_ROWS, 128)
+    rest = width - SPLIT
+    vmem = pl.BlockSpec(memory_space=pltpu.VMEM)
+
+    def trio(lead, cols, own=True):
+        kinds = [
+            pltpu.VMEM(lead + (rows_in, cols), low),
+            pltpu.VMEM(lead + (rows_out, cols_out), low),
+            pltpu.VMEM(lead + (SMALL_ROWS, 128), jnp.float32),
+        ]
+        return kinds
+
+    scratch = trio((4, 2, 2), width)
+    scratch += [pltpu.VMEM((4, 2, rows_in, SPLIT), low)] + trio((4, 2), rest)
+    scratch += [pltpu.VMEM((4, rows_in, SPLIT), low)]
+    scratch += trio((4, 2, 2), width)
+    scratch += [pltpu.VMEM((4, 2, rows_in, SPLIT), low)] + trio((4, 2), rest)
+    scratch += [pltpu.VMEM((4, rows_in, SPLIT), low)]
+    scratch += [pltpu.VMEM((1, 8, 128), low)] + trio((4,), rest)
+    scratch += [pltpu.VMEM((3, rows_in, SPLIT), low)] + trio((3,), rest)
+    scratch += [
+        pltpu.VMEM((4, 8, 128), jnp.float32),
+        pltpu.VMEM((8, 8, 128), jnp.float32),
+        pltpu.SemaphoreType.DMA((23,)),
+        pltpu.SemaphoreType.DMA((23,)),
+        pltpu.SemaphoreType.DMA((12,)),
+        pltpu.SemaphoreType.DMA((12,)),
+    ]
+    return pl.pallas_call(
+        reduce_kernel,
+        out_shape=(
+            jax.ShapeDtypeStruct((rows_in, width), jnp.float32),
+            jax.ShapeDtypeStruct((rows_out, cols_out), jnp.float32),
+            jax.ShapeDtypeStruct((SMALL_ROWS, 128), jnp.float32),
+            jax.ShapeDtypeStruct((8, 128), jnp.float32),
+        ),
+        in_specs=[vmem] * 3,
+        out_specs=(vmem,) * 4,
+        scratch_shapes=scratch,
+        compiler_params=pltpu.CompilerParams(
+            collective_id=1, has_side_effects=True, vmem_limit_bytes=48 << 20
+        ),
+        name="reduce_all",
+    )(gi, go, gs)
 
 
 def layer_norm(values, gain_row, shift_row):
@@ -137,19 +499,44 @@
     biases,
     biases_m,
     biases_v,
+    special,
 ):
     in_copy = in_mats.astype(jnp.bfloat16)
     out_copy = out_mat.astype(jnp.bfloat16)
     kern_copy = kernels.astype(jnp.bfloat16)
     gain_copy = gains.astype(jnp.bfloat16)
     bias_copy = biases.astype(jnp.bfloat16)
-    gathered = (
-        lax.all_gather(in_copy, ("wide", "narrow"), axis=0, tiled=True),
-        lax.all_gather(out_copy, ("wide", "narrow"), axis=0, tiled=True),
-        lax.all_gather(kern_copy, ("wide", "narrow"), axis=1, tiled=True),
-        lax.all_gather(gain_copy, ("wide", "narrow"), axis=1, tiled=True),
-        lax.all_gather(bias_copy, ("wide", "narrow"), axis=1, tiled=True),
-    )
+    shards = (kern_copy, gain_copy, bias_copy)
+    sizes = [shard.shape[0] for shard in shards]
+    if special:
+        per = sum(sizes) * kern_copy.shape[1]
+        flat = jnp.concatenate(
+            [jnp.concatenate(shards, axis=0).reshape(-1), counts.astype(jnp.bfloat16)]
+        )
+        flat = jnp.pad(flat, (0, SMALL_ROWS * 128 - per - 1)).reshape(SMALL_ROWS, 128)
+        all_in, all_out, all_small = gather_all(in_copy, out_copy, flat)
+        all_small = all_small.reshape(32, SMALL_ROWS * 128)
+        live_total = jnp.sum(all_small[:, per].astype(jnp.float32)) * images.shape[1]
+        rows = all_small[:, :per].reshape(32, sum(sizes), -1).transpose(1, 0, 2)
+        rows = rows.reshape(sum(sizes), -1)
+        gathered = (
+            all_in.reshape(-1, in_copy.shape[1]),
+            all_out.reshape(-1, out_copy.shape[1]),
+            rows[: sizes[0]],
+            rows[sizes[0] : sizes[0] + sizes[1]],
+            rows[sizes[0] + sizes[1] :],
+        )
+    else:
+        gathered = (
+            lax.all_gather(in_copy, ("wide", "narrow"), axis=0, tiled=True),
+            lax.all_gather(out_copy, ("wide", "narrow"), axis=0, tiled=True),
+            lax.all_gather(kern_copy, ("wide", "narrow"), axis=1, tiled=True),
+            lax.all_gather(gain_copy, ("wide", "narrow"), axis=1, tiled=True),
+            lax.all_gather(bias_copy, ("wide", "narrow"), axis=1, tiled=True),
+        )
+        live_total = lax.psum(
+            counts[0].astype(jnp.float32) * images.shape[1], ("wide", "narrow")
+        )
     wide_in = gathered[0]
     wide_out = gathered[1]
     kern_all = gathered[2].astype(jnp.float32)
@@ -160,8 +547,7 @@
     flat_rows = num_images * num_tokens
     hidden_rows = MLP_WIDTH // D
     live = (jnp.arange(num_images, dtype=jnp.int32) < counts[0]).astype(jnp.float32)
-    local_tokens = counts[0].astype(jnp.float32) * num_tokens
-    scale_factor = 1.0 / lax.psum(local_tokens, ("wide", "narrow"))
+    scale_factor = 1.0 / live_total
     (after_cpe, normed), pre_back = jax.vjp(
         pre_block, inputs, kern_all[:9], bias_all[BROWS - 2], gain_all[0], bias_all[0]
     )
@@ -196,15 +582,8 @@
         jnp.dot(activated_low, wide_out, preferred_element_type=jnp.float32) + bias_all[BROWS - 3]
     )
     block_out = (second + branch_out).reshape(num_images, num_tokens, channels).astype(jnp.bfloat16)
-    regathered = (
-        lax.all_gather(in_copy, ("wide", "narrow"), axis=0, tiled=True),
-        lax.all_gather(out_copy, ("wide", "narrow"), axis=0, tiled=True),
-        lax.all_gather(kern_copy, ("wide", "narrow"), axis=1, tiled=True),
-        lax.all_gather(gain_copy, ("wide", "narrow"), axis=1, tiled=True),
-        lax.all_gather(bias_copy, ("wide", "narrow"), axis=1, tiled=True),
-    )
-    back_in = regathered[0]
-    back_out = regathered[1]
+    back_in = wide_in
+    back_out = wide_out
     out_grad = (cotangent.astype(jnp.float32) * live[:, None, None]).reshape(flat_rows, channels)
     out_grad_low = out_grad.astype(jnp.bfloat16)
     grad_fc2 = cross_rows(activated_low, out_grad_low)
@@ -250,31 +629,33 @@
         axis=0,
     )
     grad_in = jnp.concatenate([grad_qkv_mat, grad_proj, grad_fc1], axis=1)
-    summed = (
-        lax.psum_scatter(
-            grad_in * scale_factor, ("wide", "narrow"), scatter_dimension=0, tiled=True
-        ),
-        lax.psum_scatter(
-            grad_fc2 * scale_factor, ("wide", "narrow"), scatter_dimension=0, tiled=True
-        ),
-        lax.psum_scatter(
-            grad_kern * scale_factor, ("wide", "narrow"), scatter_dimension=1, tiled=True
-        ),
-        lax.psum_scatter(
-            grad_gain * scale_factor, ("wide", "narrow"), scatter_dimension=1, tiled=True
-        ),
-        lax.psum_scatter(
-            grad_bias * scale_factor, ("wide", "narrow"), scatter_dimension=1, tiled=True
-        ),
-    )
-    local_squares = (
-        jnp.sum(summed[0] * summed[0])
-        + jnp.sum(summed[1] * summed[1])
-        + jnp.sum(summed[2] * summed[2])
-        + jnp.sum(summed[3] * summed[3])
-        + jnp.sum(summed[4] * summed[4])
-    )
-    grad_norm = jnp.sqrt(lax.psum(local_squares, ("wide", "narrow")))
+    parts = (grad_kern, grad_gain, grad_bias)
+    if special:
+        rows = jnp.concatenate(parts, axis=0)
+        small = rows.reshape(sum(sizes), 32, -1).transpose(1, 0, 2).reshape(32, per)
+        small = jnp.pad(small, ((0, 0), (0, SMALL_ROWS * 128 - per)))
+        sum_in, sum_out, sum_small, squares = reduce_all(
+            grad_in.astype(jnp.bfloat16), grad_fc2.astype(jnp.bfloat16), small
+        )
+        rows = sum_small.reshape(-1)[:per].reshape(sum(sizes), -1)
+        summed = (
+            sum_in,
+            sum_out,
+            rows[: sizes[0]],
+            rows[sizes[0] : sizes[0] + sizes[1]],
+            rows[sizes[0] + sizes[1] :],
+        )
+        total_squares = jnp.sum(squares)
+    else:
+        summed = tuple(
+            lax.psum_scatter(part, ("wide", "narrow"), scatter_dimension=dim, tiled=True)
+            for part, dim in zip((grad_in, grad_fc2) + parts, (0, 0, 1, 1, 1))
+        )
+        total_squares = lax.psum(
+            sum(jnp.sum(part * part) for part in summed), ("wide", "narrow")
+        )
+    summed = tuple(part * scale_factor for part in summed)
+    grad_norm = jnp.sqrt(total_squares) * scale_factor
     clip_factor = jnp.minimum(1.0, 1.0 / (grad_norm + 1e-06))
     in_new = adamw_update(
         in_mats, in_mats_m, in_mats_v, summed[0], clip_factor, RATES[0], DECAYS[0]
@@ -335,8 +716,9 @@
         P(None, ("wide", "narrow")),
         P(None, ("wide", "narrow")),
     )
+    special = dict(mesh.shape) == {"wide": 8, "narrow": 4}
     return jax.shard_map(
-        local,
+        functools.partial(local, special=special),
         mesh=mesh,
         in_specs=placed,
         out_specs=(

time: 1650 us -> 1050 us (0.64)
  waiting for transfers between devices: 578 us -> 0 us
  blocking collectives: 196 us -> 0 us
  Pallas kernels: 0 us -> 114 us
  local copies, waits for them, and re-layouts: 182 us -> 259 us
  between operations: 24.4 us -> 6.92 us
    unnamed x10 -> x0, waiting for transfers between devices: 292 us -> none
    reduce_scatter x2 -> x0, waiting for transfers between devices: 286 us -> none  [the longest x1 147 us: local(): lax.psum_scatter(grad_in * scale_factor, ('wide', 'narrow'), scatter_dime...]
    all_gather x3 -> x0, blocking collectives: 123 us -> none  [the longest x1 43.7 us: local(): lax.all_gather(kern_copy, ('wide', 'narrow'), axis=1, tiled=True)]
    pallas_call x0 -> x2, Pallas kernels: none -> 114 us  [the longest x1 73.8 us: reduce_all(): pl.pallas_call(reduce_kernel, out_shape=(jax.ShapeDtypeStruct((rows_in, w...]
    psum x2 -> x0, blocking collectives: 73.7 us -> none  [the longest x1 37 us: local(): scale_factor = 1.0 / lax.psum(local_tokens, ('wide', 'narrow'))]
    broadcast_in_dim x0 -> x49, local copies, waits for them, and re-layouts: none -> 38.5 us  [depthwise(): summed_taps = summed_taps + window * taps[row_tap * kernel_width + col_tap]]
    reduce_sum x4, other arithmetic: 65.9 us -> 86.5 us  [depthwise(): summed_taps = summed_taps + window * taps[row_tap * kernel_width + col_tap]]
  transfers between devices with their start and end apart: 7 -> 0, of which waited for: 5 -> 0; matrix products, arithmetic and copies ran while one was open for 26% -> 0% of each run, Pallas kernels for 0% -> 0%
where the time goes in v1:
time: 1050 us; the launch traced here: 1040 us
  other arithmetic  425 us (40%)
  local copies, waits for them, and re-layouts  259 us (25%)
  matrix products  236 us (22%)
  Pallas kernels  114 us (11%)
    reduce_sum x4, other arithmetic, depthwise(): summed_taps = summed_taps + window * taps[row_tap * kernel_width + col_tap]  86.5 us
    add_any x3, other arithmetic, depthwise(): window = padded[:, row_tap:row_tap + GRID, col_tap:col_tap + GRID, :]  80.3 us
    pallas_call x1, Pallas kernels, reduce_all(): pl.pallas_call(reduce_kernel, out_shape=(jax.ShapeDtypeStruct((rows_in, w...  73.8 us
    add x1, other arithmetic, attend(): depthwise(grid_values, crpe_taps * tap_mask(channels), 7) + crpe_shift  72 us
    mul x4, other arithmetic, depthwise(): summed_taps = summed_taps + window * taps[row_tap * kernel_width + col_tap]  67.8 us
    dot_general x3, matrix products, attend(): jnp.einsum('bnhd,bnhe->bhde', weights.reshape(shape_heads), values.reshap...  62.8 us
    dot_general x3, matrix products, attend(): jnp.einsum('bnhd,bhde->bnhe', queries.reshape(shape_heads), context, prec...  57.1 us
    pallas_call x1, Pallas kernels, gather_all(): pl.pallas_call(gather_kernel, out_shape=(jax.ShapeDtypeStruct((32,) + in_...  40.4 us

profile of v1, /device:TPU:0, one launch (start us, length us, event | category | flops | bytes accessed | tf_op | source)
XLA Modules:
  0.0 1041.5 jit_solution(13347648896718846108)
XLA Ops:
  12.7 5.1 reshape.697
  30.4 40.4 %gather_all.1 = (bf16[32,16,4096]{2,1,0:T(8,128)(2,1)}, bf16[32,64,512]{2,1,0:T(8,128)(2,1)}, bf16[32,16,128]{2,1,0:T(8,128)(2,1)}) custom-call(bf16[16,4096]{1,0:T(8,128)(2,1)} %convert_element_type.134.wi, bf16[64,512]{1,0:T(8,128)(2,1)} %convert_element_type.135.wo, bf16[16,128]{1,0:T(8,128)(2,1)} %fusion.74.sm), custom_call_target="tpu_custom_call" | custom-call | tf_op jit(solution)/shard_map/gather_all/pallas_call | solution.py:156
  91.1 5.5 add_add_fusion.4
  114.3 8.5 convolution_add_fusion
  122.9 11.3 %reshape.705 = f32[34,50,1536]{2,1,0:T(8,128)} reshape(f32[1700,1536]{1,0:T(8,128)} %convolution_add_fusion) | data formatting | bytes 20889600 | tf_op jit(solution)/shard_map/reshape | solution.py:560
  144.6 72.0 %add_add_fusion.3 = f32[34,7,7,512]{3,2,1,0:T(8,128)} fusion(f32[34,7,7,512]{3,2,1,0:T(8,128)} %reshape.709, f32[512]{0:T(512)S(1)} %copy-done.169, f32[512]{0:T(512)S(1)} %copy-done.83, f32[512]{0:T(512)S(1)} %copy-done.101, f32[512]{0:T(512)S(1)} %copy-done.121, f32[512]{0:T(512)S(1)} %copy-done.123, f32[512]{0:T(512)S(1)} %copy-done.125, ...), kind=kLoop, calls=%fused_computation.184 | loop fusion | flops 83593216 | bytes 6926336 | tf_op jit(solution)/shard_map/jvp()/add | solution.py:445
  216.6 15.4 %reshape.710 = f32[34,49,512]{2,1,0:T(8,128)} reshape(f32[34,7,7,512]{3,2,1,0:T(8,128)} %add_add_fusion.3) | data formatting | bytes 6823936 | tf_op jit(solution)/shard_map/jvp()/reshape | solution.py:446
  232.0 6.1 slice_multiply_fusion.2
  242.5 10.9 %fusion.99 = (f32[34,512]{1,0:T(8,128)S(1)}, f32[34,50,512]{2,1,0:T(8,128)}, f32[34,50,512]{2,1,0:T(8,128)}, f32[34,50,512]{2,1,0:T(8,128)}) fusion(f32[34,50,512]{2,1,0:T(8,128)} %fusion, f32[34,50,1536]{2,1,0:T(8,128)} %reshape.705), kind=kLoop, calls=%fused_computation.422 | loop fusion | flops 1723392 | bytes 24440832 | tf_op jit(solution)/shard_map/jvp()/reduce_sum | solution.py:434
  254.1 6.5 reshape.708
  265.2 6.5 reshape.706
  271.7 6.6 reshape.707
  278.3 23.3 %fusion.18 = f32[34,8,64,64]{3,2,1,0:T(8,128)S(1)} fusion(f32[34,50,8,64]{3,2,1,0:T(8,128)} %reshape.707, f32[34,50,8,64]{3,2,1,0:T(8,128)} %reshape.706), kind=kOutput, calls=%fused_computation.92 | convolution fusion | flops 668467200 | bytes 11419648 | tf_op jit(solution)/shard_map/jvp(bnhd,bnhe->bhde)/dot_general | solution.py:436
  301.6 15.7 %multiply_bitcast_fusion = f32[34,50,8,64]{3,1,2,0:T(8,128)} fusion(f32[34,8,64,64]{3,2,1,0:T(8,128)S(1)} %fusion.18, f32[34,50,8,64]{3,2,1,0:T(8,128)S(1)} %bitcast.145), kind=kOutput, calls=%fused_computation.84 | convolution fusion | flops 669337600 | bytes 11419648 | tf_op jit(solution)/shard_map/jvp(bnhd,bhde->bnhe)/dot_general | solution.py:442
  317.4 7.4 copy.243
  324.8 7.3 mul.1613
  347.4 39.3 %multiply_convert_fusion = (bf16[1700,2048]{1,0:T(8,128)(2,1)}, f32[1700,2048]{1,0:T(8,128)}, f32[1700,2048]{1,0:T(8,128)}) fusion(f32[2048]{0:T(1024)S(1)} %copy-done.174, bf16[512,4096]{1,0:T(8,128)(2,1)} %bitcast.161, f32[1700,512]{1,0:T(8,128)S(1)} %get-tuple-element.343, f32[512]{0:T(512)S(1)} %copy-done.177, f32[512]{0:T(512)S(1)} %copy-done.175, ...), kind=kOutput, calls=%fused_computation.62 | convolution fusion | flops 3799296000 | bytes 40420640 | tf_op jit(solution)/shard_map/dot_general | solution.py:576
  386.7 16.4 %convert_reduce_fusion = (f32[2048]{0:T(1024)S(1)}, bf16[1700,2048]{1,0:T(8,128)(2,1)}) fusion(f32[1700,2048]{1,0:T(8,128)} %get-tuple-element.252, bf16[1700,512]{1,0:T(8,128)(2,1)S(1)} %copy-done.24, bf16[2048,512]{1,0:T(8,128)(2,1)S(1)} %bitcast.224, f32[1700,2048]{1,0:T(8,128)} %get-tuple-element.344, f32[2048]{0:T(1024)S(1)} %copy-done.174), kind=kOutput, calls=%fused_computation.60 | convolution fusion | flops 3624343552 | bytes 38670336 | tf_op jit(solution)/shard_map/dot_general | solution.py:464
  403.1 8.4 add_convert_fusion.4
  420.4 9.8 convolution_convert_fusion.1
  430.2 8.1 multiply_reduce_fusion.62
  451.4 6.2 broadcast_multiply_fusion.58
  457.6 6.4 mul.1839
  464.0 20.1 %fusion.33 = f32[34,50,8,64]{3,1,2,0:T(8,128)S(1)} fusion(f32[34,8,64,64]{3,2,1,0:T(8,128)} %copy-done.4, f32[34,50,8,64]{3,2,1,0:T(8,128)} %mul.1839), kind=kOutput, calls=%fused_computation.205 | convolution fusion | flops 668467200 | bytes 11419648 | tf_op jit(solution)/shard_map/transpose(jvp(bnhd,bhde->bnhe))/dot_general | solution.py:442
  484.2 21.2 %fusion.9 = f32[34,8,64,64]{3,2,1,0:T(8,128)} fusion(f32[34,50,8,64]{3,2,1,0:T(8,128)S(1)} %copy-done.5, f32[34,50,8,64]{3,2,1,0:T(8,128)} %reshape.708), kind=kOutput, calls=%fused_computation.82 | convolution fusion | flops 668467200 | bytes 11419648 | tf_op jit(solution)/shard_map/transpose(jvp(bnhd,bhde->bnhe))/dot_general | solution.py:442
  509.5 7.2 reshape.720
  516.7 19.7 %fusion.28 = f32[34,50,8,64]{3,1,2,0:T(8,128)} fusion(f32[34,8,64,64]{3,2,1,0:T(8,128)} %fusion.9, f32[34,50,8,64]{3,2,1,0:T(8,128)} %reshape.707), kind=kOutput, calls=%fused_computation.204 | convolution fusion | flops 668467200 | bytes 11419648 | tf_op jit(solution)/shard_map/transpose(jvp(bnhd,bnhe->bhde))/dot_general | solution.py:436
  536.5 19.8 %fusion.25 = f32[34,50,8,64]{3,1,2,0:T(8,128)S(1)} fusion(f32[34,8,64,64]{3,2,1,0:T(8,128)} %fusion.9, f32[34,50,8,64]{3,2,1,0:T(8,128)} %reshape.706), kind=kOutput, calls=%fused_computation.203 | convolution fusion | flops 668467200 | bytes 11419648 | tf_op jit(solution)/shard_map/transpose(jvp(bnhd,bnhe->bhde))/dot_general | solution.py:436
  560.5 7.3 reshape.718
  567.7 7.4 copy.256
  575.1 7.5 reshape.719
  595.9 10.8 %fusion.84 = (f32[512]{0:T(512)S(1)}, f32[512]{0:T(512)S(1)}, f32[34,49,512]{2,1,0:T(8,128)}, f32[34,49,512]{2,1,0:T(8,128)S(1)}) fusion(f32[34,50,1536]{2,1,0:T(8,128)} %reshape.705, f32[34,50,512]{2,1,0:T(8,128)} %reshape.715, f32[34,49,512]{2,1,0:T(8,128)} %reshape.710), kind=kLoop, calls=%fused_computation.414 | loop fusion | flops 4263936 | bytes 20475904 | tf_op jit(solution)/shard_map/transpose(jvp())/reduce_sum | solution.py:445
  606.7 5.0 pad_add_fusion.15
  617.8 31.4 %multiply_reduce_fusion.48 = (f32[512]{0:T(512)S(1)}, f32[512]{0:T(512)S(1)}, f32[512]{0:T(512)S(1)}, f32[512]{0:T(512)S(1)}, f32[512]{0:T(512)S(1)}, /*index=5*...) fusion(f32[34,7,7,512]{3,2,1,0:T(8,128)} %reshape.716, ...), kind=kLoop, calls=%fused_computation.163 | loop fusion | flops 30698496 | bytes 6860800 | tf_op jit(solution)/shard_map/transpose(jvp())/reduce_sum | solution.py:398
  649.2 9.2 multiply_reduce_fusion.49
  686.7 23.1 %multiply_reduce_fusion.47 = (f32[512]{0:T(512)S(1)}, f32[512]{0:T(512)S(1)}, f32[512]{0:T(512)S(1)}, f32[512]{0:T(512)S(1)}, f32[512]{0:T(512)S(1)}, /*index=5*...) fusion(f32[34,7,7,512]{3,2,1,0:T(8,128)} %reshape.716, ...), kind=kLoop, calls=%fused_computation.162 | loop fusion | flops 25583616 | bytes 27332608 | tf_op jit(solution)/shard_map/transpose(jvp())/reduce_sum | solution.py:398
  720.2 8.6 add_select_fusion
  729.1 9.4 broadcast_multiply_fusion.2
  738.8 22.4 %broadcast_multiply_fusion.1 = (f32[34,7,7,512]{3,2,1,0:T(8,128)}, f32[34,7,7,512]{3,2,1,0:T(8,128)}, f32[34,7,7,512]{3,2,1,0:T(8,128)}, f32[34,7,7,512]{3,2,1,0...) fusion(f32[34,7,7,512]{3,2,1,0:T(8,128)S(1)} %copy-done.1, ...), kind=kLoop, calls=%fused_computation.213 | loop fusion | flops 15353856 | bytes 64864256 | tf_op jit(solution)/shard_map/transpose(jvp())/mul | solution.py:398
  761.4 22.5 %broadcast_multiply_fusion = (f32[34,7,7,512]{3,2,1,0:T(8,128)}, f32[34,7,7,512]{3,2,1,0:T(8,128)}, f32[34,7,7,512]{3,2,1,0:T(8,128)}, f32[34,7,7,512]{3,2,1,0:T...) fusion(f32[34,7,7,512]{3,2,1,0:T(8,128)S(1)} %copy-done.1, ...), kind=kLoop, calls=%fused_computation.212 | loop fusion | flops 15353856 | bytes 64864256 | tf_op jit(solution)/shard_map/transpose(jvp())/mul | solution.py:398
  784.0 59.1 %pad_add_fusion = f32[34,13,13,512]{3,2,1,0:T(8,128)} fusion(f32[34,7,7,512]{3,2,1,0:T(8,128)} %get-tuple-element.277, f32[34,7,7,512]{3,2,1,0:T(8,128)} %get-tuple-element.278, f32[34,7,7,512]{3,2,1,0:T(8,128)} %get-tuple-element.279, f32[34,7,7,512]{3,2,1,0:T(8,128)} %get-tuple-element.280, f32[34,7,7,512]{3,2,1,0:T(8,128)} %get-tuple-element.281, ...), kind=kLoop, calls=%fused_computation.58 | loop fusion | flops 123561984 | bytes 158482432 | tf_op jit(solution)/shard_map/transpose(jvp())/add_any | solution.py:397
  843.1 10.5 %pad_add_fusion.8 = f32[34,7,7,512]{3,2,1,0:T(8,128)} fusion(f32[34,7,7,512]{3,2,1,0:T(8,128)} %get-tuple-element.259, f32[34,7,7,512]{3,2,1,0:T(8,128)} %get-tuple-element.260, f32[34,7,7,512]{3,2,1,0:T(8,128)} %get-tuple-element.261, f32[34,7,7,512]{3,2,1,0:T(8,128)} %get-tuple-element.262, f32[34,7,7,512]{3,2,1,0:T(8,128)} %get-tuple-element.263, ...), kind=kLoop, calls=%fused_computation.107 | loop fusion | flops 5117952 | bytes 27295744 | tf_op jit(solution)/shard_map/transpose(jvp())/add_any | solution.py:397
  866.1 5.6 fusion.85
  896.3 13.4 %broadcast_multiply_fusion.49 = (f32[34,7,7,512]{3,2,1,0:T(8,128)}, f32[34,7,7,512]{3,2,1,0:T(8,128)}, f32[34,7,7,512]{3,2,1,0:T(8,128)}, f32[34,7,7,512]{3,2,1,...) fusion(f32[34,7,7,512]{3,2,1,0:T(8,128)} %reshape.721, ...), kind=kLoop, calls=%fused_computation.263 | loop fusion | flops 7676928 | bytes 34138112 | tf_op jit(solution)/shard_map/transpose(jvp())/mul | solution.py:398
  909.7 10.7 %pad_add_fusion.1 = f32[34,9,9,512]{3,2,1,0:T(8,128)} fusion(f32[34,7,7,512]{3,2,1,0:T(8,128)} %get-tuple-element.274, f32[34,7,7,512]{3,2,1,0:T(8,128)} %get-tuple-element.275, f32[34,7,7,512]{3,2,1,0:T(8,128)} %get-tuple-element.267), kind=kLoop, calls=%fused_computation.78 | loop fusion | flops 2820096 | bytes 15876096 | tf_op jit(solution)/shard_map/transpose(jvp())/add_any | solution.py:397
  920.4 22.7 %multiply_reduce_fusion.58 = (f32[512]{0:T(512)S(1)}, f32[512]{0:T(512)S(1)}, f32[512]{0:T(512)S(1)}, f32[512]{0:T(512)S(1)}, f32[512]{0:T(512)S(1)}, /*index=5*...) fusion(f32[34,7,7,512]{3,2,1,0:T(8,128)} %reshape.721, f32[34,7,7,512]{3,2,1,0:T(8,128)} %reshape.697, ...), kind=kLoop, calls=%fused_computation.173 | loop fusion | flops 19614720 | bytes 34136064 | tf_op jit(solution)/shard_map/transpose(jvp())/reduce_sum | solution.py:398
  948.6 73.8 %reduce_all.1 = (f32[16,4096]{1,0:T(8,128)S(1)}, f32[64,512]{1,0:T(8,128)S(1)}, f32[16,128]{1,0:T(8,128)S(1)}, f32[8,128]{1,0:T(8,128)S(1)}) custom-call(bf16[4,2,2,2,16,4096]{5,4,3,2,1,0:T(8,128)(2,1)} %pad_maximum_fusion.gi, bf16[4,2,2,2,64,512]{5,4,3,2,1,0:T(8,128)(2,1)S(1)} %bitcast.141, f32[4,2,2,2,16,128]{5,4,3,2,1,0:T(8,128)S(1)} %bitcast.142), custom_call_target="tpu_custom_call" | custom-call | tf_op jit(solution)/shard_map/reduce_all/pallas_call | solution.py:367
  1033.7 6.2 pad_add_fusion.14
  (587 shorter events, 236.7 us)
Async XLA Ops:
  2.0 78.7 %copy-start.179 = (s32[49]{0:T(128)}, s32[49]{0:T(128)S(1)}, u32[]{:S(2)}) copy-start(s32[49]{0:T(128)S(1)} %get-tuple-element.351) | copy-start | bytes 592
  2.0 78.7 %copy-start.181 = (s32[49]{0:T(128)}, s32[49]{0:T(128)S(1)}, u32[]{:S(2)}) copy-start(s32[49]{0:T(128)S(1)} %get-tuple-element.352) | copy-start | bytes 592
  2.0 78.7 %copy-start.167 = (s32[512]{0:T(512)}, s32[512]{0:T(512)S(1)}, u32[]{:S(2)}) copy-start(s32[512]{0:T(512)S(1)} %select_select_fusion) | copy-start | bytes 6148
  84.5 59.7 %copy-start.49 = (f32[512]{0:T(512)}, f32[512]{0:T(512)S(1)}, u32[]{:S(2)}) copy-start(f32[512]{0:T(512)S(1)} %get-tuple-element.212) | copy-start | bytes 6148
  84.5 59.7 %copy-start.51 = (f32[512]{0:T(512)}, f32[512]{0:T(512)S(1)}, u32[]{:S(2)}) copy-start(f32[512]{0:T(512)S(1)} %get-tuple-element.213) | copy-start | bytes 6148
  84.5 59.7 %copy-start.53 = (f32[512]{0:T(512)}, f32[512]{0:T(512)S(1)}, u32[]{:S(2)}) copy-start(f32[512]{0:T(512)S(1)} %get-tuple-element.214) | copy-start | bytes 6148
  84.5 59.7 %copy-start.55 = (f32[512]{0:T(512)}, f32[512]{0:T(512)S(1)}, u32[]{:S(2)}) copy-start(f32[512]{0:T(512)S(1)} %get-tuple-element.215) | copy-start | bytes 6148
  84.5 59.7 %copy-start.57 = (f32[512]{0:T(512)}, f32[512]{0:T(512)S(1)}, u32[]{:S(2)}) copy-start(f32[512]{0:T(512)S(1)} %get-tuple-element.216) | copy-start | bytes 6148
  84.5 59.7 %copy-start.59 = (f32[512]{0:T(512)}, f32[512]{0:T(512)S(1)}, u32[]{:S(2)}) copy-start(f32[512]{0:T(512)S(1)} %get-tuple-element.217) | copy-start | bytes 6148
  84.5 59.7 %copy-start.61 = (f32[512]{0:T(512)}, f32[512]{0:T(512)S(1)}, u32[]{:S(2)}) copy-start(f32[512]{0:T(512)S(1)} %get-tuple-element.218) | copy-start | bytes 6148
  87.8 56.4 %copy-start.63 = (f32[512]{0:T(512)}, f32[512]{0:T(512)S(1)}, u32[]{:S(2)}) copy-start(f32[512]{0:T(512)S(1)} %get-tuple-element.201) | copy-start | bytes 6148
  87.8 56.4 %copy-start.65 = (f32[512]{0:T(512)}, f32[512]{0:T(512)S(1)}, u32[]{:S(2)}) copy-start(f32[512]{0:T(512)S(1)} %get-tuple-element.202) | copy-start | bytes 6148
  87.8 56.4 %copy-start.67 = (f32[512]{0:T(512)}, f32[512]{0:T(512)S(1)}, u32[]{:S(2)}) copy-start(f32[512]{0:T(512)S(1)} %get-tuple-element.203) | copy-start | bytes 6148
  87.8 56.4 %copy-start.69 = (f32[512]{0:T(512)}, f32[512]{0:T(512)S(1)}, u32[]{:S(2)}) copy-start(f32[512]{0:T(512)S(1)} %get-tuple-element.204) | copy-start | bytes 6148
  87.8 56.4 %copy-start.71 = (f32[512]{0:T(512)}, f32[512]{0:T(512)S(1)}, u32[]{:S(2)}) copy-start(f32[512]{0:T(512)S(1)} %get-tuple-element.205) | copy-start | bytes 6148
  87.8 56.4 %copy-start.73 = (f32[512]{0:T(512)}, f32[512]{0:T(512)S(1)}, u32[]{:S(2)}) copy-start(f32[512]{0:T(512)S(1)} %get-tuple-element.206) | copy-start | bytes 6148
  87.8 56.4 %copy-start.75 = (f32[512]{0:T(512)}, f32[512]{0:T(512)S(1)}, u32[]{:S(2)}) copy-start(f32[512]{0:T(512)S(1)} %get-tuple-element.207) | copy-start | bytes 6148
  87.8 56.4 %copy-start.77 = (f32[512]{0:T(512)}, f32[512]{0:T(512)S(1)}, u32[]{:S(2)}) copy-start(f32[512]{0:T(512)S(1)} %get-tuple-element.208) | copy-start | bytes 6148
  87.9 56.4 %copy-start.79 = (f32[512]{0:T(512)}, f32[512]{0:T(512)S(1)}, u32[]{:S(2)}) copy-start(f32[512]{0:T(512)S(1)} %get-tuple-element.209) | copy-start | bytes 6148
  271.7 29.9 %slice-start = ((s8[6963200]{0:T(1024)(128)(4,1)}), s8[2768896]{0:T(1024)(128)(4,1)S(1)}, s32[]{:S(2)}) async-start(s8[6963200]{0:T(1024)(128)(4,1)} %bitcast.144), calls=%async_computation | async-start | bytes 5537792
  341.9 61.2 %copy-start.7 = (f32[1700,512]{1,0:T(8,128)}, f32[1700,512]{1,0:T(8,128)S(1)}, u32[]{:S(2)}) copy-start(f32[1700,512]{1,0:T(8,128)S(1)} %get-tuple-element.343) | copy-start | bytes 10444804
  347.4 39.3 %copy-start.24 = (bf16[1700,512]{1,0:T(8,128)(2,1)S(1)}, bf16[1700,512]{1,0:T(8,128)(2,1)}, u32[]{:S(2)}) copy-start(bf16[1700,512]{1,0:T(8,128)(2,1)} %convert_element_type.152) | copy-start | bytes 5222404
  347.4 39.3 %copy-start.187 = (bf16[32,64,512]{2,1,0:T(8,128)(2,1)S(1)}, bf16[32,64,512]{2,1,0:T(8,128)(2,1)}, u32[]{:S(2)}) copy-start(bf16[32,64,512]{2,1,0:T(8,128)(2,1)} %get-tuple-element.32) | copy-start | bytes 6291460
  617.8 31.4 %copy-start = (f32[34,7,7,512]{3,2,1,0:T(8,128)S(1)}, f32[34,7,7,512]{3,2,1,0:T(8,128)}, u32[]{:S(2)}) copy-start(f32[34,7,7,512]{3,2,1,0:T(8,128)} %reshape.716) | copy-start | bytes 10235908
  617.8 31.4 %copy-start.3 = (f32[34,7,7,512]{3,2,1,0:T(8,128)S(1)}, f32[34,7,7,512]{3,2,1,0:T(8,128)}, u32[]{:S(2)}) copy-start(f32[34,7,7,512]{3,2,1,0:T(8,128)} %reshape.709) | copy-start | bytes 10235908
  660.8 25.8 %copy-start.136 = (f32[512]{0:T(512)S(1)}, f32[512]{0:T(512)}, u32[]{:S(2)}) copy-start(f32[512]{0:T(512)} %get-tuple-element.211) | copy-start | bytes 6148
  660.8 25.8 %copy-start.138 = (f32[512]{0:T(512)S(1)}, f32[512]{0:T(512)}, u32[]{:S(2)}) copy-start(f32[512]{0:T(512)} %get-tuple-element.219) | copy-start | bytes 6148
  660.8 25.8 %copy-start.140 = (f32[512]{0:T(512)S(1)}, f32[512]{0:T(512)}, u32[]{:S(2)}) copy-start(f32[512]{0:T(512)} %get-tuple-element.220) | copy-start | bytes 6148
  660.8 25.8 %copy-start.142 = (f32[512]{0:T(512)S(1)}, f32[512]{0:T(512)}, u32[]{:S(2)}) copy-start(f32[512]{0:T(512)} %get-tuple-element.221) | copy-start | bytes 6148
  660.9 25.8 %copy-start.144 = (f32[512]{0:T(512)S(1)}, f32[512]{0:T(512)}, u32[]{:S(2)}) copy-start(f32[512]{0:T(512)} %get-tuple-element.192) | copy-start | bytes 6148
  660.9 25.8 %copy-start.146 = (f32[512]{0:T(512)S(1)}, f32[512]{0:T(512)}, u32[]{:S(2)}) copy-start(f32[512]{0:T(512)} %get-tuple-element.173) | copy-start | bytes 6148
  686.7 33.4 %copy-start.168 = (s32[512]{0:T(512)S(1)}, s32[512]{0:T(512)}, u32[]{:S(2)}) copy-start(s32[512]{0:T(512)} %copy-done.167) | copy-start | bytes 6148
  686.7 33.4 %copy-start.180 = (s32[49]{0:T(128)S(1)}, s32[49]{0:T(128)}, u32[]{:S(2)}) copy-start(s32[49]{0:T(128)} %copy-done.179) | copy-start | bytes 592
  686.7 33.4 %copy-start.182 = (s32[49]{0:T(128)S(1)}, s32[49]{0:T(128)}, u32[]{:S(2)}) copy-start(s32[49]{0:T(128)} %copy-done.181) | copy-start | bytes 592
  920.4 23.6 %copy-start.30 = (f32[1,32,16]{0,2,1:T(8,128)S(1)}, f32[1,32,16]{0,2,1:T(8,128)}, u32[]{:S(2)}) copy-start(f32[1,32,16]{0,2,1:T(8,128)} %concatenate.82) | copy-start | bytes 6148
  948.4 75.5 %copy-start.183 = (f32[2,16]{1,0:T(2,128)S(1)}, f32[2,16]{1,0:T(2,128)}, u32[]{:S(2)}) copy-start(f32[2,16]{1,0:T(2,128)} %param.30) | copy-start | bytes 388
  948.4 75.5 %copy-start.184 = (f32[2,16]{1,0:T(2,128)S(1)}, f32[2,16]{1,0:T(2,128)}, u32[]{:S(2)}) copy-start(f32[2,16]{1,0:T(2,128)} %param.31) | copy-start | bytes 388
  948.4 75.5 %copy-start.185 = (f32[2,16]{1,0:T(2,128)S(1)}, f32[2,16]{1,0:T(2,128)}, u32[]{:S(2)}) copy-start(f32[2,16]{1,0:T(2,128)} %param.32) | copy-start | bytes 388
  948.4 76.1 %copy-start.47 = (f32[12,16]{1,0:T(8,128)S(1)}, f32[12,16]{1,0:T(8,128)}, u32[]{:S(2)}) copy-start(f32[12,16]{1,0:T(8,128)} %param.33) | copy-start | bytes 2308
  948.4 76.1 %copy-start.170 = (f32[12,16]{1,0:T(8,128)S(1)}, f32[12,16]{1,0:T(8,128)}, u32[]{:S(2)}) copy-start(f32[12,16]{1,0:T(8,128)} %param.34) | copy-start | bytes 2308
  948.4 76.1 %copy-start.171 = (f32[12,16]{1,0:T(8,128)S(1)}, f32[12,16]{1,0:T(8,128)}, u32[]{:S(2)}) copy-start(f32[12,16]{1,0:T(8,128)} %param.35) | copy-start | bytes 2308
  948.5 76.8 %copy-start.48 = (f32[58,16]{0,1:T(8,128)S(1)}, f32[58,16]{0,1:T(8,128)}, u32[]{:S(2)}) copy-start(f32[58,16]{0,1:T(8,128)} %param.27) | copy-start | bytes 11140
  948.5 76.8 %copy-start.172 = (f32[58,16]{0,1:T(8,128)S(1)}, f32[58,16]{0,1:T(8,128)}, u32[]{:S(2)}) copy-start(f32[58,16]{0,1:T(8,128)} %param.28) | copy-start | bytes 11140
  948.5 76.8 %copy-start.173 = (f32[58,16]{0,1:T(8,128)S(1)}, f32[58,16]{0,1:T(8,128)}, u32[]{:S(2)}) copy-start(f32[58,16]{0,1:T(8,128)} %param.29) | copy-start | bytes 11140
  948.5 77.4 %copy-start.34 = (f32[64,512]{1,0:T(8,128)S(1)}, f32[64,512]{1,0:T(8,128)}, u32[]{:S(2)}) copy-start(f32[64,512]{1,0:T(8,128)} %param.24) | copy-start | bytes 393220
  948.6 79.1 %copy-start.32 = (f32[16,4096]{1,0:T(8,128)S(1)}, f32[16,4096]{1,0:T(8,128)}, u32[]{:S(2)}) copy-start(f32[16,4096]{1,0:T(8,128)} %param.21) | copy-start | bytes 786436
  948.6 79.1 %copy-start.40 = (f32[16,4096]{1,0:T(8,128)S(1)}, f32[16,4096]{1,0:T(8,128)}, u32[]{:S(2)}) copy-start(f32[16,4096]{1,0:T(8,128)} %param.22) | copy-start | bytes 786436
  948.6 79.1 %copy-start.41 = (f32[16,4096]{1,0:T(8,128)S(1)}, f32[16,4096]{1,0:T(8,128)}, u32[]{:S(2)}) copy-start(f32[16,4096]{1,0:T(8,128)} %param.23) | copy-start | bytes 786436
  (143 other events, 1318.0 us)

commit v2 on v1

--- a/solution.py
+++ b/solution.py
@@ -382,23 +382,6 @@
     )(gi, go, gs)
 
 
-def layer_norm(values, gain_row, shift_row):
-    centred = values - jnp.mean(values, axis=-1, keepdims=True)
-    variance = jnp.mean(centred * centred, axis=-1, keepdims=True)
-    return centred * lax.rsqrt(variance + NORM_EPS) * gain_row + shift_row
-
-
-def depthwise(patch_grid, taps, kernel_width):
-    margin = kernel_width // 2
-    padded = jnp.pad(patch_grid, ((0, 0), (margin, margin), (margin, margin), (0, 0)))
-    summed_taps = jnp.zeros_like(patch_grid)
-    for row_tap in range(kernel_width):
-        for col_tap in range(kernel_width):
-            window = padded[:, row_tap : row_tap + GRID, col_tap : col_tap + GRID, :]
-            summed_taps = summed_taps + window * taps[row_tap * kernel_width + col_tap]
-    return summed_taps
-
-
 def tap_mask(channels):
     head_width = channels // HEADS
     channel_ids = jnp.arange(channels, dtype=jnp.int32)
@@ -414,60 +397,522 @@
     return inside.astype(jnp.float32)
 
 
-def pre_block(inputs, cpe_taps, cpe_shift, gain_row, shift_row):
-    num_images, num_tokens, channels = inputs.shape
-    patches = inputs[:, 1:].reshape(num_images, GRID, GRID, channels)
-    mixed = patches + depthwise(patches, cpe_taps, 3) + cpe_shift
-    after_cpe = jnp.concatenate(
-        [inputs[:, :1], mixed.reshape(num_images, GRID * GRID, channels)], axis=1
-    )
-    return (after_cpe, layer_norm(after_cpe, gain_row, shift_row))
-
-
-def attend(qkv_rows, crpe_taps, crpe_shift):
-    num_images, num_tokens, triple = qkv_rows.shape
-    channels = triple // 3
-    head_width = channels // HEADS
-    queries = qkv_rows[..., :channels]
-    key_rows = qkv_rows[..., channels : 2 * channels]
-    values = qkv_rows[..., 2 * channels :]
-    weights = jax.nn.softmax(key_rows, axis=1)
-    shape_heads = (num_images, num_tokens, HEADS, head_width)
-    context = jnp.einsum(
-        "bnhd,bnhe->bhde",
-        weights.reshape(shape_heads),
-        values.reshape(shape_heads),
-        precision=HIGHEST,
-    )
-    factor = jnp.einsum("bnhd,bhde->bnhe", queries.reshape(shape_heads), context, precision=HIGHEST)
-    factor = factor.reshape(num_images, num_tokens, channels)
-    grid_values = values[:, 1:].reshape(num_images, GRID, GRID, channels)
-    conv_values = depthwise(grid_values, crpe_taps * tap_mask(channels), 7) + crpe_shift
-    relative = queries[:, 1:] * conv_values.reshape(num_images, GRID * GRID, channels)
-    relative = jnp.concatenate(
-        [jnp.zeros((num_images, 1, channels), jnp.float32), relative], axis=1
-    )
-    return factor * head_width ** (-0.5) + relative
-
-
-def gelu_exact(values):
-    return jax.nn.gelu(values, approximate=False)
-
-
 def cross_rows(left, right):
     return lax.dot_general(
         left, right, (((0,), (0,)), ((), ())), preferred_element_type=jnp.float32
     )
 
 
-def transposed(gradient, weight):
+SIDE = 8
+SLOT = 64
+CHUNK = 10
+
+
+def rows_of(ref):
+    return ref[...].reshape(-1, ref.shape[-1])
+
+
+def tokens_of(value):
+    return value.reshape(-1, SIDE, value.shape[-1])
+
+
+def column_partial(value):
+    return jnp.sum(tokens_of(value), axis=0)
+
+
+def dot(left, right):
+    return jnp.dot(left, right, preferred_element_type=jnp.float32)
+
+
+def dot_nt(left, right):
     return lax.dot_general(
-        gradient, weight, (((1,), (1,)), ((), ())), preferred_element_type=jnp.float32
-    )
-
-
-def column_sums(rounded):
-    return jnp.sum(rounded.astype(jnp.float32), axis=0)
+        left, right, (((1,), (1,)), ((), ())), preferred_element_type=jnp.float32
+    )
+
+
+def dot_tn(left, right):
+    return lax.dot_general(
+        left, right, (((0,), (0,)), ((), ())), preferred_element_type=jnp.float32
+    )
+
+
+def lane_tile(j):
+    if isinstance(j, int):
+        return pl.ds(j * 128, 128)
+    return pl.ds(pl.multiple_of(j * 128, 128), 128)
+
+
+def grid_token(row, col):
+    return 1 + row * GRID + col
+
+
+def conv_tile(src, taps, base, width, reach, lanes, finish, flip=False):
+    margin = width // 2
+    offsets = range(-reach, reach + 1)
+
+    def tap(dy, dx):
+        if flip:
+            dy, dx = -dy, -dx
+        index = base + (dy + margin) * width + dx + margin
+        return jnp.broadcast_to(taps[index : index + 1, lanes], (SIDE, 128))
+
+    held = {(dy, dx): tap(dy, dx) for dy in offsets for dx in offsets}
+    for row in range(GRID):
+        sums = [jnp.zeros((SIDE, 128), jnp.float32) for _ in range(GRID)]
+        for dy in offsets:
+            if not 0 <= row + dy < GRID:
+                continue
+            line = [src[grid_token(row + dy, col), :, lanes] for col in range(GRID)]
+            for dx in offsets:
+                for col in range(GRID):
+                    if 0 <= col + dx < GRID:
+                        sums[col] = sums[col] + line[col + dx] * held[dy, dx]
+        for col in range(GRID):
+            finish(grid_token(row, col), sums[col])
+
+
+def tap_sums(grad, src, base, width, reach, lanes, total):
+    margin = width // 2
+    offsets = range(-reach, reach + 1)
+    for dy in offsets:
+        sums = {dx: jnp.zeros((SIDE, 128), jnp.float32) for dx in offsets}
+        for row in range(GRID):
+            if not 0 <= row + dy < GRID:
+                continue
+            up = [grad[grid_token(row, col), :, lanes] for col in range(GRID)]
+            line = [src[grid_token(row + dy, col), :, lanes] for col in range(GRID)]
+            for dx in offsets:
+                for col in range(GRID):
+                    if 0 <= col + dx < GRID:
+                        sums[dx] = sums[dx] + up[col] * line[col + dx]
+        for dx in offsets:
+            index = base + (dy + margin) * width + dx + margin
+            total[index, :, lanes] = total[index, :, lanes] + sums[dx]
+
+
+REACHES = ((0, 1), (1, 2))
+
+
+def relative_tiles(body):
+    body(0, 1)
+    body(1, 2)
+
+    def rest(j, carry):
+        body(j, 3)
+        return carry
+
+    lax.fori_loop(2, 4, rest, 0)
+
+
+def all_tiles(body):
+    def step(j, carry):
+        body(j)
+        return carry
+
+    lax.fori_loop(0, 4, step, 0)
+
+
+def all_chunks(body):
+    def step(k, carry):
+        body(pl.ds(k * CHUNK, CHUNK), pl.ds(pl.multiple_of(k * CHUNK * SIDE, 16), CHUNK * SIDE))
+        return carry
+
+    lax.fori_loop(0, 50 // CHUNK, step, 0)
+
+
+def normalise(values):
+    centred = values - jnp.mean(values, axis=-1, keepdims=True)
+    scale = lax.rsqrt(jnp.mean(centred * centred, axis=-1, keepdims=True) + NORM_EPS)
+    return centred * scale, scale
+
+
+def norm_back(grad, hat, scale, gain):
+    inner = grad * gain
+    mean = jnp.mean(inner, axis=-1, keepdims=True)
+    along = jnp.mean(inner * hat, axis=-1, keepdims=True)
+    return scale * (inner - mean - hat * along)
+
+
+def take_images(src, slots, first, limit):
+    for i in range(SIDE):
+        image = src[i]
+        keep = jnp.full(image.shape, first + i, jnp.int32) < limit
+        image = jnp.where(keep, image.astype(jnp.float32), 0.0).astype(jnp.bfloat16)
+        slots[i * SLOT : i * SLOT + image.shape[0], :] = image
+
+
+def forward_kernel(
+    num_images, counts, x_in, dy_in, order, same, w_in, w_out, taps, gains, biases,
+    out, act_o, gh_o, n1_o, n2_o, at_o, gf_o, gp_o, gx_o, xt_o, hat_o, sc_o, q_o, k_o, v_o, cv_o,
+    cols_o, hcols_o,
+    slots, x, x1, v, conv, hat2, slope, gn, scale2,
+):
+    low = jnp.bfloat16
+    step = pl.program_id(0)
+    first = step * SIDE
+
+    @pl.when(step == 0)
+    def _():
+        slots[...] = jnp.zeros_like(slots)
+        cols_o[...] = jnp.zeros_like(cols_o)
+        hcols_o[...] = jnp.zeros_like(hcols_o)
+
+    take_images(x_in, slots, first, num_images)
+    value = dot(order[...], slots[...])
+    x[...] = tokens_of(value)
+    xt_o[...] = value.astype(low)
+    take_images(dy_in, slots, first, jnp.minimum(counts[0], num_images))
+    gf_o[...] = dot(order[...], slots[...]).astype(low)
+
+    def position(j):
+        lanes = lane_tile(j)
+        shift = jnp.broadcast_to(biases[10:11, lanes], (SIDE, 128))
+
+        def finish(token, total):
+            x1[token, :, lanes] = x[token, :, lanes] + total + shift
+
+        conv_tile(x, taps, 0, 3, 1, lanes, finish)
+        x1[0, :, lanes] = x[0, :, lanes]
+
+    all_tiles(position)
+
+    def first_norm(tokens, rows):
+        hat, scale = normalise(x1[tokens].reshape(-1, D))
+        hat_o[rows, :] = hat.astype(low)
+        sc_o[rows, :] = jnp.broadcast_to(scale, (CHUNK * SIDE, 128))
+        n1_o[rows, :] = (hat * gains[0:1, :] + biases[0:1, :]).astype(low)
+
+    all_chunks(first_norm)
+    n1 = n1_o[...]
+    gn[...] = tokens_of(dot(n1, w_in[:, D : 2 * D]))
+
+    def weights(j):
+        lanes = lane_tile(j)
+        keys = gn[:, :, lanes]
+        powers = jnp.exp(keys - jnp.max(keys, axis=0, keepdims=True))
+        share = 0.125 / jnp.sum(powers, axis=0, keepdims=True)
+        k_o[:, lanes] = (powers * share).reshape(-1, 128).astype(low)
+
+    all_tiles(weights)
+    value = dot(n1, w_in[:, 2 * D : 3 * D]) + biases[3:4, :]
+    v[...] = tokens_of(value)
+    v_o[...] = value.astype(low)
+
+    def relative(j, reach):
+        lanes = lane_tile(j)
+        shift = jnp.broadcast_to(biases[11:12, lanes], (SIDE, 128))
+
+        def finish(token, total):
+            conv[token, :, lanes] = total + shift
+
+        conv_tile(v, taps, 9, 7, reach, lanes, finish)
+        conv[0, :, lanes] = jnp.zeros((SIDE, 128), jnp.float32)
+
+    relative_tiles(relative)
+    cv_o[...] = rows_of(conv).astype(low)
+    value = dot(n1, w_in[:, :D]) + biases[2:3, :]
+    q_o[...] = value.astype(low)
+    conv[...] = conv[...] * tokens_of(value)
+
+    def attention(j):
+        lanes = lane_tile(j)
+        qs, ks, vs = q_o[:, lanes], k_o[:, lanes], v_o[:, lanes]
+        parts = []
+        for h in (slice(0, 64), slice(64, 128)):
+            scores = dot_nt(qs[:, h], ks[:, h]).astype(low) * same[...]
+            parts.append(dot(scores, vs[:, h]))
+        value = jnp.concatenate(parts, axis=1) + conv[:, :, lanes].reshape(-1, 128)
+        at_o[:, lanes] = value.astype(low)
+
+    all_tiles(attention)
+    x1[...] = x1[...] + tokens_of(dot(at_o[...], w_in[:, 3 * D : 4 * D]) + biases[4:5, :])
+
+    def second_norm(tokens, rows):
+        hat, scale = normalise(x1[tokens].reshape(-1, D))
+        hat2[tokens] = tokens_of(hat)
+        scale2[tokens] = jnp.broadcast_to(tokens_of(scale), (CHUNK, SIDE, 128))
+        n2_o[rows, :] = (hat * gains[1:2, :] + biases[1:2, :]).astype(low)
+
+    all_chunks(second_norm)
+    n2 = n2_o[...]
+    for part in range(MLP_WIDTH // D):
+        cols = pl.ds(part * D, D)
+        gn[...] = tokens_of(dot(n2, w_in[:, pl.ds((4 + part) * D, D)]))
+
+        def gelu(tokens, rows):
+            h = gn[tokens].reshape(-1, D) + biases[5 + part : 6 + part, :]
+            below = 0.5 + 0.5 * lax.erf(h * (0.5**0.5))
+            density = jnp.exp(-0.5 * h * h) * 0.3989422804014327
+            act_o[rows, cols] = (h * below).astype(low)
+            slope[rows, cols] = below + h * density
+
+        all_chunks(gelu)
+    value = rows_of(x1) + dot(act_o[...], w_out[...]) + biases[9:10, :]
+    back = lax.dot_general(
+        order[...], value.astype(low), (((0,), (0,)), ((), ())), preferred_element_type=jnp.float32
+    )
+    for i in range(SIDE):
+        out[i] = back[i * SLOT : i * SLOT + out.shape[1], :].astype(low)
+
+    gf = gf_o[...]
+    for part in range(MLP_WIDTH // D):
+        cols = pl.ds(part * D, D)
+        grad = (dot_nt(gf, w_out[cols, :]) * slope[:, cols]).astype(low)
+        gh_o[:, cols] = grad
+        hcols_o[:, cols] = hcols_o[:, cols] + column_partial(grad.astype(jnp.float32))
+    gn[...] = tokens_of(dot_nt(gh_o[...], w_in[:, 4 * D :]))
+
+    def second_back(tokens, rows):
+        grad = gn[tokens].reshape(-1, D)
+        hat = hat2[tokens].reshape(-1, D)
+        scale = scale2[tokens].reshape(-1, 128)[:, 0:1]
+        upstream = gf_o[rows, :].astype(jnp.float32)
+        total = upstream + norm_back(grad, hat, scale, gains[1:2, :])
+        gx_o[rows, :] = total
+        rounded = total.astype(low)
+        gp_o[rows, :] = rounded
+        cols_o[0] = cols_o[0] + column_partial(grad)
+        cols_o[1] = cols_o[1] + column_partial(grad * hat)
+        cols_o[2] = cols_o[2] + column_partial(rounded.astype(jnp.float32))
+        cols_o[3] = cols_o[3] + column_partial(upstream)
+
+    all_chunks(second_back)
+
+
+def backward_kernel(
+    num_images, order, same, w_in, taps, gains, gx, hat, sc, q, k, v, cv, xt,
+    out, gq_o, cols_o, taps_o,
+    ga, gc, vf, gv, gqs, gks, xf, g1,
+):
+    low = jnp.bfloat16
+    step = pl.program_id(0)
+
+    @pl.when(step == 0)
+    def _():
+        cols_o[...] = jnp.zeros_like(cols_o)
+        taps_o[...] = jnp.zeros_like(taps_o)
+
+    grad = dot_nt(gx[...].astype(low), w_in[:, 3 * D : 4 * D])
+    ga[...] = grad.astype(low)
+    gqs[...] = tokens_of(grad * cv[...].astype(jnp.float32))
+    gc[...] = tokens_of(grad * q[...].astype(jnp.float32))
+    gc[0] = jnp.zeros((SIDE, D), jnp.float32)
+    vf[...] = tokens_of(v[...].astype(jnp.float32))
+    xf[...] = tokens_of(xt[...].astype(jnp.float32))
+    cols_o[0] = cols_o[0] + jnp.sum(gc[...], axis=0)
+
+    def relative(j, reach):
+        lanes = lane_tile(j)
+
+        def finish(token, total):
+            gv[token, :, lanes] = total
+
+        conv_tile(gc, taps, 9, 7, reach, lanes, finish, flip=True)
+        gv[0, :, lanes] = jnp.zeros((SIDE, 128), jnp.float32)
+        tap_sums(gc, vf, 9, 7, reach, lanes, taps_o)
+
+    relative_tiles(relative)
+
+    def attention(j):
+        lanes = lane_tile(j)
+        qs, ks, vs, gs = q[:, lanes], k[:, lanes], v[:, lanes], ga[:, lanes]
+        to_q, to_k, to_v = [], [], []
+        for h in (slice(0, 64), slice(64, 128)):
+            scores = dot_nt(qs[:, h], ks[:, h]).astype(low) * same[...]
+            grads = dot_nt(gs[:, h], vs[:, h]).astype(low) * same[...]
+            to_v.append(dot_tn(scores, gs[:, h]))
+            to_q.append(dot(grads, ks[:, h]))
+            to_k.append(dot_tn(grads, qs[:, h]))
+        gqs[:, :, lanes] = gqs[:, :, lanes] + tokens_of(jnp.concatenate(to_q, axis=1))
+        gv[:, :, lanes] = gv[:, :, lanes] + tokens_of(jnp.concatenate(to_v, axis=1))
+        gks[:, :, lanes] = tokens_of(jnp.concatenate(to_k, axis=1))
+
+    all_tiles(attention)
+
+    def finish_qkv(j):
+        lanes = lane_tile(j)
+        share = tokens_of(k[:, lanes].astype(jnp.float32))
+        up = gks[:, :, lanes]
+        along = jnp.sum(share * up, axis=0, keepdims=True) * 8.0
+        gq_o[:, pl.ds(pl.multiple_of(D + j * 128, 128), 128)] = (
+            (share * (up - along)).reshape(-1, 128).astype(low)
+        )
+        part = gqs[:, :, lanes].reshape(-1, 128).astype(low)
+        gq_o[:, lanes] = part
+        cols_o[1, :, lanes] = cols_o[1, :, lanes] + column_partial(part.astype(jnp.float32))
+        part = gv[:, :, lanes].reshape(-1, 128).astype(low)
+        gq_o[:, pl.ds(pl.multiple_of(2 * D + j * 128, 128), 128)] = part
+        cols_o[2, :, lanes] = cols_o[2, :, lanes] + column_partial(part.astype(jnp.float32))
+
+    all_tiles(finish_qkv)
+    gks[...] = tokens_of(dot_nt(gq_o[...], w_in[:, : 3 * D]))
+
+    def first_back(tokens, rows):
+        grad = gks[tokens].reshape(-1, D)
+        hats = hat[rows, :].astype(jnp.float32)
+        scale = sc[rows, 0:1]
+        total = gx[rows, :] + norm_back(grad, hats, scale, gains[0:1, :])
+        g1[tokens] = tokens_of(total)
+        cols_o[3] = cols_o[3] + column_partial(grad)
+        cols_o[4] = cols_o[4] + column_partial(grad * hats)
+        cols_o[5] = cols_o[5] + column_partial(total)
+
+    all_chunks(first_back)
+    cols_o[5] = cols_o[5] - g1[0]
+
+    def position(j):
+        lanes = lane_tile(j)
+
+        def finish(token, total):
+            gv[token, :, lanes] = g1[token, :, lanes] + total
+
+        conv_tile(g1, taps, 0, 3, 1, lanes, finish, flip=True)
+        gv[0, :, lanes] = g1[0, :, lanes]
+        tap_sums(g1, xf, 0, 3, 1, lanes, taps_o)
+
+    all_tiles(position)
+    value = rows_of(gv)
+    back = jnp.zeros((SIDE * SLOT, D), jnp.float32)
+    for _ in range(3):
+        piece = value.astype(low)
+        value = value - piece.astype(jnp.float32)
+        back = back + dot_tn(order[...], piece)
+    for i in range(SIDE):
+        out[i] = back[i * SLOT : i * SLOT + out.shape[1], :]
+
+
+def fixed(shape):
+    zeros = (0,) * len(shape)
+    return pl.BlockSpec(shape, lambda g: zeros, pipeline_mode=pl.Buffered(1))
+
+
+def compute(images, cotangent, counts, w_in, w_out, kern, gains, biases):
+    low, full = jnp.bfloat16, jnp.float32
+    num_images, num_tokens, channels = images.shape
+    groups = -(-num_images // SIDE)
+    rows = num_tokens * SIDE
+    total = groups * rows
+    taps = jnp.concatenate([kern[:9], kern[9:] * tap_mask(channels)], axis=0)
+    row_ids = lax.broadcasted_iota(jnp.int32, (rows, SIDE * SLOT), 0)
+    col_ids = lax.broadcasted_iota(jnp.int32, (rows, SIDE * SLOT), 1)
+    order = (row_ids == (col_ids % SLOT) * SIDE + col_ids // SLOT).astype(low)
+    row_ids = lax.broadcasted_iota(jnp.int32, (rows, rows), 0)
+    col_ids = lax.broadcasted_iota(jnp.int32, (rows, rows), 1)
+    same = (row_ids % SIDE == col_ids % SIDE).astype(low)
+
+    def block(cols):
+        return pl.BlockSpec((rows, cols), lambda g: (g, 0))
+
+    def image_block():
+        return pl.BlockSpec((SIDE, num_tokens, channels), lambda g: (g, 0, 0))
+
+    def made(cols, kind=low):
+        return jax.ShapeDtypeStruct((total, cols), kind)
+
+    def grid_scratch(cols=channels):
+        return pltpu.VMEM((num_tokens, SIDE, cols), full)
+
+    wide = w_out.shape[0]
+    forward = pl.pallas_call(
+        functools.partial(forward_kernel, num_images),
+        grid=(groups,),
+        in_specs=[
+            pl.BlockSpec(memory_space=pltpu.SMEM),
+            image_block(),
+            image_block(),
+            fixed(order.shape),
+            fixed(same.shape),
+            fixed(w_in.shape),
+            fixed(w_out.shape),
+            fixed(taps.shape),
+            fixed(gains.shape),
+            fixed(biases.shape),
+        ],
+        out_specs=[image_block(), block(wide), block(wide)]
+        + [block(channels)] * 8
+        + [block(128)]
+        + [block(channels)] * 4
+        + [fixed((4, SIDE, channels)), fixed((SIDE, wide))],
+        out_shape=[jax.ShapeDtypeStruct(images.shape, low), made(wide), made(wide)]
+        + [made(channels)] * 5
+        + [made(channels, full), made(channels), made(channels), made(128, full)]
+        + [made(channels)] * 4
+        + [
+            jax.ShapeDtypeStruct((4, SIDE, channels), full),
+            jax.ShapeDtypeStruct((SIDE, wide), full),
+        ],
+        scratch_shapes=[pltpu.VMEM((SIDE * SLOT, channels), low)]
+        + [grid_scratch() for _ in range(5)]
+        + [pltpu.VMEM((rows, wide), full), grid_scratch(), grid_scratch(128)],
+        compiler_params=pltpu.CompilerParams(vmem_limit_bytes=60 << 20),
+        name="forward",
+    )
+    (
+        out, act, gh, n1, n2, attended, gf, gp, gx, xt, hat, scale, q, k, v, cv, cols, hcols,
+    ) = forward(counts, images, cotangent, order, same, w_in, w_out, taps, gains, biases)
+
+    backward = pl.pallas_call(
+        functools.partial(backward_kernel, num_images),
+        grid=(groups,),
+        in_specs=[
+            fixed(order.shape),
+            fixed(same.shape),
+            fixed(w_in.shape),
+            fixed(taps.shape),
+            fixed(gains.shape),
+            block(channels),
+            block(channels),
+            block(128),
+        ]
+        + [block(channels)] * 5,
+        out_specs=[
+            image_block(),
+            block(3 * channels),
+            fixed((6, SIDE, channels)),
+            fixed((taps.shape[0], SIDE, channels)),
+        ],
+        out_shape=[
+            jax.ShapeDtypeStruct(images.shape, full),
+            made(3 * channels),
+            jax.ShapeDtypeStruct((6, SIDE, channels), full),
+            jax.ShapeDtypeStruct((taps.shape[0], SIDE, channels), full),
+        ],
+        scratch_shapes=[pltpu.VMEM((rows, channels), low)] + [grid_scratch() for _ in range(7)],
+        compiler_params=pltpu.CompilerParams(vmem_limit_bytes=60 << 20),
+        name="backward",
+    )
+    input_grad, gq, cols_back, grad_taps = backward(
+        order, same, w_in, taps, gains, gx, hat, scale, q, k, v, cv, xt
+    )
+    grad_in = jnp.concatenate(
+        [
+            cross_rows(n1, gq).astype(low),
+            cross_rows(attended, gp).astype(low),
+            cross_rows(n2, gh).astype(low),
+        ],
+        axis=1,
+    )
+    grad_out = cross_rows(act, gf).astype(low)
+    cols = jnp.sum(cols, axis=1)
+    hcols = jnp.sum(hcols, axis=0).reshape(-1, channels)
+    cols_back = jnp.sum(cols_back, axis=1)
+    grad_taps = jnp.sum(grad_taps, axis=1)
+    grad_kern = jnp.concatenate([grad_taps[:9], grad_taps[9:] * tap_mask(channels)], axis=0)
+    grad_gain = jnp.stack([cols_back[4], cols[1]])
+    grad_bias = jnp.concatenate(
+        [
+            cols_back[3:4],
+            cols[0:1],
+            cols_back[1:3],
+            cols[2:3],
+            hcols,
+            cols[3:4],
+            cols_back[5:6],
+            cols_back[0:1],
+        ],
+        axis=0,
+    )
+    return out, input_grad, grad_in, grad_out, grad_kern, grad_gain, grad_bias
 
 
 def adamw_update(master, first_moment, second_moment, gradient, clip_factor, rate, decay):
@@ -542,100 +987,17 @@
     kern_all = gathered[2].astype(jnp.float32)
     gain_all = gathered[3].astype(jnp.float32)
     bias_all = gathered[4].astype(jnp.float32)
-    inputs = images.astype(jnp.float32)
-    num_images, num_tokens, channels = inputs.shape
-    flat_rows = num_images * num_tokens
-    hidden_rows = MLP_WIDTH // D
-    live = (jnp.arange(num_images, dtype=jnp.int32) < counts[0]).astype(jnp.float32)
     scale_factor = 1.0 / live_total
-    (after_cpe, normed), pre_back = jax.vjp(
-        pre_block, inputs, kern_all[:9], bias_all[BROWS - 2], gain_all[0], bias_all[0]
-    )
-    normed_low = normed.astype(jnp.bfloat16).reshape(flat_rows, channels)
-    qkv_bias = jnp.concatenate([bias_all[2], jnp.zeros_like(bias_all[2]), bias_all[3]])
-    qkv_rows = (
-        jnp.dot(normed_low, wide_in[:, : 3 * channels], preferred_element_type=jnp.float32)
-        + qkv_bias
-    )
-    qkv_shaped = qkv_rows.reshape(num_images, num_tokens, 3 * channels)
-    attended, attend_back = jax.vjp(attend, qkv_shaped, kern_all[9:], bias_all[BROWS - 1])
-    attended_low = attended.astype(jnp.bfloat16).reshape(flat_rows, channels)
-    projected = (
-        jnp.dot(
-            attended_low,
-            wide_in[:, 3 * channels : 4 * channels],
-            preferred_element_type=jnp.float32,
-        )
-        + bias_all[4]
-    )
-    second = after_cpe.reshape(flat_rows, channels) + projected
-    normed_two, norm_back = jax.vjp(layer_norm, second, gain_all[1], bias_all[1])
-    normed_two_low = normed_two.astype(jnp.bfloat16)
-    fc_bias = bias_all[5 : 5 + hidden_rows].reshape(-1)
-    hidden_pre = (
-        jnp.dot(normed_two_low, wide_in[:, 4 * channels :], preferred_element_type=jnp.float32)
-        + fc_bias
-    )
-    activated, gelu_back = jax.vjp(gelu_exact, hidden_pre)
-    activated_low = activated.astype(jnp.bfloat16)
-    branch_out = (
-        jnp.dot(activated_low, wide_out, preferred_element_type=jnp.float32) + bias_all[BROWS - 3]
-    )
-    block_out = (second + branch_out).reshape(num_images, num_tokens, channels).astype(jnp.bfloat16)
-    back_in = wide_in
-    back_out = wide_out
-    out_grad = (cotangent.astype(jnp.float32) * live[:, None, None]).reshape(flat_rows, channels)
-    out_grad_low = out_grad.astype(jnp.bfloat16)
-    grad_fc2 = cross_rows(activated_low, out_grad_low)
-    grad_fc2_bias = column_sums(out_grad_low)
-    grad_act = transposed(out_grad_low, back_out)
-    grad_hidden = gelu_back(grad_act)[0].astype(jnp.bfloat16)
-    grad_fc1 = cross_rows(normed_two_low, grad_hidden)
-    grad_fc1_bias = column_sums(grad_hidden).reshape(hidden_rows, channels)
-    grad_normed_two = transposed(grad_hidden, back_in[:, 4 * channels :])
-    grad_second_norm, grad_gain_two, grad_shift_two = norm_back(grad_normed_two)
-    grad_second = out_grad + grad_second_norm
-    grad_second_low = grad_second.astype(jnp.bfloat16)
-    grad_proj = cross_rows(attended_low, grad_second_low)
-    grad_proj_bias = column_sums(grad_second_low)
-    grad_attended = transposed(grad_second_low, back_in[:, 3 * channels : 4 * channels])
-    grad_qkv, grad_crpe_taps, grad_crpe_shift = attend_back(
-        grad_attended.reshape(num_images, num_tokens, channels)
-    )
-    grad_qkv_low = grad_qkv.reshape(flat_rows, 3 * channels).astype(jnp.bfloat16)
-    grad_qkv_mat = cross_rows(normed_low, grad_qkv_low)
-    qkv_sums = column_sums(grad_qkv_low)
-    grad_normed = transposed(grad_qkv_low, back_in[:, : 3 * channels])
-    input_grad, grad_cpe_taps, grad_cpe_shift, grad_gain_one, grad_shift_one = pre_back(
-        (
-            grad_second.reshape(num_images, num_tokens, channels),
-            grad_normed.reshape(num_images, num_tokens, channels),
-        )
-    )
-    grad_kern = jnp.concatenate([grad_cpe_taps, grad_crpe_taps], axis=0)
-    grad_gain = jnp.stack([grad_gain_one, grad_gain_two])
-    grad_bias = jnp.concatenate(
-        [
-            grad_shift_one[None],
-            grad_shift_two[None],
-            qkv_sums[None, :channels],
-            qkv_sums[None, 2 * channels :],
-            grad_proj_bias[None],
-            grad_fc1_bias,
-            grad_fc2_bias[None],
-            grad_cpe_shift[None],
-            grad_crpe_shift[None],
-        ],
-        axis=0,
-    )
-    grad_in = jnp.concatenate([grad_qkv_mat, grad_proj, grad_fc1], axis=1)
+    block_out, input_grad, grad_in, grad_fc2, grad_kern, grad_gain, grad_bias = compute(
+        images, cotangent, counts, wide_in, wide_out, kern_all, gain_all, bias_all
+    )
     parts = (grad_kern, grad_gain, grad_bias)
     if special:
         rows = jnp.concatenate(parts, axis=0)
         small = rows.reshape(sum(sizes), 32, -1).transpose(1, 0, 2).reshape(32, per)
         small = jnp.pad(small, ((0, 0), (0, SMALL_ROWS * 128 - per)))
         sum_in, sum_out, sum_small, squares = reduce_all(
-            grad_in.astype(jnp.bfloat16), grad_fc2.astype(jnp.bfloat16), small
+            grad_in, grad_fc2, small
         )
         rows = sum_small.reshape(-1)[:per].reshape(sum(sizes), -1)
         summed = (
@@ -648,7 +1010,7 @@
         total_squares = jnp.sum(squares)
     else:
         summed = tuple(
-            lax.psum_scatter(part, ("wide", "narrow"), scatter_dimension=dim, tiled=True)
+            lax.psum_scatter(part.astype(jnp.float32), ("wide", "narrow"), scatter_dimension=dim, tiled=True)
             for part, dim in zip((grad_in, grad_fc2) + parts, (0, 0, 1, 1, 1))
         )
         total_squares = lax.psum(

time: 1050 us -> 357 us (0.34)
  other arithmetic: 425 us -> 23.4 us
  local copies, waits for them, and re-layouts: 259 us -> 21.7 us
  matrix products: 236 us -> 28.9 us
  Pallas kernels: 114 us -> 278 us
    dot_general x14 -> x0, matrix products: 216 us -> none  [the longest x3 62.8 us: attend(): jnp.einsum('bnhd,bnhe->bhde', weights.reshape(shape_heads), values.reshap...]
    pallas_call x0 -> x2, Pallas kernels: none -> 164 us  [the longest x1 89.3 us: compute(): forward(counts, images, cotangent, order, same, w_in, w_out, taps, gains,...]
    reduce_sum x16 -> x4, other arithmetic: 133 us -> 3.18 us  [the longest x1 1.43 us: compute(): grad_taps = jnp.sum(grad_taps, axis=1)]
    reshape x20 -> x0, local copies, waits for them, and re-layouts: 121 us -> none  [the longest x2 20.3 us: attend(): conv_values.reshape(num_images, GRID * GRID, channels)]
    add_any x8 -> x0, other arithmetic: 97.5 us -> none  [the longest x3 80.3 us: depthwise(): window = padded[:, row_tap:row_tap + GRID, col_tap:col_tap + GRID, :]]
    mul x8 -> x2, other arithmetic: 85.7 us -> 1.48 us  [the longest x1 1.4 us: compute(): grad_taps[9:] * tap_mask(channels)]
    add x2 -> x1, other arithmetic: 77.5 us -> 0.01 us  [compute(): order = (row_ids == col_ids % SLOT * SIDE + col_ids // SLOT).astype(low)]
    broadcast_in_dim x50 -> x0, local copies, waits for them, and re-layouts: 38.5 us -> none  [the longest x49 38.5 us: depthwise(): summed_taps = summed_taps + window * taps[row_tap * kernel_width + col_tap]]
where the time goes in v2:
time: 357 us; the launch traced here: 356 us
  Pallas kernels  278 us (78%)
  matrix products  28.9 us (8%)
  other arithmetic  23.4 us (7%)
  local copies, waits for them, and re-layouts  21.7 us (6%)
  between operations  4.24 us (1%)
    pallas_call x1, Pallas kernels, compute(): forward(counts, images, cotangent, order, same, w_in, w_out, taps, gains,...  89.3 us
    pallas_call x1, Pallas kernels, compute(): backward(order, same, w_in, taps, gains, gx, hat, scale, q, k, v, cv, xt)  74.2 us
    pallas_call x1, Pallas kernels, reduce_all(): pl.pallas_call(reduce_kernel, out_shape=(jax.ShapeDtypeStruct((rows_in, w...  73.9 us
    pallas_call x1, Pallas kernels, gather_all(): pl.pallas_call(gather_kernel, out_shape=(jax.ShapeDtypeStruct((32,) + in_...  40.4 us
    dot_general x4, matrix products, cross_rows(): lax.dot_general(left, right, (((0,), (0,)), ((), ())), preferred_element_...  28.9 us
    concatenate x13, local copies, waits for them, and re-layouts, local(): rows = jnp.concatenate(parts, axis=0)  12.9 us

profile of v2, /device:TPU:0, one launch (start us, length us, event | category | flops | bytes accessed | tf_op | source)
XLA Modules:
  0.0 356.0 jit_solution(3981672474872355540)
XLA Ops:
  1.3 0.7 convert_element_type.84
  2.2 0.7 convert_element_type.83
  2.9 0.7 convert_element_type.85
  4.0 0.6 fusion.11.sm
  4.6 1.5 convert_element_type.82.wo
  6.1 1.6 convert_element_type.81.wi
  7.7 0.9 fusion.order
  8.6 1.0 fusion.1.same
  9.6 40.4 %gather_all.1 = (bf16[32,16,4096]{2,1,0:T(8,128)(2,1)}, bf16[32,64,512]{2,1,0:T(8,128)(2,1)}, bf16[32,16,128]{2,1,0:T(8,128)(2,1)}) custom-call(bf16[16,4096]{1,0:T(8,128)(2,1)} %convert_element_type.81.wi, bf16[64,512]{1,0:T(8,128)(2,1)} %convert_element_type.82.wo, bf16[16,128]{1,0:T(8,128)(2,1)} %fusion.11.sm), custom_call_target="tpu_custom_call" | custom-call | tf_op jit(solution)/shard_map/gather_all/pallas_call | solution.py:156
  50.0 0.9 copy.118
  50.9 0.6 convert_reduce_fusion
  52.2 0.2 copy.112
  52.5 0.7 reshape.151.gains
  53.4 0.8 reshape.152.biases
  54.2 0.3 copy.90
  54.9 0.7 pad_maximum_fusion.1.taps
  55.6 89.3 %forward.1 = (bf16[34,50,512]{2,1,0:T(8,128)(2,1)}, bf16[2000,2048]{1,0:T(8,128)(2,1)}, bf16[2000,2048]{1,0:T(8,128)(2,1)}, bf16[2000,512]{1,0:T(8,128)(2,1)}, b...) custom-call(s32[1]{0:T(128)S(6)} %copy.119.counts, ...), custom_call_target="tpu_custom_call" | custom-call | tf_op jit(solution)/shard_map/forward/pallas_call | solution.py:852
  144.9 0.9 reduce_sum.56
  145.8 0.9 reduce_sum.57
  146.8 0.3 copy.103
  147.5 0.9 concatenate.60
  148.4 0.9 concatenate.58
  149.3 3.5 convolution_convert_fusion.3
  153.1 10.1 %convolution_convert_fusion.1 = bf16[512,2048]{1,0:T(8,128)(2,1)} fusion(bf16[2000,512]{1,0:T(8,128)(2,1)} %get-tuple-element.69, bf16[2000,2048]{1,0:T(8,128)(2,1)} %get-tuple-element.70), kind=kOutput, calls=%fused_computation.2 | convolution fusion | flops 4195352576 | bytes 12337152 | tf_op jit(solution)/shard_map/dot_general | solution.py:401
  163.1 8.4 %convolution_convert_fusion = bf16[2048,512]{1,0:T(8,128)(2,1)S(1)} fusion(bf16[2000,2048]{1,0:T(8,128)(2,1)} %get-tuple-element.71, bf16[2000,512]{1,0:T(8,128)(2,1)S(1)} %copy-done.12), kind=kOutput, calls=%fused_computation.1 | convolution fusion | flops 4195352576 | bytes 12337152 | tf_op jit(solution)/shard_map/dot_general | solution.py:401
  171.5 74.2 %backward.1 = (f32[34,50,512]{2,1,0:T(8,128)}, bf16[2000,1536]{1,0:T(8,128)(2,1)}, f32[6,8,512]{2,1,0:T(8,128)}, f32[58,8,512]{2,1,0:T(8,128)}) custom-call(bf16[400,512]{1,0:T(8,128)(2,1)} %fusion.order, bf16[400,400]{1,0:T(8,128)(2,1)} %fusion.1.same, bf16[512,4096]{1,0:T(8,128)(2,1)} %bitcast.37, f32[58,512]{1,0:T(8,128)} %pad_maximum_fusion.1.taps, ...), custom_call_target="tpu_custom_call" | custom-call | tf_op jit(solution)/shard_map/backward/pallas_call | solution.py:884
  245.7 7.0 %convolution_convert_fusion.2 = bf16[512,1536]{1,0:T(8,128)(2,1)S(1)} fusion(bf16[2000,512]{1,0:T(8,128)(2,1)} %get-tuple-element.65, bf16[2000,1536]{1,0:T(8,128)(2,1)} %get-tuple-element.66), kind=kOutput, calls=%fused_computation.3 | convolution fusion | flops 3146514432 | bytes 9764864 | tf_op jit(solution)/shard_map/dot_general | solution.py:401
  252.7 2.2 pad_maximum_fusion
  254.9 0.6 slice_reduce_fusion
  255.5 1.4 reduce_sum.54
  257.0 0.6 slice.106
  257.6 1.4 slice_select_fusion
  259.0 1.7 copy.95
  260.7 1.6 copy.110
  262.3 0.9 copy.111
  263.2 1.6 concatenate.64
  264.8 1.6 concatenate.63
  266.4 0.9 concatenate.59
  267.3 0.9 concatenate.57
  268.2 2.8 concatenate.56
  271.0 1.3 copy.107
  272.7 73.9 %reduce_all.1 = (f32[16,4096]{1,0:T(8,128)S(1)}, f32[64,512]{1,0:T(8,128)S(1)}, f32[16,128]{1,0:T(8,128)S(1)}, f32[8,128]{1,0:T(8,128)S(1)}) custom-call(bf16[4,2,2,2,16,4096]{5,4,3,2,1,0:T(8,128)(2,1)} %bitcast.35, bf16[4,2,2,2,64,512]{5,4,3,2,1,0:T(8,128)(2,1)S(1)} %bitcast.32, f32[4,2,2,2,16,128]{5,4,3,2,1,0:T(8,128)S(1)} %bitcast.33), custom_call_target="tpu_custom_call" | custom-call | tf_op jit(solution)/shard_map/reduce_all/pallas_call | solution.py:367
  346.5 0.6 reduce_sum.58
  348.0 1.3 fusion.30
  349.2 1.4 fusion.28
  350.7 1.4 fusion.32
  352.1 1.7 fusion.34
  353.8 1.1 fusion.36
  (63 shorter events, 2.5 us)
Async XLA Ops:
  2.0 52.6 %copy-start.9 = (s32[49]{0:T(128)}, s32[49]{0:T(128)S(1)}, u32[]{:S(2)}) copy-start(s32[49]{0:T(128)S(1)} %get-tuple-element.163) | copy-start | bytes 592
  2.0 52.6 %copy-start.10 = (s32[49]{0:T(128)}, s32[49]{0:T(128)S(1)}, u32[]{:S(2)}) copy-start(s32[49]{0:T(128)S(1)} %get-tuple-element.164) | copy-start | bytes 592
  153.0 10.1 %copy-start.12 = (bf16[2000,512]{1,0:T(8,128)(2,1)S(1)}, bf16[2000,512]{1,0:T(8,128)(2,1)}, u32[]{:S(2)}) copy-start(bf16[2000,512]{1,0:T(8,128)(2,1)} %get-tuple-element.72) | copy-start | bytes 6144004
  245.7 7.0 %copy-start = (bf16[512,2048]{1,0:T(8,128)(2,1)S(1)}, bf16[512,2048]{1,0:T(8,128)(2,1)}, u32[]{:S(2)}) copy-start(bf16[512,2048]{1,0:T(8,128)(2,1)} %convolution_convert_fusion.1) | copy-start | bytes 6291460
  252.7 2.2 copy-start.8
  254.9 13.3 %copy-start.2 = (f32[1,32,16]{0,2,1:T(8,128)S(1)}, f32[1,32,16]{0,2,1:T(8,128)}, u32[]{:S(2)}) copy-start(f32[1,32,16]{0,2,1:T(8,128)} %concatenate.60) | copy-start | bytes 6148
  254.9 13.3 %copy-start.3 = (f32[1,32,16]{0,2,1:T(8,128)S(1)}, f32[1,32,16]{0,2,1:T(8,128)}, u32[]{:S(2)}) copy-start(f32[1,32,16]{0,2,1:T(8,128)} %concatenate.58) | copy-start | bytes 6148
  272.6 75.4 %copy-start.11 = (f32[2,16]{1,0:T(2,128)S(1)}, f32[2,16]{1,0:T(2,128)}, u32[]{:S(2)}) copy-start(f32[2,16]{1,0:T(2,128)} %param.30) | copy-start | bytes 388
  272.6 79.5 %copy-start.4 = (f32[64,512]{1,0:T(8,128)S(1)}, f32[64,512]{1,0:T(8,128)}, u32[]{:S(2)}) copy-start(f32[64,512]{1,0:T(8,128)} %param.24) | copy-start | bytes 393220
  272.6 79.4 %copy-start.7 = (f32[64,512]{1,0:T(8,128)S(1)}, f32[64,512]{1,0:T(8,128)}, u32[]{:S(2)}) copy-start(f32[64,512]{1,0:T(8,128)} %param.25) | copy-start | bytes 393220
  272.6 81.2 %copy-start.1 = (f32[16,4096]{1,0:T(8,128)S(1)}, f32[16,4096]{1,0:T(8,128)}, u32[]{:S(2)}) copy-start(f32[16,4096]{1,0:T(8,128)} %param.21) | copy-start | bytes 786436
  272.6 81.2 %copy-start.5 = (f32[16,4096]{1,0:T(8,128)S(1)}, f32[16,4096]{1,0:T(8,128)}, u32[]{:S(2)}) copy-start(f32[16,4096]{1,0:T(8,128)} %param.22) | copy-start | bytes 786436
  272.6 81.2 %copy-start.6 = (f32[16,4096]{1,0:T(8,128)S(1)}, f32[16,4096]{1,0:T(8,128)}, u32[]{:S(2)}) copy-start(f32[16,4096]{1,0:T(8,128)} %param.23) | copy-start | bytes 786436

commit v3 on v2

--- a/solution.py
+++ b/solution.py
@@ -382,21 +382,6 @@
     )(gi, go, gs)
 
 
-def tap_mask(channels):
-    head_width = channels // HEADS
-    channel_ids = jnp.arange(channels, dtype=jnp.int32)
-    reach_cells = jnp.where(
-        channel_ids < 2 * head_width, 1, jnp.where(channel_ids < 5 * head_width, 2, 3)
-    )
-    tap_ids = jnp.arange(49, dtype=jnp.int32)
-    row_offset = jnp.abs(tap_ids // 7 - 3)
-    col_offset = jnp.abs(tap_ids % 7 - 3)
-    inside = (row_offset[:, None] <= reach_cells[None, :]) & (
-        col_offset[:, None] <= reach_cells[None, :]
-    )
-    return inside.astype(jnp.float32)
-
-
 def cross_rows(left, right):
     return lax.dot_general(
         left, right, (((0,), (0,)), ((), ())), preferred_element_type=jnp.float32
@@ -404,12 +389,10 @@
 
 
 SIDE = 8
-SLOT = 64
+TALL = 512
 CHUNK = 10
-
-
-def rows_of(ref):
-    return ref[...].reshape(-1, ref.shape[-1])
+GAIN_ROW = 58
+BIAS_ROW = 60
 
 
 def tokens_of(value):
@@ -442,11 +425,24 @@
     return pl.ds(pl.multiple_of(j * 128, 128), 128)
 
 
-def grid_token(row, col):
-    return 1 + row * GRID + col
-
-
-def conv_tile(src, taps, base, width, reach, lanes, finish, flip=False):
+def grid_rows(row, col):
+    return pl.ds((1 + row * GRID + col) * SIDE, SIDE)
+
+
+CLASS_ROWS = pl.ds(0, SIDE)
+
+
+def put(grid, at, value):
+    for j in range(D // 128):
+        grid[j, at, :] = value[:, j * 128 : j * 128 + 128]
+
+
+def get(grid, at, tiles=(0, 1, 2, 3)):
+    return jnp.concatenate([grid[j, at, :] for j in tiles], axis=1)
+
+
+def conv_tile(src, taps, base, width, reach, j, finish, flip=False):
+    lanes = lane_tile(j)
     margin = width // 2
     offsets = range(-reach, reach + 1)
 
@@ -462,16 +458,17 @@
         for dy in offsets:
             if not 0 <= row + dy < GRID:
                 continue
-            line = [src[grid_token(row + dy, col), :, lanes] for col in range(GRID)]
+            line = [src[j, grid_rows(row + dy, col), :] for col in range(GRID)]
             for dx in offsets:
                 for col in range(GRID):
                     if 0 <= col + dx < GRID:
                         sums[col] = sums[col] + line[col + dx] * held[dy, dx]
         for col in range(GRID):
-            finish(grid_token(row, col), sums[col])
-
-
-def tap_sums(grad, src, base, width, reach, lanes, total):
+            finish(grid_rows(row, col), sums[col])
+
+
+def tap_sums(grad, src, base, width, reach, j, total):
+    lanes = lane_tile(j)
     margin = width // 2
     offsets = range(-reach, reach + 1)
     for dy in offsets:
@@ -479,8 +476,8 @@
         for row in range(GRID):
             if not 0 <= row + dy < GRID:
                 continue
-            up = [grad[grid_token(row, col), :, lanes] for col in range(GRID)]
-            line = [src[grid_token(row + dy, col), :, lanes] for col in range(GRID)]
+            up = [grad[j, grid_rows(row, col), :] for col in range(GRID)]
+            line = [src[j, grid_rows(row + dy, col), :] for col in range(GRID)]
             for dx in offsets:
                 for col in range(GRID):
                     if 0 <= col + dx < GRID:
@@ -490,7 +487,13 @@
             total[index, :, lanes] = total[index, :, lanes] + sums[dx]
 
 
-REACHES = ((0, 1), (1, 2))
+def mask_far_taps(rows):
+    lanes = pl.ds(256, 128)
+    keep = (lax.broadcasted_iota(jnp.int32, (1, 128), 1) >= 64).astype(jnp.float32)
+    for tap in range(49):
+        if max(abs(tap // 7 - 3), abs(tap % 7 - 3)) == 3:
+            line = pl.ds(9 + tap, 1)
+            rows[line, lanes] = rows[line, lanes] * keep
 
 
 def relative_tiles(body):
@@ -514,7 +517,7 @@
 
 def all_chunks(body):
     def step(k, carry):
-        body(pl.ds(k * CHUNK, CHUNK), pl.ds(pl.multiple_of(k * CHUNK * SIDE, 16), CHUNK * SIDE))
+        body(pl.ds(pl.multiple_of(k * CHUNK * SIDE, 16), CHUNK * SIDE))
         return carry
 
     lax.fori_loop(0, 50 // CHUNK, step, 0)
@@ -533,126 +536,145 @@
     return scale * (inner - mean - hat * along)
 
 
-def take_images(src, slots, first, limit):
+def spread_images(src, grid, first, limit):
     for i in range(SIDE):
         image = src[i]
         keep = jnp.full(image.shape, first + i, jnp.int32) < limit
-        image = jnp.where(keep, image.astype(jnp.float32), 0.0).astype(jnp.bfloat16)
-        slots[i * SLOT : i * SLOT + image.shape[0], :] = image
+        at = pl.ds(i, image.shape[0], stride=SIDE)
+        put(grid, at, jnp.where(keep, image.astype(jnp.float32), 0.0))
+
+
+def set_parameters(small, par, heads):
+    par[...] = small[...].astype(jnp.float32).T
+    mask_far_taps(par)
+    row_head = lax.broadcasted_iota(jnp.int32, heads.shape, 0) // 64
+    col_head = lax.broadcasted_iota(jnp.int32, heads.shape, 1) // 64
+    heads[...] = jnp.where(row_head == col_head, 1.0, 0.0).astype(heads.dtype)
+
+
+def every_image(body):
+    for i in range(SIDE):
+        for half in range(2):
+            body(pl.ds(i, TALL // SIDE, stride=SIDE), (2 * half, 2 * half + 1))
 
 
 def forward_kernel(
-    num_images, counts, x_in, dy_in, order, same, w_in, w_out, taps, gains, biases,
+    num_images, rows, counts, x_in, dy_in, w_in, w_out, small,
     out, act_o, gh_o, n1_o, n2_o, at_o, gf_o, gp_o, gx_o, xt_o, hat_o, sc_o, q_o, k_o, v_o, cv_o,
     cols_o, hcols_o,
-    slots, x, x1, v, conv, hat2, slope, gn, scale2,
+    par, heads, x, x1, v, q, k, conv, hat2, slope, gn, scale2,
 ):
     low = jnp.bfloat16
     step = pl.program_id(0)
     first = step * SIDE
+    live = pl.ds(0, rows)
 
     @pl.when(step == 0)
     def _():
-        slots[...] = jnp.zeros_like(slots)
+        set_parameters(small, par, heads)
+        for grid in (q, k, v):
+            grid[...] = jnp.zeros_like(grid)
         cols_o[...] = jnp.zeros_like(cols_o)
         hcols_o[...] = jnp.zeros_like(hcols_o)
 
-    take_images(x_in, slots, first, num_images)
-    value = dot(order[...], slots[...])
-    x[...] = tokens_of(value)
-    xt_o[...] = value.astype(low)
-    take_images(dy_in, slots, first, jnp.minimum(counts[0], num_images))
-    gf_o[...] = dot(order[...], slots[...]).astype(low)
+    def bias(row):
+        return par[BIAS_ROW + row : BIAS_ROW + row + 1, :]
+
+    def gain(row):
+        return par[GAIN_ROW + row : GAIN_ROW + row + 1, :]
+
+    spread_images(x_in, x, first, num_images)
+    xt_o[...] = get(x, live).astype(low)
+    spread_images(dy_in, gn, first, jnp.minimum(counts[0], num_images))
+    gf_o[...] = get(gn, live).astype(low)
 
     def position(j):
         lanes = lane_tile(j)
-        shift = jnp.broadcast_to(biases[10:11, lanes], (SIDE, 128))
-
-        def finish(token, total):
-            x1[token, :, lanes] = x[token, :, lanes] + total + shift
-
-        conv_tile(x, taps, 0, 3, 1, lanes, finish)
-        x1[0, :, lanes] = x[0, :, lanes]
+        shift = jnp.broadcast_to(par[BIAS_ROW + 10 : BIAS_ROW + 11, lanes], (SIDE, 128))
+
+        def finish(at, total):
+            x1[j, at, :] = x[j, at, :] + total + shift
+
+        conv_tile(x, par, 0, 3, 1, j, finish)
+        x1[j, CLASS_ROWS, :] = x[j, CLASS_ROWS, :]
 
     all_tiles(position)
 
-    def first_norm(tokens, rows):
-        hat, scale = normalise(x1[tokens].reshape(-1, D))
-        hat_o[rows, :] = hat.astype(low)
-        sc_o[rows, :] = jnp.broadcast_to(scale, (CHUNK * SIDE, 128))
-        n1_o[rows, :] = (hat * gains[0:1, :] + biases[0:1, :]).astype(low)
+    def first_norm(at):
+        hat, scale = normalise(get(x1, at))
+        hat_o[at, :] = hat.astype(low)
+        sc_o[at, :] = jnp.broadcast_to(scale, (CHUNK * SIDE, 128))
+        n1_o[at, :] = (hat * gain(0) + bias(0)).astype(low)
 
     all_chunks(first_norm)
     n1 = n1_o[...]
-    gn[...] = tokens_of(dot(n1, w_in[:, D : 2 * D]))
+    put(gn, live, dot(n1, w_in[:, D : 2 * D]))
 
     def weights(j):
         lanes = lane_tile(j)
-        keys = gn[:, :, lanes]
+        keys = tokens_of(gn[j, live, :])
         powers = jnp.exp(keys - jnp.max(keys, axis=0, keepdims=True))
         share = 0.125 / jnp.sum(powers, axis=0, keepdims=True)
-        k_o[:, lanes] = (powers * share).reshape(-1, 128).astype(low)
+        value = (powers * share).reshape(-1, 128)
+        k[j, live, :] = value
+        k_o[:, lanes] = value.astype(low)
 
     all_tiles(weights)
-    value = dot(n1, w_in[:, 2 * D : 3 * D]) + biases[3:4, :]
-    v[...] = tokens_of(value)
+    value = dot(n1, w_in[:, 2 * D : 3 * D]) + bias(3)
+    put(v, live, value)
     v_o[...] = value.astype(low)
 
     def relative(j, reach):
         lanes = lane_tile(j)
-        shift = jnp.broadcast_to(biases[11:12, lanes], (SIDE, 128))
-
-        def finish(token, total):
-            conv[token, :, lanes] = total + shift
-
-        conv_tile(v, taps, 9, 7, reach, lanes, finish)
-        conv[0, :, lanes] = jnp.zeros((SIDE, 128), jnp.float32)
+        shift = jnp.broadcast_to(par[BIAS_ROW + 11 : BIAS_ROW + 12, lanes], (SIDE, 128))
+
+        def finish(at, total):
+            conv[j, at, :] = total + shift
+
+        conv_tile(v, par, 9, 7, reach, j, finish)
+        conv[j, CLASS_ROWS, :] = jnp.zeros((SIDE, 128), jnp.float32)
 
     relative_tiles(relative)
-    cv_o[...] = rows_of(conv).astype(low)
-    value = dot(n1, w_in[:, :D]) + biases[2:3, :]
+    cv_o[...] = get(conv, live).astype(low)
+    value = dot(n1, w_in[:, :D]) + bias(2)
     q_o[...] = value.astype(low)
-    conv[...] = conv[...] * tokens_of(value)
-
-    def attention(j):
-        lanes = lane_tile(j)
-        qs, ks, vs = q_o[:, lanes], k_o[:, lanes], v_o[:, lanes]
-        parts = []
-        for h in (slice(0, 64), slice(64, 128)):
-            scores = dot_nt(qs[:, h], ks[:, h]).astype(low) * same[...]
-            parts.append(dot(scores, vs[:, h]))
-        value = jnp.concatenate(parts, axis=1) + conv[:, :, lanes].reshape(-1, 128)
-        at_o[:, lanes] = value.astype(low)
-
-    all_tiles(attention)
-    x1[...] = x1[...] + tokens_of(dot(at_o[...], w_in[:, 3 * D : 4 * D]) + biases[4:5, :])
-
-    def second_norm(tokens, rows):
-        hat, scale = normalise(x1[tokens].reshape(-1, D))
-        hat2[tokens] = tokens_of(hat)
-        scale2[tokens] = jnp.broadcast_to(tokens_of(scale), (CHUNK, SIDE, 128))
-        n2_o[rows, :] = (hat * gains[1:2, :] + biases[1:2, :]).astype(low)
+    put(q, live, value)
+
+    def attention(at, tiles):
+        context = dot_tn(get(k, at, tiles).astype(low), get(v, at, tiles).astype(low))
+        context = context.astype(low) * heads[...]
+        value = dot(get(q, at, tiles).astype(low), context)
+        for n, j in enumerate(tiles):
+            gn[j, at, :] = value[:, n * 128 : n * 128 + 128]
+
+    every_image(attention)
+    for j in range(D // 128):
+        at_o[:, lane_tile(j)] = (gn[j, live, :] + conv[j, live, :] * q[j, live, :]).astype(low)
+    put(x1, live, get(x1, live) + (dot(at_o[...], w_in[:, 3 * D : 4 * D]) + bias(4)))
+
+    def second_norm(at):
+        hat, scale = normalise(get(x1, at))
+        hat2[at, :] = hat
+        scale2[at, :] = jnp.broadcast_to(scale, (CHUNK * SIDE, 128))
+        n2_o[at, :] = (hat * gain(1) + bias(1)).astype(low)
 
     all_chunks(second_norm)
     n2 = n2_o[...]
     for part in range(MLP_WIDTH // D):
         cols = pl.ds(part * D, D)
-        gn[...] = tokens_of(dot(n2, w_in[:, pl.ds((4 + part) * D, D)]))
-
-        def gelu(tokens, rows):
-            h = gn[tokens].reshape(-1, D) + biases[5 + part : 6 + part, :]
+        put(gn, live, dot(n2, w_in[:, pl.ds((4 + part) * D, D)]))
+
+        def gelu(at):
+            h = get(gn, at) + bias(5 + part)
             below = 0.5 + 0.5 * lax.erf(h * (0.5**0.5))
             density = jnp.exp(-0.5 * h * h) * 0.3989422804014327
-            act_o[rows, cols] = (h * below).astype(low)
-            slope[rows, cols] = below + h * density
+            act_o[at, cols] = (h * below).astype(low)
+            slope[at, cols] = below + h * density
 
         all_chunks(gelu)
-    value = rows_of(x1) + dot(act_o[...], w_out[...]) + biases[9:10, :]
-    back = lax.dot_general(
-        order[...], value.astype(low), (((0,), (0,)), ((), ())), preferred_element_type=jnp.float32
-    )
+    put(x1, live, get(x1, live) + dot(act_o[...], w_out[...]) + bias(9))
     for i in range(SIDE):
-        out[i] = back[i * SLOT : i * SLOT + out.shape[1], :].astype(low)
+        out[i] = get(x1, pl.ds(i, out.shape[1], stride=SIDE)).astype(low)
 
     gf = gf_o[...]
     for part in range(MLP_WIDTH // D):
@@ -660,17 +682,17 @@
         grad = (dot_nt(gf, w_out[cols, :]) * slope[:, cols]).astype(low)
         gh_o[:, cols] = grad
         hcols_o[:, cols] = hcols_o[:, cols] + column_partial(grad.astype(jnp.float32))
-    gn[...] = tokens_of(dot_nt(gh_o[...], w_in[:, 4 * D :]))
-
-    def second_back(tokens, rows):
-        grad = gn[tokens].reshape(-1, D)
-        hat = hat2[tokens].reshape(-1, D)
-        scale = scale2[tokens].reshape(-1, 128)[:, 0:1]
-        upstream = gf_o[rows, :].astype(jnp.float32)
-        total = upstream + norm_back(grad, hat, scale, gains[1:2, :])
-        gx_o[rows, :] = total
+    put(gn, live, dot_nt(gh_o[...], w_in[:, 4 * D :]))
+
+    def second_back(at):
+        grad = get(gn, at)
+        hat = hat2[at, :]
+        scale = scale2[at, 0:1]
+        upstream = gf_o[at, :].astype(jnp.float32)
+        total = upstream + norm_back(grad, hat, scale, gain(1))
+        gx_o[at, :] = total
         rounded = total.astype(low)
-        gp_o[rows, :] = rounded
+        gp_o[at, :] = rounded
         cols_o[0] = cols_o[0] + column_partial(grad)
         cols_o[1] = cols_o[1] + column_partial(grad * hat)
         cols_o[2] = cols_o[2] + column_partial(rounded.astype(jnp.float32))
@@ -680,105 +702,114 @@
 
 
 def backward_kernel(
-    num_images, order, same, w_in, taps, gains, gx, hat, sc, q, k, v, cv, xt,
-    out, gq_o, cols_o, taps_o,
-    ga, gc, vf, gv, gqs, gks, xf, g1,
+    rows, w_in, small, cols_in, hcols_in, gx, hat, sc, q_in, k_in, v_in, cv, xt,
+    out, gq_o, small_o,
+    par, heads, cols, taps, lines, g, gc, q, k, v, gq, gk, gv, x, g1,
 ):
     low = jnp.bfloat16
     step = pl.program_id(0)
+    live = pl.ds(0, rows)
 
     @pl.when(step == 0)
     def _():
-        cols_o[...] = jnp.zeros_like(cols_o)
-        taps_o[...] = jnp.zeros_like(taps_o)
+        set_parameters(small, par, heads)
+        for grid in (g, q, k, v, gq, gk, gv):
+            grid[...] = jnp.zeros_like(grid)
+        cols[...] = jnp.zeros_like(cols)
+        taps[...] = jnp.zeros_like(taps)
 
     grad = dot_nt(gx[...].astype(low), w_in[:, 3 * D : 4 * D])
-    ga[...] = grad.astype(low)
-    gqs[...] = tokens_of(grad * cv[...].astype(jnp.float32))
-    gc[...] = tokens_of(grad * q[...].astype(jnp.float32))
-    gc[0] = jnp.zeros((SIDE, D), jnp.float32)
-    vf[...] = tokens_of(v[...].astype(jnp.float32))
-    xf[...] = tokens_of(xt[...].astype(jnp.float32))
-    cols_o[0] = cols_o[0] + jnp.sum(gc[...], axis=0)
+    put(g, live, grad)
+    for j in range(D // 128):
+        lanes = lane_tile(j)
+        part = g[j, live, :]
+        queries = q_in[:, lanes].astype(jnp.float32)
+        q[j, live, :] = queries
+        k[j, live, :] = k_in[:, lanes].astype(jnp.float32)
+        v[j, live, :] = v_in[:, lanes].astype(jnp.float32)
+        x[j, live, :] = xt[:, lanes].astype(jnp.float32)
+        gq[j, live, :] = part * cv[:, lanes].astype(jnp.float32)
+        gc[j, live, :] = part * queries
+        gc[j, CLASS_ROWS, :] = jnp.zeros((SIDE, 128), jnp.float32)
+        cols[0, :, lanes] = cols[0, :, lanes] + column_partial(gc[j, live, :])
 
     def relative(j, reach):
-        lanes = lane_tile(j)
-
-        def finish(token, total):
-            gv[token, :, lanes] = total
-
-        conv_tile(gc, taps, 9, 7, reach, lanes, finish, flip=True)
-        gv[0, :, lanes] = jnp.zeros((SIDE, 128), jnp.float32)
-        tap_sums(gc, vf, 9, 7, reach, lanes, taps_o)
+        def finish(at, total):
+            gv[j, at, :] = total
+
+        conv_tile(gc, par, 9, 7, reach, j, finish, flip=True)
+        gv[j, CLASS_ROWS, :] = jnp.zeros((SIDE, 128), jnp.float32)
+        tap_sums(gc, v, 9, 7, reach, j, taps)
 
     relative_tiles(relative)
 
-    def attention(j):
-        lanes = lane_tile(j)
-        qs, ks, vs, gs = q[:, lanes], k[:, lanes], v[:, lanes], ga[:, lanes]
-        to_q, to_k, to_v = [], [], []
-        for h in (slice(0, 64), slice(64, 128)):
-            scores = dot_nt(qs[:, h], ks[:, h]).astype(low) * same[...]
-            grads = dot_nt(gs[:, h], vs[:, h]).astype(low) * same[...]
-            to_v.append(dot_tn(scores, gs[:, h]))
-            to_q.append(dot(grads, ks[:, h]))
-            to_k.append(dot_tn(grads, qs[:, h]))
-        gqs[:, :, lanes] = gqs[:, :, lanes] + tokens_of(jnp.concatenate(to_q, axis=1))
-        gv[:, :, lanes] = gv[:, :, lanes] + tokens_of(jnp.concatenate(to_v, axis=1))
-        gks[:, :, lanes] = tokens_of(jnp.concatenate(to_k, axis=1))
-
-    all_tiles(attention)
+    def attention(at, tiles):
+        qs, ks, vs, gs = (get(grid, at, tiles).astype(low) for grid in (q, k, v, g))
+        context = dot_tn(ks, vs).astype(low) * heads[...]
+        grads = dot_tn(qs, gs).astype(low) * heads[...]
+        to_q, to_k, to_v = dot_nt(gs, context), dot_nt(vs, grads), dot(ks, grads)
+        for n, j in enumerate(tiles):
+            here = slice(n * 128, n * 128 + 128)
+            gq[j, at, :] = gq[j, at, :] + to_q[:, here]
+            gk[j, at, :] = to_k[:, here]
+            gv[j, at, :] = gv[j, at, :] + to_v[:, here]
+
+    every_image(attention)
 
     def finish_qkv(j):
         lanes = lane_tile(j)
-        share = tokens_of(k[:, lanes].astype(jnp.float32))
-        up = gks[:, :, lanes]
+        share = tokens_of(k[j, live, :])
+        up = tokens_of(gk[j, live, :])
         along = jnp.sum(share * up, axis=0, keepdims=True) * 8.0
         gq_o[:, pl.ds(pl.multiple_of(D + j * 128, 128), 128)] = (
             (share * (up - along)).reshape(-1, 128).astype(low)
         )
-        part = gqs[:, :, lanes].reshape(-1, 128).astype(low)
+        part = gq[j, live, :].astype(low)
         gq_o[:, lanes] = part
-        cols_o[1, :, lanes] = cols_o[1, :, lanes] + column_partial(part.astype(jnp.float32))
-        part = gv[:, :, lanes].reshape(-1, 128).astype(low)
+        cols[1, :, lanes] = cols[1, :, lanes] + column_partial(part.astype(jnp.float32))
+        part = gv[j, live, :].astype(low)
         gq_o[:, pl.ds(pl.multiple_of(2 * D + j * 128, 128), 128)] = part
-        cols_o[2, :, lanes] = cols_o[2, :, lanes] + column_partial(part.astype(jnp.float32))
+        cols[2, :, lanes] = cols[2, :, lanes] + column_partial(part.astype(jnp.float32))
 
     all_tiles(finish_qkv)
-    gks[...] = tokens_of(dot_nt(gq_o[...], w_in[:, : 3 * D]))
-
-    def first_back(tokens, rows):
-        grad = gks[tokens].reshape(-1, D)
-        hats = hat[rows, :].astype(jnp.float32)
-        scale = sc[rows, 0:1]
-        total = gx[rows, :] + norm_back(grad, hats, scale, gains[0:1, :])
-        g1[tokens] = tokens_of(total)
-        cols_o[3] = cols_o[3] + column_partial(grad)
-        cols_o[4] = cols_o[4] + column_partial(grad * hats)
-        cols_o[5] = cols_o[5] + column_partial(total)
+    put(gk, live, dot_nt(gq_o[...], w_in[:, : 3 * D]))
+
+    def first_back(at):
+        grad = get(gk, at)
+        hats = hat[at, :].astype(jnp.float32)
+        total = gx[at, :] + norm_back(grad, hats, sc[at, 0:1], par[GAIN_ROW : GAIN_ROW + 1, :])
+        put(g1, at, total)
+        cols[3] = cols[3] + column_partial(grad)
+        cols[4] = cols[4] + column_partial(grad * hats)
+        cols[5] = cols[5] + column_partial(total)
 
     all_chunks(first_back)
-    cols_o[5] = cols_o[5] - g1[0]
+    cols[5] = cols[5] - get(g1, CLASS_ROWS)
 
     def position(j):
-        lanes = lane_tile(j)
-
-        def finish(token, total):
-            gv[token, :, lanes] = g1[token, :, lanes] + total
-
-        conv_tile(g1, taps, 0, 3, 1, lanes, finish, flip=True)
-        gv[0, :, lanes] = g1[0, :, lanes]
-        tap_sums(g1, xf, 0, 3, 1, lanes, taps_o)
+        def finish(at, total):
+            gv[j, at, :] = g1[j, at, :] + total
+
+        conv_tile(g1, par, 0, 3, 1, j, finish, flip=True)
+        gv[j, CLASS_ROWS, :] = g1[j, CLASS_ROWS, :]
+        tap_sums(g1, x, 0, 3, 1, j, taps)
 
     all_tiles(position)
-    value = rows_of(gv)
-    back = jnp.zeros((SIDE * SLOT, D), jnp.float32)
-    for _ in range(3):
-        piece = value.astype(low)
-        value = value - piece.astype(jnp.float32)
-        back = back + dot_tn(order[...], piece)
     for i in range(SIDE):
-        out[i] = back[i * SLOT : i * SLOT + out.shape[1], :]
+        out[i] = get(gv, pl.ds(i, out.shape[1], stride=SIDE))
+
+    @pl.when(step == pl.num_programs(0) - 1)
+    def _():
+        lines[...] = jnp.zeros_like(lines)
+        for tap in range(taps.shape[0]):
+            lines[tap : tap + 1, :] = jnp.sum(taps[tap], axis=0, keepdims=True)
+        mask_far_taps(lines)
+        hidden = [hcols_in[:, i * D : i * D + D] for i in range(MLP_WIDTH // D)]
+        order = [cols[4], cols_in[1], cols[3], cols_in[0], cols[1], cols[2], cols_in[2]]
+        for i, part in enumerate(order + hidden + [cols_in[3], cols[5], cols[0]]):
+            row = GAIN_ROW + i
+            lines[row : row + 1, :] = jnp.sum(part, axis=0, keepdims=True)
+        small_o[...] = lines[...].T
 
 
 def fixed(shape):
@@ -786,19 +817,12 @@
     return pl.BlockSpec(shape, lambda g: zeros, pipeline_mode=pl.Buffered(1))
 
 
-def compute(images, cotangent, counts, w_in, w_out, kern, gains, biases):
+def compute(images, cotangent, counts, w_in, w_out, small):
     low, full = jnp.bfloat16, jnp.float32
     num_images, num_tokens, channels = images.shape
     groups = -(-num_images // SIDE)
     rows = num_tokens * SIDE
     total = groups * rows
-    taps = jnp.concatenate([kern[:9], kern[9:] * tap_mask(channels)], axis=0)
-    row_ids = lax.broadcasted_iota(jnp.int32, (rows, SIDE * SLOT), 0)
-    col_ids = lax.broadcasted_iota(jnp.int32, (rows, SIDE * SLOT), 1)
-    order = (row_ids == (col_ids % SLOT) * SIDE + col_ids // SLOT).astype(low)
-    row_ids = lax.broadcasted_iota(jnp.int32, (rows, rows), 0)
-    col_ids = lax.broadcasted_iota(jnp.int32, (rows, rows), 1)
-    same = (row_ids % SIDE == col_ids % SIDE).astype(low)
 
     def block(cols):
         return pl.BlockSpec((rows, cols), lambda g: (g, 0))
@@ -809,24 +833,21 @@
     def made(cols, kind=low):
         return jax.ShapeDtypeStruct((total, cols), kind)
 
-    def grid_scratch(cols=channels):
-        return pltpu.VMEM((num_tokens, SIDE, cols), full)
-
+    def grid():
+        return pltpu.VMEM((channels // 128, TALL, 128), full)
+
+    shared = [pltpu.VMEM((128, channels), full), pltpu.VMEM((256, 256), low)]
     wide = w_out.shape[0]
     forward = pl.pallas_call(
-        functools.partial(forward_kernel, num_images),
+        functools.partial(forward_kernel, num_images, rows),
         grid=(groups,),
         in_specs=[
             pl.BlockSpec(memory_space=pltpu.SMEM),
             image_block(),
             image_block(),
-            fixed(order.shape),
-            fixed(same.shape),
             fixed(w_in.shape),
             fixed(w_out.shape),
-            fixed(taps.shape),
-            fixed(gains.shape),
-            fixed(biases.shape),
+            fixed(small.shape),
         ],
         out_specs=[image_block(), block(wide), block(wide)]
         + [block(channels)] * 8
@@ -841,48 +862,49 @@
             jax.ShapeDtypeStruct((4, SIDE, channels), full),
             jax.ShapeDtypeStruct((SIDE, wide), full),
         ],
-        scratch_shapes=[pltpu.VMEM((SIDE * SLOT, channels), low)]
-        + [grid_scratch() for _ in range(5)]
-        + [pltpu.VMEM((rows, wide), full), grid_scratch(), grid_scratch(128)],
+        scratch_shapes=shared
+        + [grid() for _ in range(6)]
+        + [pltpu.VMEM((rows, channels), full), pltpu.VMEM((rows, wide), full), grid(), pltpu.VMEM((rows, 128), full)],
         compiler_params=pltpu.CompilerParams(vmem_limit_bytes=60 << 20),
         name="forward",
     )
     (
         out, act, gh, n1, n2, attended, gf, gp, gx, xt, hat, scale, q, k, v, cv, cols, hcols,
-    ) = forward(counts, images, cotangent, order, same, w_in, w_out, taps, gains, biases)
+    ) = forward(counts, images, cotangent, w_in, w_out, small)
 
     backward = pl.pallas_call(
-        functools.partial(backward_kernel, num_images),
+        functools.partial(backward_kernel, rows),
         grid=(groups,),
         in_specs=[
-            fixed(order.shape),
-            fixed(same.shape),
-            fixed(w_in.shape),
-            fixed(taps.shape),
-            fixed(gains.shape),
+            pl.BlockSpec(
+                (channels, 4 * channels), lambda g: (0, 0), pipeline_mode=pl.Buffered(1)
+            ),
+            fixed(small.shape),
+            fixed(cols.shape),
+            fixed(hcols.shape),
             block(channels),
             block(channels),
             block(128),
         ]
         + [block(channels)] * 5,
-        out_specs=[
-            image_block(),
-            block(3 * channels),
-            fixed((6, SIDE, channels)),
-            fixed((taps.shape[0], SIDE, channels)),
-        ],
+        out_specs=[image_block(), block(3 * channels), fixed(small.shape)],
         out_shape=[
             jax.ShapeDtypeStruct(images.shape, full),
             made(3 * channels),
-            jax.ShapeDtypeStruct((6, SIDE, channels), full),
-            jax.ShapeDtypeStruct((taps.shape[0], SIDE, channels), full),
+            jax.ShapeDtypeStruct(small.shape, full),
         ],
-        scratch_shapes=[pltpu.VMEM((rows, channels), low)] + [grid_scratch() for _ in range(7)],
+        scratch_shapes=shared
+        + [
+            pltpu.VMEM((6, SIDE, channels), full),
+            pltpu.VMEM((GAIN_ROW, SIDE, channels), full),
+            pltpu.VMEM((128, channels), full),
+        ]
+        + [grid() for _ in range(10)],
         compiler_params=pltpu.CompilerParams(vmem_limit_bytes=60 << 20),
         name="backward",
     )
-    input_grad, gq, cols_back, grad_taps = backward(
-        order, same, w_in, taps, gains, gx, hat, scale, q, k, v, cv, xt
+    input_grad, gq, grad_small = backward(
+        w_in, small, cols, hcols, gx, hat, scale, q, k, v, cv, xt
     )
     grad_in = jnp.concatenate(
         [
@@ -893,26 +915,7 @@
         axis=1,
     )
     grad_out = cross_rows(act, gf).astype(low)
-    cols = jnp.sum(cols, axis=1)
-    hcols = jnp.sum(hcols, axis=0).reshape(-1, channels)
-    cols_back = jnp.sum(cols_back, axis=1)
-    grad_taps = jnp.sum(grad_taps, axis=1)
-    grad_kern = jnp.concatenate([grad_taps[:9], grad_taps[9:] * tap_mask(channels)], axis=0)
-    grad_gain = jnp.stack([cols_back[4], cols[1]])
-    grad_bias = jnp.concatenate(
-        [
-            cols_back[3:4],
-            cols[0:1],
-            cols_back[1:3],
-            cols[2:3],
-            hcols,
-            cols[3:4],
-            cols_back[5:6],
-            cols_back[0:1],
-        ],
-        axis=0,
-    )
-    return out, input_grad, grad_in, grad_out, grad_kern, grad_gain, grad_bias
+    return out, input_grad, grad_in, grad_out, grad_small
 
 
 def adamw_update(master, first_moment, second_moment, gradient, clip_factor, rate, decay):
@@ -948,74 +951,52 @@
 ):
     in_copy = in_mats.astype(jnp.bfloat16)
     out_copy = out_mat.astype(jnp.bfloat16)
-    kern_copy = kernels.astype(jnp.bfloat16)
-    gain_copy = gains.astype(jnp.bfloat16)
-    bias_copy = biases.astype(jnp.bfloat16)
-    shards = (kern_copy, gain_copy, bias_copy)
+    shards = (kernels, gains, biases)
     sizes = [shard.shape[0] for shard in shards]
+    used = sum(sizes)
+    count_row = jnp.broadcast_to(counts.astype(jnp.float32)[:, None], (1, kernels.shape[1]))
+    rows = jnp.concatenate(shards + (count_row,), axis=0)
+    small = jnp.pad(rows, ((0, 128 - used - 1), (0, 0))).T.astype(jnp.bfloat16)
     if special:
-        per = sum(sizes) * kern_copy.shape[1]
-        flat = jnp.concatenate(
-            [jnp.concatenate(shards, axis=0).reshape(-1), counts.astype(jnp.bfloat16)]
+        all_in, all_out, all_small = gather_all(in_copy, out_copy, small)
+    else:
+        all_in, all_out, all_small = (
+            lax.all_gather(part, ("wide", "narrow"), axis=0, tiled=True)
+            for part in (in_copy, out_copy, small)
         )
-        flat = jnp.pad(flat, (0, SMALL_ROWS * 128 - per - 1)).reshape(SMALL_ROWS, 128)
-        all_in, all_out, all_small = gather_all(in_copy, out_copy, flat)
-        all_small = all_small.reshape(32, SMALL_ROWS * 128)
-        live_total = jnp.sum(all_small[:, per].astype(jnp.float32)) * images.shape[1]
-        rows = all_small[:, :per].reshape(32, sum(sizes), -1).transpose(1, 0, 2)
-        rows = rows.reshape(sum(sizes), -1)
-        gathered = (
-            all_in.reshape(-1, in_copy.shape[1]),
-            all_out.reshape(-1, out_copy.shape[1]),
-            rows[: sizes[0]],
-            rows[sizes[0] : sizes[0] + sizes[1]],
-            rows[sizes[0] + sizes[1] :],
-        )
-    else:
-        gathered = (
-            lax.all_gather(in_copy, ("wide", "narrow"), axis=0, tiled=True),
-            lax.all_gather(out_copy, ("wide", "narrow"), axis=0, tiled=True),
-            lax.all_gather(kern_copy, ("wide", "narrow"), axis=1, tiled=True),
-            lax.all_gather(gain_copy, ("wide", "narrow"), axis=1, tiled=True),
-            lax.all_gather(bias_copy, ("wide", "narrow"), axis=1, tiled=True),
-        )
-        live_total = lax.psum(
-            counts[0].astype(jnp.float32) * images.shape[1], ("wide", "narrow")
-        )
-    wide_in = gathered[0]
-    wide_out = gathered[1]
-    kern_all = gathered[2].astype(jnp.float32)
-    gain_all = gathered[3].astype(jnp.float32)
-    bias_all = gathered[4].astype(jnp.float32)
+    all_small = all_small.reshape(-1, small.shape[0], 128)
+    live_total = jnp.sum(all_small[:, 0, used].astype(jnp.float32)) * images.shape[1]
     scale_factor = 1.0 / live_total
-    block_out, input_grad, grad_in, grad_fc2, grad_kern, grad_gain, grad_bias = compute(
-        images, cotangent, counts, wide_in, wide_out, kern_all, gain_all, bias_all
-    )
-    parts = (grad_kern, grad_gain, grad_bias)
+    block_out, input_grad, grad_in, grad_fc2, grad_small = compute(
+        images,
+        cotangent,
+        counts,
+        all_in.reshape(-1, in_copy.shape[1]),
+        all_out.reshape(-1, out_copy.shape[1]),
+        all_small.reshape(-1, 128),
+    )
     if special:
-        rows = jnp.concatenate(parts, axis=0)
-        small = rows.reshape(sum(sizes), 32, -1).transpose(1, 0, 2).reshape(32, per)
-        small = jnp.pad(small, ((0, 0), (0, SMALL_ROWS * 128 - per)))
-        sum_in, sum_out, sum_small, squares = reduce_all(
-            grad_in, grad_fc2, small
-        )
-        rows = sum_small.reshape(-1)[:per].reshape(sum(sizes), -1)
-        summed = (
-            sum_in,
-            sum_out,
-            rows[: sizes[0]],
-            rows[sizes[0] : sizes[0] + sizes[1]],
-            rows[sizes[0] + sizes[1] :],
-        )
+        sum_in, sum_out, sum_small, squares = reduce_all(grad_in, grad_fc2, grad_small)
         total_squares = jnp.sum(squares)
     else:
-        summed = tuple(
-            lax.psum_scatter(part.astype(jnp.float32), ("wide", "narrow"), scatter_dimension=dim, tiled=True)
-            for part, dim in zip((grad_in, grad_fc2) + parts, (0, 0, 1, 1, 1))
+        sum_in, sum_out, sum_small = (
+            lax.psum_scatter(
+                part.astype(jnp.float32), ("wide", "narrow"), scatter_dimension=0, tiled=True
+            )
+            for part in (grad_in, grad_fc2, grad_small)
         )
         total_squares = lax.psum(
-            sum(jnp.sum(part * part) for part in summed), ("wide", "narrow")
+            sum(jnp.sum(part * part) for part in (sum_in, sum_out, sum_small)),
+            ("wide", "narrow"),
         )
+    rows = sum_small.T
+    summed = (
+        sum_in,
+        sum_out,
+        rows[: sizes[0]],
+        rows[sizes[0] : sizes[0] + sizes[1]],
+        rows[sizes[0] + sizes[1] : used],
+    )
     summed = tuple(part * scale_factor for part in summed)
     grad_norm = jnp.sqrt(total_squares) * scale_factor
     clip_factor = jnp.minimum(1.0, 1.0 / (grad_norm + 1e-06))

time: 357 us -> 317 us (0.89)
  Pallas kernels: 278 us -> 261 us
  local copies, waits for them, and re-layouts: 21.7 us -> 9.59 us
  other arithmetic: 23.4 us -> 13.2 us
    pallas_call x2, Pallas kernels: 164 us -> 147 us  [the longest x1 87.7 us: compute(): forward(counts, images, cotangent, w_in, w_out, small)]
    concatenate x14 -> x1, local copies, waits for them, and re-layouts: 13 us -> 0.08 us  [local(): rows = jnp.concatenate(shards + (count_row,), axis=0)]
    unnamed x32 -> x36, local copies, waits for them, and re-layouts: 1.58 us -> 8.35 us
    convert_element_type x5, other arithmetic: 6.8 us -> 2.7 us  [adamw_update(): return (master_new, first_new, second_new, master_new.astype(jnp.bfloat16))]
    convert_element_type x8 -> x0, other arithmetic: 4 us -> none  [the longest x1 0.99 us: compute(): same = (row_ids % SIDE == col_ids % SIDE).astype(low)]
where the time goes in v3:
time: 317 us
  Pallas kernels  261 us (82%)
  matrix products  28.9 us (9%)
  other arithmetic  13.2 us (4%)
  local copies, waits for them, and re-layouts  9.59 us (3%)
  between operations  4.04 us (1%)
    pallas_call x1, Pallas kernels, compute(): forward(counts, images, cotangent, w_in, w_out, small)  87.7 us
    pallas_call x1, Pallas kernels, reduce_all(): pl.pallas_call(reduce_kernel, out_shape=(jax.ShapeDtypeStruct((rows_in, w...  73.9 us
    pallas_call x1, Pallas kernels, compute(): backward(w_in, small, cols, hcols, gx, hat, scale, q, k, v, cv, xt)  59 us
    pallas_call x1, Pallas kernels, gather_all(): pl.pallas_call(gather_kernel, out_shape=(jax.ShapeDtypeStruct((32,) + in_...  40.4 us
    dot_general x4, matrix products, cross_rows(): lax.dot_general(left, right, (((0,), (0,)), ((), ())), preferred_element_...  28.9 us
    unnamed x36, local copies, waits for them, and re-layouts  8.35 us

profile of v3, /device:TPU:0, one launch (start us, length us, event | category | flops | bytes accessed | tf_op | source)
XLA Modules:
  0.0 316.7 jit_solution(4563207359095761871)
XLA Ops:
  1.3 0.1 pad.12.clone
  1.4 0.7 broadcast_multiply_fusion.2
  2.1 0.7 broadcast_multiply_fusion.1
  2.7 0.8 broadcast_multiply_fusion
  3.5 0.1 copy.64
  3.6 0.7 convert.15
  4.3 0.1 copy.69
  4.4 0.1 copy.68
  4.5 0.1 copy.67
  4.6 0.8 copy.63
  5.3 0.1 maximum_maximum_fusion
  5.4 0.6 pad_bitcast_fusion.sm
  6.0 0.8 copy.71
  6.8 0.8 copy.72
  7.6 0.8 copy.70
  8.3 1.5 convert_element_type.46.wo
  9.9 1.6 convert_element_type.45.wi
  11.5 40.4 %gather_all.1 = (bf16[32,16,4096]{2,1,0:T(8,128)(2,1)}, bf16[32,64,512]{2,1,0:T(8,128)(2,1)}, bf16[32,16,128]{2,1,0:T(8,128)(2,1)}) custom-call(bf16[16,4096]{1,0:T(8,128)(2,1)} %convert_element_type.45.wi, bf16[64,512]{1,0:T(8,128)(2,1)} %convert_element_type.46.wo, bf16[16,128]{1,0:T(8,128)(2,1)} %pad_bitcast_fusion.sm), custom_call_target="tpu_custom_call" | custom-call | tf_op jit(solution)/shard_map/gather_all/pallas_call | solution.py:156
  51.9 1.6 convert_reduce_fusion
  54.1 87.7 %forward.1 = (bf16[34,50,512]{2,1,0:T(8,128)(2,1)}, bf16[2000,2048]{1,0:T(8,128)(2,1)}, bf16[2000,2048]{1,0:T(8,128)(2,1)}, bf16[2000,512]{1,0:T(8,128)(2,1)}, b...) custom-call(s32[1]{0:T(128)S(6)} %copy.84.counts, ...), custom_call_target="tpu_custom_call" | custom-call | tf_op jit(solution)/shard_map/forward/pallas_call | solution.py:873
  141.8 3.5 %convolution_convert_fusion.3 = bf16[512,512]{0,1:T(8,128)(2,1)S(1)} fusion(bf16[2000,512]{1,0:T(8,128)(2,1)} %get-tuple-element.68, bf16[2000,512]{1,0:T(8,128)(2,1)} %get-tuple-element.69), kind=kOutput, calls=%fused_computation.4 | convolution fusion | flops 1048838144 | bytes 4620288 | tf_op jit(solution)/shard_map/dot_general | solution.py:386
  145.3 0.2 copy.65
  145.6 10.0 %convolution_convert_fusion.1 = bf16[512,2048]{1,0:T(8,128)(2,1)} fusion(bf16[2000,512]{1,0:T(8,128)(2,1)} %get-tuple-element.70, bf16[2000,2048]{1,0:T(8,128)(2,1)} %get-tuple-element.71), kind=kOutput, calls=%fused_computation.2 | convolution fusion | flops 4195352576 | bytes 12337152 | tf_op jit(solution)/shard_map/dot_general | solution.py:386
  155.6 8.4 %convolution_convert_fusion = bf16[2048,512]{1,0:T(8,128)(2,1)S(1)} fusion(bf16[2000,2048]{1,0:T(8,128)(2,1)} %get-tuple-element.72, bf16[2000,512]{1,0:T(8,128)(2,1)S(1)} %copy-done.11), kind=kOutput, calls=%fused_computation.1 | convolution fusion | flops 4195352576 | bytes 12337152 | tf_op jit(solution)/shard_map/dot_general | solution.py:386
  164.0 59.0 %backward.1 = (f32[34,50,512]{2,1,0:T(8,128)}, bf16[2000,1536]{1,0:T(8,128)(2,1)}, f32[512,128]{1,0:T(8,128)}) custom-call(bf16[512,4096]{1,0:T(8,128)(2,1)} %bitcast.24, bf16[512,128]{1,0:T(8,128)(2,1)} %bitcast.28, f32[4,8,512]{2,1,0:T(8,128)} %get-tuple-element.55.cols_in, f32[8,2048]{1,0:T(8,128)} %get-tuple-element.56.hcols_in, ...), custom_call_target="tpu_custom_call" | custom-call | tf_op jit(solution)/shard_map/backward/pallas_call | solution.py:906
  223.0 7.0 %convolution_convert_fusion.2 = bf16[512,1536]{1,0:T(8,128)(2,1)S(1)} fusion(bf16[2000,512]{1,0:T(8,128)(2,1)} %get-tuple-element.66, bf16[2000,1536]{1,0:T(8,128)(2,1)} %get-tuple-element.67), kind=kOutput, calls=%fused_computation.3 | convolution fusion | flops 3146514432 | bytes 9764864 | tf_op jit(solution)/shard_map/dot_general | solution.py:386
  230.0 0.0 copy-start
  230.0 2.2 pad_maximum_fusion
  232.2 0.0 copy-start.3
  232.3 0.0 copy-start.6
  232.3 0.0 copy-start.7
  232.3 0.0 copy-start.2
  232.3 0.0 copy-start.4
  232.3 73.9 %reduce_all.1 = (f32[16,4096]{1,0:T(8,128)S(1)}, f32[64,512]{1,0:T(8,128)S(1)}, f32[16,128]{1,0:T(8,128)S(1)}, f32[8,128]{1,0:T(8,128)S(1)}) custom-call(bf16[4,2,2,2,16,4096]{5,4,3,2,1,0:T(8,128)(2,1)} %bitcast.25, bf16[4,2,2,2,64,512]{5,4,3,2,1,0:T(8,128)(2,1)S(1)} %bitcast.18, f32[4,2,2,2,16,128]{5,4,3,2,1,0:T(8,128)S(1)} %bitcast.19), custom_call_target="tpu_custom_call" | custom-call | tf_op jit(solution)/shard_map/reduce_all/pallas_call | solution.py:367
  306.2 0.6 reduce_sum.18
  307.6 0.1 fusion.10
  307.7 0.6 copy.78
  308.3 0.6 copy.75
  308.9 0.6 copy.76
  309.6 0.6 copy.77
  310.2 0.1 fusion.8
  310.3 0.7 copy.82
  311.0 0.7 copy.79
  311.7 0.7 copy.80
  312.3 0.7 copy.81
  313.0 0.6 fusion.12
  313.7 0.8 fusion.14
  314.5 1.1 fusion.16
  (19 shorter events, 0.0 us)
Async XLA Ops:
  145.6 10.1 %copy-start.11 = (bf16[2000,512]{1,0:T(8,128)(2,1)S(1)}, bf16[2000,512]{1,0:T(8,128)(2,1)}, u32[]{:S(2)}) copy-start(bf16[2000,512]{1,0:T(8,128)(2,1)} %get-tuple-element.73) | copy-start | bytes 6144004
  223.0 7.0 %copy-start.1 = (bf16[512,2048]{1,0:T(8,128)(2,1)S(1)}, bf16[512,2048]{1,0:T(8,128)(2,1)}, u32[]{:S(2)}) copy-start(bf16[512,2048]{1,0:T(8,128)(2,1)} %convolution_convert_fusion.1) | copy-start | bytes 6291460
  230.0 2.3 copy-start
  232.2 80.8 %copy-start.8 = (f32[58,16]{0,1:T(8,128)S(1)}, f32[58,16]{0,1:T(8,128)}, u32[]{:S(2)}) copy-start(f32[58,16]{0,1:T(8,128)} %param.27) | copy-start | bytes 11140
  232.2 80.8 %copy-start.9 = (f32[58,16]{0,1:T(8,128)S(1)}, f32[58,16]{0,1:T(8,128)}, u32[]{:S(2)}) copy-start(f32[58,16]{0,1:T(8,128)} %param.28) | copy-start | bytes 11140
  232.2 80.8 %copy-start.10 = (f32[58,16]{0,1:T(8,128)S(1)}, f32[58,16]{0,1:T(8,128)}, u32[]{:S(2)}) copy-start(f32[58,16]{0,1:T(8,128)} %param.29) | copy-start | bytes 11140
  232.2 81.4 %copy-start.3 = (f32[64,512]{1,0:T(8,128)S(1)}, f32[64,512]{1,0:T(8,128)}, u32[]{:S(2)}) copy-start(f32[64,512]{1,0:T(8,128)} %param.24) | copy-start | bytes 393220
  232.3 81.4 %copy-start.6 = (f32[64,512]{1,0:T(8,128)S(1)}, f32[64,512]{1,0:T(8,128)}, u32[]{:S(2)}) copy-start(f32[64,512]{1,0:T(8,128)} %param.25) | copy-start | bytes 393220
  232.3 81.4 %copy-start.7 = (f32[64,512]{1,0:T(8,128)S(1)}, f32[64,512]{1,0:T(8,128)}, u32[]{:S(2)}) copy-start(f32[64,512]{1,0:T(8,128)} %param.26) | copy-start | bytes 393220
  232.3 82.2 %copy-start.2 = (f32[16,4096]{1,0:T(8,128)S(1)}, f32[16,4096]{1,0:T(8,128)}, u32[]{:S(2)}) copy-start(f32[16,4096]{1,0:T(8,128)} %param.21) | copy-start | bytes 786436
  232.3 82.2 %copy-start.4 = (f32[16,4096]{1,0:T(8,128)S(1)}, f32[16,4096]{1,0:T(8,128)}, u32[]{:S(2)}) copy-start(f32[16,4096]{1,0:T(8,128)} %param.22) | copy-start | bytes 786436
  232.3 82.2 %copy-start.5 = (f32[16,4096]{1,0:T(8,128)S(1)}, f32[16,4096]{1,0:T(8,128)}, u32[]{:S(2)}) copy-start(f32[16,4096]{1,0:T(8,128)} %param.23) | copy-start | bytes 786436

commit v4 on v3

--- a/solution.py
+++ b/solution.py
@@ -176,25 +176,60 @@
     return (left.astype(jnp.float32) + right.astype(jnp.float32)).astype(left.dtype)
 
 
+IN_CHUNKS = 4
+OUT_CHUNKS = 2
+LAGS = (1, 3, 5, 7)
+
+
 def reduce_kernel(
-    gi, go, gs, fi, fo, fs, fq,
-    ai, ao, a_s, b1, b2i, b2o, b2s, b3,
-    ri, ro, rs, r1, r2i, r2o, r2s, r3,
-    t1, t2i, t2o, t2s, u1, u2i, u2o, u2s,
-    squares_narrow, squares_wide, send_sem, recv_sem, norm_send, norm_recv,
+    n1_h, gq_h, at_h, gp_h, n2_h, gh_h, act_h, gf_h, gs, fi, fo, fs, fq,
+    n1, gq, at_v, gp, n2, gh, act, gf,
+    gi, go, r0i, r0o, r0s, r1i, r1o, r1s, r2i, r2o, r2s, r3i, r3o, r3s,
+    squares_narrow, squares_wide, load_sem, send_sem, recv_sem, norm_send, norm_recv,
 ):
     at = place()
     z, y, x, c = at
     w = z * 2 + y
     n = x * 2 + c
+    loads = []
+    half = gh.shape[1] // 2
+    for src, dst, cols in (
+        (n2_h, n2, None),
+        (gh_h, gh, pl.ds(0, half)),
+        (gh_h, gh, pl.ds(half, half)),
+        (gf_h, gf, None),
+        (act_h, act, None),
+        (n1_h, n1, None),
+        (gq_h, gq, None),
+        (at_h, at_v, None),
+        (gp_h, gp, None),
+    ):
+        real, padded = src.shape[0], dst.shape[0]
+        if cols is None:
+            cols = pl.ds(0, src.shape[1])
+        if padded > real:
+            dst[pl.ds(real, padded - real), cols] = jnp.zeros(
+                (padded - real, cols.size), dst.dtype
+            )
+        src, dst = src.at[:, cols], dst.at[pl.ds(0, real), cols]
+        copy = pltpu.make_async_copy(src, dst, load_sem.at[len(loads)])
+        copy.start()
+        loads.append(copy)
+    waited = [0]
+
+    def loaded(upto):
+        while waited[0] < upto:
+            loads[waited[0]].wait()
+            waited[0] += 1
+
     partners = [(w, lax.rem(n + s, 4)) for s in (1, 2, 3)]
     partners += [(lax.rem(w + s, 8), n) for s in range(1, 8)]
     barrier = pltpu.get_barrier_semaphore()
     for partner in partners:
         pl.semaphore_signal(barrier, inc=1, device_id=partner, device_id_type=MESH_ID)
-    pl.semaphore_wait(barrier, len(partners))
 
     count = [0]
+    sent = []
 
     def send(src, dst, axis, step=1):
         index = count[0]
@@ -208,98 +243,134 @@
             device_id_type=MESH_ID,
         )
         copy.start()
+        sent.append(copy)
         return copy
 
-    first = [
-        send(gi.at[:, :, :, 1 - c], ri, 3),
-        send(go.at[:, :, :, 1 - c], ro, 3),
-        send(gs.at[:, :, :, 1 - c], rs, 3),
-    ]
-    for copy in first:
-        copy.wait_recv()
-
-    def add_first(k, carry):
-        zi, yi, xi = k // 4, lax.rem(k // 2, 2), lax.rem(k, 2)
-        ai[zi, yi, xi] = add_low(gi[zi, yi, xi, c], ri[zi, yi, xi])
-        ao[zi, yi, xi] = add_low(go[zi, yi, xi, c], ro[zi, yi, xi])
-        a_s[zi, yi, xi] = add_low(gs[zi, yi, xi, c], rs[zi, yi, xi])
-        return carry
-
-    lax.fori_loop(0, 16, add_first, 0)
-    width = gi.shape[-1]
-    left, right = pl.ds(0, SPLIT), pl.ds(SPLIT, width - SPLIT)
-    second = [
-        send(ai.at[:, :, 1 - x, :, left], r1, 2),
-        send(ai.at[:, 1 - y, :, :, right], r2i, 1),
-        send(ao.at[:, 1 - y], r2o, 1),
-        send(a_s.at[:, 1 - y], r2s, 1),
-    ]
-    for copy in second:
-        copy.wait_recv()
-
-    def add_second(k, carry):
-        zi, j = k // 2, lax.rem(k, 2)
-        b1[zi, j] = add_low(ai[zi, j, x, :, left], r1[zi, j])
-        b2i[zi, j] = add_low(ai[zi, y, j, :, right], r2i[zi, j])
-        b2o[zi, j] = add_low(ao[zi, y, j], r2o[zi, j])
-        b2s[zi, j] = add_low(a_s[zi, y, j], r2s[zi, j])
-        return carry
-
-    lax.fori_loop(0, 8, add_second, 0)
-    third = [
-        send(b1.at[:, 1 - y], r3, 1),
-        send(b2i.at[:, 1 - x], t2i, 2),
-        send(b2o.at[:, 1 - x], t2o, 2),
-        send(b2s.at[:, 1 - x], t2s, 2),
-    ]
-    for copy in third:
-        copy.wait_recv()
-
-    def add_third(k, carry):
-        b3[k] = add_low(b1[k, y], r3[k])
-        r2i[k, 0] = add_low(b2i[k, x], t2i[k])
-        r2o[k, 0] = add_low(b2o[k, x], t2o[k])
-        r2s[k, 0] = add_low(b2s[k, x], t2s[k])
-        return carry
-
-    lax.fori_loop(0, 4, add_third, 0)
-    fourth = []
-    for step in (1, 2, 3):
-        to = lax.rem(z + step, 4)
-        fourth += [
-            send(b3.at[to], u1.at[step - 1], 0, step),
-            send(r2i.at[to, 0], u2i.at[step - 1], 0, step),
-            send(r2o.at[to, 0], u2o.at[step - 1], 0, step),
-            send(r2s.at[to, 0], u2s.at[step - 1], 0, step),
+    def product(left, right, cols):
+        value = dot_tn(left[...], right[:, cols]).astype(gi.dtype)
+        return value.reshape(4, 2, 2, 2, -1, value.shape[1])
+
+    def make_in(chunk):
+        width = gi.shape[-1]
+        if chunk >= 2:
+            loaded(chunk)
+            gi[chunk] = product(n2, gh, pl.ds((chunk - 2) * width, width))
+        elif chunk == 1:
+            loaded(9)
+            gi[1, :, :, :, :, :, pl.ds(0, D)] = product(n1, gq, pl.ds(width, D))
+            gi[1, :, :, :, :, :, pl.ds(D, D)] = product(at_v, gp, pl.ds(0, D))
+        else:
+            loaded(7)
+            gi[0] = product(n1, gq, pl.ds(0, width))
+
+    def make_out(chunk):
+        if chunk:
+            return
+        loaded(5)
+        width = go.shape[-1]
+
+        def block(m, carry):
+            left = act[:, pl.ds(pl.multiple_of(m * D, D), D)]
+            value = dot_tn(left, gf[...]).astype(go.dtype)
+            for k in range(OUT_CHUNKS):
+                part = value[:, k * width : k * width + width]
+                go[k, m] = part.reshape(2, 2, 2, -1, width)
+            return carry
+
+        lax.fori_loop(0, 4, block, 0)
+
+    def entry(make, chunk, color, g, r0, r1, r2, r3, out, cols):
+        return dict(
+            make=make, chunk=chunk, color=color, g=g, r0=r0, r1=r1, r2=r2, r3=r3, out=out, cols=cols
+        )
+
+    entries = [entry(None, 0, 1, gs, r0s, r1s, r2s, r3s, fs, pl.ds(0, 128))]
+
+    def in_entry(chunk, color):
+        refs = [ref.at[chunk] for ref in (gi, r0i, r1i, r2i, r3i)]
+        width = gi.shape[-1]
+        return entry(make_in, chunk, color, *refs, fi, pl.ds(chunk * width, width))
+
+    def out_entry(chunk, color):
+        refs = [ref.at[chunk] for ref in (go, r0o, r1o, r2o, r3o)]
+        width = go.shape[-1]
+        return entry(make_out, chunk, color, *refs, fo, pl.ds(chunk * width, width))
+
+    entries += [in_entry(2, 0), in_entry(3, 1), out_entry(0, 0), out_entry(1, 1)]
+    entries += [in_entry(0, 0), in_entry(1, 1)]
+
+    def begin(e):
+        e["copy"] = send(e["g"].at[:, :, :, 1 - c], e["r0"], 3)
+
+    def across(e):
+        e["copy"].wait_recv()
+        g, r0 = e["g"], e["r0"]
+
+        def add(k, carry):
+            zi, yi, xi = k // 4, lax.rem(k // 2, 2), lax.rem(k, 2)
+            r0[zi, yi, xi] = add_low(g[zi, yi, xi, c], r0[zi, yi, xi])
+            return carry
+
+        lax.fori_loop(0, 16, add, 0)
+        if e["color"] == 0:
+            e["copy"] = send(r0.at[:, :, 1 - x], e["r1"], 2)
+        else:
+            e["copy"] = send(r0.at[:, 1 - y], e["r1"], 1)
+
+    def onward(e):
+        e["copy"].wait_recv()
+        r0, r1, color = e["r0"], e["r1"], e["color"]
+
+        def add(k, carry):
+            zi, j = k // 2, lax.rem(k, 2)
+            own = r0[zi, j, x] if color == 0 else r0[zi, y, j]
+            r1[zi, j] = add_low(own, r1[zi, j])
+            return carry
+
+        lax.fori_loop(0, 8, add, 0)
+        if color == 0:
+            e["copy"] = send(r1.at[:, 1 - y], e["r2"], 1)
+        else:
+            e["copy"] = send(r1.at[:, 1 - x], e["r2"], 2)
+
+    def along(e):
+        e["copy"].wait_recv()
+        r1, r2, keep = e["r1"], e["r2"], y if e["color"] == 0 else x
+
+        def add(k, carry):
+            r2[k] = add_low(r1[k, keep], r2[k])
+            return carry
+
+        lax.fori_loop(0, 4, add, 0)
+        e["copies"] = [
+            send(r2.at[lax.rem(z + step, 4)], e["r3"].at[step - 1], 0, step) for step in (1, 2, 3)
         ]
-    for copy in fourth:
-        copy.wait_recv()
-
-    def total(own, others):
-        value = own.astype(jnp.float32)
+
+    squares = [jnp.zeros((8, 128), jnp.float32)]
+
+    def finish(e):
+        for copy in e["copies"]:
+            copy.wait_recv()
+        value = e["r2"][z].astype(jnp.float32)
         for k in range(3):
-            value = value + others[k].astype(jnp.float32)
-        return value
-
-    squares = jnp.zeros((8, 128), jnp.float32)
-
-    def tile_squares(value, squares):
+            value = value + e["r3"][k].astype(jnp.float32)
+        e["out"][:, e["cols"]] = value
         rows, cols = value.shape
-        for i in range(rows // 8):
-            for j in range(cols // 128):
-                part = value[i * 8 : i * 8 + 8, j * 128 : j * 128 + 128]
-                squares = squares + part * part
-        return squares
-
-    for own, others, out, cols in (
-        (b3[z], u1, fi, left),
-        (r2i[z, 0], u2i, fi, right),
-        (r2o[z, 0], u2o, fo, pl.ds(0, fo.shape[1])),
-        (r2s[z, 0], u2s, fs, pl.ds(0, 128)),
-    ):
-        value = total(own, others)
-        out[:, cols] = value
-        squares = tile_squares(value, squares)
+        total = jnp.sum((value * value).reshape(rows // 8, 8, cols), axis=0)
+        for j in range(cols // 128):
+            squares[0] = squares[0] + total[:, j * 128 : j * 128 + 128]
+
+    for t in range(len(entries) + LAGS[-1]):
+        for action, lag in zip((finish, along, onward, across), LAGS[::-1]):
+            if 0 <= t - lag < len(entries):
+                action(entries[t - lag])
+        if t < len(entries):
+            e = entries[t]
+            if e["make"] is not None:
+                e["make"](e["chunk"])
+            if t == 0:
+                pl.semaphore_wait(barrier, len(partners))
+            begin(e)
 
     def exchange(buffer, mine, size, axis, base):
         copies = []
@@ -322,64 +393,58 @@
             value = value + buffer[k]
         return value
 
-    squares_narrow[n] = squares
-    squares = exchange(squares_narrow, n, 4, 1, 0)
-    squares_wide[w] = squares
+    squares_narrow[n] = squares[0]
+    squares_wide[w] = exchange(squares_narrow, n, 4, 1, 0)
     fq[...] = exchange(squares_wide, w, 8, 0, 4)
-    for copy in first + second + third + fourth:
+    for copy in sent:
         copy.wait_send()
 
 
-def reduce_all(grad_in, grad_out, small):
-    low = jnp.bfloat16
-    rows_in, width = grad_in.shape[0] // 32, grad_in.shape[1]
-    rows_out, cols_out = grad_out.shape[0] // 32, grad_out.shape[1]
-    gi = grad_in.reshape(4, 2, 2, 2, rows_in, width)
-    go = grad_out.reshape(4, 2, 2, 2, rows_out, cols_out)
-    gs = small.reshape(4, 2, 2, 2, SMALL_ROWS, 128)
-    rest = width - SPLIT
+def reduce_all(n1, gq, attended, gp, n2, gh, act, gf, small):
+    low, full = jnp.bfloat16, jnp.float32
+    arrays = (n1, gq, attended, gp, n2, gh, act, gf)
+    width = gq.shape[1] + gp.shape[1] + gh.shape[1]
+    rows_in, rows_out = n1.shape[1] // 32, act.shape[1] // 32
+    cols_out = gf.shape[1]
     vmem = pl.BlockSpec(memory_space=pltpu.VMEM)
-
-    def trio(lead, cols, own=True):
-        kinds = [
-            pltpu.VMEM(lead + (rows_in, cols), low),
-            pltpu.VMEM(lead + (rows_out, cols_out), low),
-            pltpu.VMEM(lead + (SMALL_ROWS, 128), jnp.float32),
+    hbm = pl.BlockSpec(memory_space=pl.ANY)
+
+    def trio(lead):
+        return [
+            pltpu.VMEM((IN_CHUNKS,) + lead + (rows_in, width // IN_CHUNKS), low),
+            pltpu.VMEM((OUT_CHUNKS,) + lead + (rows_out, cols_out // OUT_CHUNKS), low),
+            pltpu.VMEM(lead + (SMALL_ROWS, 128), full),
         ]
-        return kinds
-
-    scratch = trio((4, 2, 2), width)
-    scratch += [pltpu.VMEM((4, 2, rows_in, SPLIT), low)] + trio((4, 2), rest)
-    scratch += [pltpu.VMEM((4, rows_in, SPLIT), low)]
-    scratch += trio((4, 2, 2), width)
-    scratch += [pltpu.VMEM((4, 2, rows_in, SPLIT), low)] + trio((4, 2), rest)
-    scratch += [pltpu.VMEM((4, rows_in, SPLIT), low)]
-    scratch += [pltpu.VMEM((1, 8, 128), low)] + trio((4,), rest)
-    scratch += [pltpu.VMEM((3, rows_in, SPLIT), low)] + trio((3,), rest)
+
+    padded = -(-n1.shape[0] // 256) * 256
+    scratch = [pltpu.VMEM((padded, array.shape[1]), array.dtype) for array in arrays]
+    scratch += trio((4, 2, 2, 2))[:2] + trio((4, 2, 2)) + trio((4, 2)) + trio((4,)) + trio((3,))
+    copies = (IN_CHUNKS + OUT_CHUNKS + 1) * 6
     scratch += [
-        pltpu.VMEM((4, 8, 128), jnp.float32),
-        pltpu.VMEM((8, 8, 128), jnp.float32),
-        pltpu.SemaphoreType.DMA((23,)),
-        pltpu.SemaphoreType.DMA((23,)),
+        pltpu.VMEM((4, 8, 128), full),
+        pltpu.VMEM((8, 8, 128), full),
+        pltpu.SemaphoreType.DMA((len(arrays) + 1,)),
+        pltpu.SemaphoreType.DMA((copies,)),
+        pltpu.SemaphoreType.DMA((copies,)),
         pltpu.SemaphoreType.DMA((12,)),
         pltpu.SemaphoreType.DMA((12,)),
     ]
     return pl.pallas_call(
         reduce_kernel,
         out_shape=(
-            jax.ShapeDtypeStruct((rows_in, width), jnp.float32),
-            jax.ShapeDtypeStruct((rows_out, cols_out), jnp.float32),
-            jax.ShapeDtypeStruct((SMALL_ROWS, 128), jnp.float32),
-            jax.ShapeDtypeStruct((8, 128), jnp.float32),
+            jax.ShapeDtypeStruct((rows_in, width), full),
+            jax.ShapeDtypeStruct((rows_out, cols_out), full),
+            jax.ShapeDtypeStruct((SMALL_ROWS, 128), full),
+            jax.ShapeDtypeStruct((8, 128), full),
         ),
-        in_specs=[vmem] * 3,
+        in_specs=[hbm] * 8 + [vmem],
         out_specs=(vmem,) * 4,
         scratch_shapes=scratch,
         compiler_params=pltpu.CompilerParams(
-            collective_id=1, has_side_effects=True, vmem_limit_bytes=48 << 20
+            collective_id=1, has_side_effects=True, vmem_limit_bytes=62 << 20
         ),
         name="reduce_all",
-    )(gi, go, gs)
+    )(*arrays, small.reshape(4, 2, 2, 2, SMALL_ROWS, 128))
 
 
 def cross_rows(left, right):
@@ -906,16 +971,7 @@
     input_grad, gq, grad_small = backward(
         w_in, small, cols, hcols, gx, hat, scale, q, k, v, cv, xt
     )
-    grad_in = jnp.concatenate(
-        [
-            cross_rows(n1, gq).astype(low),
-            cross_rows(attended, gp).astype(low),
-            cross_rows(n2, gh).astype(low),
-        ],
-        axis=1,
-    )
-    grad_out = cross_rows(act, gf).astype(low)
-    return out, input_grad, grad_in, grad_out, grad_small
+    return out, input_grad, (n1, gq, attended, gp, n2, gh, act, gf), grad_small
 
 
 def adamw_update(master, first_moment, second_moment, gradient, clip_factor, rate, decay):
@@ -967,7 +1023,7 @@
     all_small = all_small.reshape(-1, small.shape[0], 128)
     live_total = jnp.sum(all_small[:, 0, used].astype(jnp.float32)) * images.shape[1]
     scale_factor = 1.0 / live_total
-    block_out, input_grad, grad_in, grad_fc2, grad_small = compute(
+    block_out, input_grad, factors, grad_small = compute(
         images,
         cotangent,
         counts,
@@ -976,9 +1032,14 @@
         all_small.reshape(-1, 128),
     )
     if special:
-        sum_in, sum_out, sum_small, squares = reduce_all(grad_in, grad_fc2, grad_small)
+        sum_in, sum_out, sum_small, squares = reduce_all(*factors, grad_small)
         total_squares = jnp.sum(squares)
     else:
+        n1, gq, attended, gp, n2, gh, act, gf = factors
+        grad_in = jnp.concatenate(
+            [cross_rows(n1, gq), cross_rows(attended, gp), cross_rows(n2, gh)], axis=1
+        )
+        grad_fc2 = cross_rows(act, gf)
         sum_in, sum_out, sum_small = (
             lax.psum_scatter(
                 part.astype(jnp.float32), ("wide", "narrow"), scatter_dimension=0, tiled=True

time: 317 us -> 278 us (0.88)
  matrix products: 28.9 us -> 0 us
  Pallas kernels: 261 us -> 252 us
    dot_general x4 -> x0, matrix products: 28.9 us -> none  [cross_rows(): lax.dot_general(left, right, (((0,), (0,)), ((), ())), preferred_element_...]
    pallas_call x1, Pallas kernels: 73.9 us -> 65.3 us  [reduce_all(): pl.pallas_call(reduce_kernel, out_shape=(jax.ShapeDtypeStruct((rows_in, w...]
    convert_element_type x5, other arithmetic: 2.7 us -> 6.64 us  [adamw_update(): return (master_new, first_new, second_new, master_new.astype(jnp.bfloat16))]
    unnamed x36 -> x40, local copies, waits for them, and re-layouts: 8.35 us -> 6.32 us
where the time goes in v4:
time: 278 us
  Pallas kernels  252 us (91%)
  other arithmetic  14.2 us (5%)
  local copies, waits for them, and re-layouts  7.35 us (3%)
  between operations  4.06 us (1%)
    pallas_call x1, Pallas kernels, compute(): forward(counts, images, cotangent, w_in, w_out, small)  87.5 us
    pallas_call x1, Pallas kernels, reduce_all(): pl.pallas_call(reduce_kernel, out_shape=(jax.ShapeDtypeStruct((rows_in, w...  65.3 us
    pallas_call x1, Pallas kernels, compute(): backward(w_in, small, cols, hcols, gx, hat, scale, q, k, v, cv, xt)  59 us
    pallas_call x1, Pallas kernels, gather_all(): pl.pallas_call(gather_kernel, out_shape=(jax.ShapeDtypeStruct((32,) + in_...  40.4 us
    convert_element_type x5, other arithmetic, adamw_update(): return (master_new, first_new, second_new, master_new.astype(jnp.bfloat16))  6.64 us
    unnamed x40, local copies, waits for them, and re-layouts  6.32 us

profile of v4, /device:TPU:0, one launch (start us, length us, event | category | flops | bytes accessed | tf_op | source)
XLA Modules:
  0.0 277.8 jit_solution(10104263236692600966)
XLA Ops:
  0.7 0.8 copy.62
  1.4 0.8 broadcast_multiply_fusion
  2.2 0.1 copy.63
  2.9 0.1 pad.9.clone
  3.0 0.7 convert.15
  3.7 0.1 maximum_maximum_fusion
  3.8 0.6 pad_bitcast_fusion.sm
  4.4 1.6 convert_element_type.33.wi
  6.0 1.5 convert_element_type.34.wo
  7.6 40.4 %gather_all.1 = (bf16[32,16,4096]{2,1,0:T(8,128)(2,1)}, bf16[32,64,512]{2,1,0:T(8,128)(2,1)}, bf16[32,16,128]{2,1,0:T(8,128)(2,1)}) custom-call(bf16[16,4096]{1,0:T(8,128)(2,1)} %convert_element_type.33.wi, bf16[64,512]{1,0:T(8,128)(2,1)} %convert_element_type.34.wo, bf16[16,128]{1,0:T(8,128)(2,1)} %pad_bitcast_fusion.sm), custom_call_target="tpu_custom_call" | custom-call | tf_op jit(solution)/shard_map/gather_all/pallas_call | solution.py:156
  48.0 87.5 %forward.1 = (bf16[34,50,512]{2,1,0:T(8,128)(2,1)}, bf16[2000,2048]{1,0:T(8,128)(2,1)}, bf16[2000,2048]{1,0:T(8,128)(2,1)}, bf16[2000,512]{1,0:T(8,128)(2,1)}, b...) custom-call(s32[1]{0:T(128)S(6)} %copy.82.counts, ...), custom_call_target="tpu_custom_call" | custom-call | tf_op jit(solution)/shard_map/forward/pallas_call | solution.py:938
  135.5 59.0 %backward.1 = (f32[34,50,512]{2,1,0:T(8,128)}, bf16[2000,1536]{1,0:T(8,128)(2,1)}, f32[512,128]{1,0:T(8,128)}) custom-call(bf16[512,4096]{1,0:T(8,128)(2,1)} %bitcast.9, bf16[512,128]{1,0:T(8,128)(2,1)} %bitcast.12, f32[4,8,512]{2,1,0:T(8,128)} %get-tuple-element.55.cols_in, f32[8,2048]{1,0:T(8,128)} %get-tuple-element.56.hcols_in, ...), custom_call_target="tpu_custom_call" | custom-call | tf_op jit(solution)/shard_map/backward/pallas_call | solution.py:971
  194.5 0.0 copy-start.9
  194.5 0.0 copy-start.10
  194.5 0.0 copy-start.12
  194.5 0.0 copy-start.13
  194.5 0.0 copy-start.11
  194.5 0.0 copy-start.6
  194.5 0.0 copy-start.7
  194.5 0.0 copy-start.8
  194.6 0.0 copy-start.1
  194.6 0.0 copy-start.4
  194.6 0.0 copy-start.5
  194.6 0.0 copy-start
  194.6 0.0 copy-start.2
  194.6 0.0 copy-start.3
  194.6 65.3 %reduce_all.1 = (f32[16,4096]{1,0:T(8,128)}, f32[64,512]{1,0:T(8,128)}, f32[16,128]{1,0:T(8,128)}, f32[8,128]{1,0:T(8,128)}) custom-call(bf16[2000,512]{1,0:T(8,128)(2,1)} %get-tuple-element.66.n1_h, bf16[2000,1536]{1,0:T(8,128)(2,1)} %get-tuple-element.67.gq_h, bf16[2000,512]{1,0:T(8,128)(2,1)} %get-tuple-element.68.at_h, ...), custom_call_target="tpu_custom_call" | custom-call | tf_op jit(solution)/shard_map/reduce_all/pallas_call | solution.py:432
  259.9 1.3 reduce_sum.18
  261.9 1.6 convert_reduce_fusion
  264.2 0.1 copy.69
  264.3 0.1 copy.70
  264.4 0.8 fusion.8
  265.2 0.7 copy.77
  265.9 0.7 copy.78
  266.5 0.7 copy.79
  267.2 0.7 copy.80
  267.9 0.1 copy.67
  268.0 0.1 copy.65
  268.1 0.1 copy.66
  268.2 0.1 copy.68
  268.2 0.8 fusion.10
  269.0 0.6 copy.73
  269.7 0.6 copy.74
  270.3 0.6 copy.75
  271.0 0.6 copy.76
  271.6 1.3 fusion.12
  272.9 1.7 fusion.14
  274.6 2.0 fusion.16
  (17 shorter events, 0.0 us)
Async XLA Ops:
  194.5 69.8 %copy-start.9 = (f32[12,16]{1,0:T(8,128)S(1)}, f32[12,16]{1,0:T(8,128)}, u32[]{:S(2)}) copy-start(f32[12,16]{1,0:T(8,128)} %param.34) | copy-start | bytes 2308
  194.5 69.8 %copy-start.10 = (f32[12,16]{1,0:T(8,128)S(1)}, f32[12,16]{1,0:T(8,128)}, u32[]{:S(2)}) copy-start(f32[12,16]{1,0:T(8,128)} %param.35) | copy-start | bytes 2308
  194.5 73.5 %copy-start.12 = (f32[2,16]{1,0:T(2,128)S(1)}, f32[2,16]{1,0:T(2,128)}, u32[]{:S(2)}) copy-start(f32[2,16]{1,0:T(2,128)} %param.31) | copy-start | bytes 388
  194.5 73.6 %copy-start.13 = (f32[2,16]{1,0:T(2,128)S(1)}, f32[2,16]{1,0:T(2,128)}, u32[]{:S(2)}) copy-start(f32[2,16]{1,0:T(2,128)} %param.32) | copy-start | bytes 388
  194.5 73.7 %copy-start.11 = (f32[2,16]{1,0:T(2,128)S(1)}, f32[2,16]{1,0:T(2,128)}, u32[]{:S(2)}) copy-start(f32[2,16]{1,0:T(2,128)} %param.30) | copy-start | bytes 388
  194.5 77.0 %copy-start.6 = (f32[58,16]{0,1:T(8,128)S(1)}, f32[58,16]{0,1:T(8,128)}, u32[]{:S(2)}) copy-start(f32[58,16]{0,1:T(8,128)} %param.27) | copy-start | bytes 11140
  194.5 77.0 %copy-start.7 = (f32[58,16]{0,1:T(8,128)S(1)}, f32[58,16]{0,1:T(8,128)}, u32[]{:S(2)}) copy-start(f32[58,16]{0,1:T(8,128)} %param.28) | copy-start | bytes 11140
  194.5 77.0 %copy-start.8 = (f32[58,16]{0,1:T(8,128)S(1)}, f32[58,16]{0,1:T(8,128)}, u32[]{:S(2)}) copy-start(f32[58,16]{0,1:T(8,128)} %param.29) | copy-start | bytes 11140
  194.6 78.3 %copy-start.1 = (f32[64,512]{1,0:T(8,128)S(1)}, f32[64,512]{1,0:T(8,128)}, u32[]{:S(2)}) copy-start(f32[64,512]{1,0:T(8,128)} %param.24) | copy-start | bytes 393220
  194.6 78.3 %copy-start.4 = (f32[64,512]{1,0:T(8,128)S(1)}, f32[64,512]{1,0:T(8,128)}, u32[]{:S(2)}) copy-start(f32[64,512]{1,0:T(8,128)} %param.25) | copy-start | bytes 393220
  194.6 78.3 %copy-start.5 = (f32[64,512]{1,0:T(8,128)S(1)}, f32[64,512]{1,0:T(8,128)}, u32[]{:S(2)}) copy-start(f32[64,512]{1,0:T(8,128)} %param.26) | copy-start | bytes 393220
  194.6 80.0 %copy-start = (f32[16,4096]{1,0:T(8,128)S(1)}, f32[16,4096]{1,0:T(8,128)}, u32[]{:S(2)}) copy-start(f32[16,4096]{1,0:T(8,128)} %param.21) | copy-start | bytes 786436
  194.6 80.0 %copy-start.2 = (f32[16,4096]{1,0:T(8,128)S(1)}, f32[16,4096]{1,0:T(8,128)}, u32[]{:S(2)}) copy-start(f32[16,4096]{1,0:T(8,128)} %param.22) | copy-start | bytes 786436
  194.6 80.0 %copy-start.3 = (f32[16,4096]{1,0:T(8,128)S(1)}, f32[16,4096]{1,0:T(8,128)}, u32[]{:S(2)}) copy-start(f32[16,4096]{1,0:T(8,128)} %param.23) | copy-start | bytes 786436

commit v5 on v4

--- a/solution.py
+++ b/solution.py
@@ -50,7 +50,13 @@
     return (z, y, x, 1 - c)
 
 
-def gather_kernel(wi, wo, sm, gi, go, gs, send_sem, recv_sem, own_sem):
+def square_of(lines):
+    return jnp.concatenate([lines, jnp.zeros((128 - lines.shape[0], 128), lines.dtype)], axis=0)
+
+
+def gather_kernel(
+    counts, wi_f, wo_f, kern, gain, bias, gi, go, gs, wi, wo, sm, lines, send_sem, recv_sem, own_sem
+):
     at = place()
     z, y, x, c = at
     partners = [device(*neighbour(at, 0, s)) for s in (1, 2, 3)]
@@ -58,6 +64,22 @@
     barrier = pltpu.get_barrier_semaphore()
     for partner in partners:
         pl.semaphore_signal(barrier, inc=1, device_id=partner, device_id_type=MESH_ID)
+    low = jnp.bfloat16
+    wi[...] = wi_f[...].astype(low)
+    wo[...] = wo_f[...].astype(low)
+    kept, own = kern.shape[1], kern.shape[0]
+    after_gain = kept + gain.shape[0]
+    after_bias = after_gain + bias.shape[0]
+    lines[...] = jnp.zeros_like(lines)
+    lines[kept:after_gain, 0:own] = gain[...]
+    lines[after_gain:after_bias, 0:own] = bias[...]
+    lines[after_bias : after_bias + 1, :] = jnp.full((1, 128), counts[0], jnp.int32).astype(
+        jnp.float32
+    )
+    turned = lines[...].T[0:own, :]
+    lines[0:own, :] = turned
+    lines[0:own, 0:kept] = kern[...]
+    sm[...] = lines[0:own, :].astype(low)
     pl.semaphore_wait(barrier, len(partners))
 
     width = wi.shape[1]
@@ -151,25 +173,26 @@
         copy.wait()
 
 
-def gather_all(in_copy, out_copy, small):
+def gather_all(counts, in_mats, out_mat, kern, gain, bias):
+    low = jnp.bfloat16
     hbm = pl.BlockSpec(memory_space=pl.ANY)
+    vmem = pl.BlockSpec(memory_space=pltpu.VMEM)
+    shapes = (in_mats.shape, out_mat.shape, (SMALL_ROWS, 128))
     return pl.pallas_call(
         gather_kernel,
-        out_shape=(
-            jax.ShapeDtypeStruct((32,) + in_copy.shape, in_copy.dtype),
-            jax.ShapeDtypeStruct((32,) + out_copy.shape, out_copy.dtype),
-            jax.ShapeDtypeStruct((32,) + small.shape, small.dtype),
-        ),
-        in_specs=[hbm] * 3,
+        out_shape=tuple(jax.ShapeDtypeStruct((32,) + shape, low) for shape in shapes),
+        in_specs=[pl.BlockSpec(memory_space=pltpu.SMEM)] + [vmem] * 5,
         out_specs=(hbm,) * 3,
-        scratch_shapes=[
+        scratch_shapes=[pltpu.VMEM(shape, low) for shape in shapes]
+        + [
+            pltpu.VMEM((128, 128), jnp.float32),
             pltpu.SemaphoreType.DMA((4, 32)),
             pltpu.SemaphoreType.DMA((4, 32)),
             pltpu.SemaphoreType.DMA((4,)),
         ],
         compiler_params=pltpu.CompilerParams(collective_id=0, has_side_effects=True),
         name="gather_all",
-    )(in_copy, out_copy, small)
+    )(counts, in_mats, out_mat, kern, gain, bias)
 
 
 def add_low(left, right):
@@ -178,7 +201,7 @@
 
 IN_CHUNKS = 4
 OUT_CHUNKS = 2
-LAGS = (1, 3, 5, 7)
+LAGS = (2, 4, 6, 8)
 
 
 def reduce_kernel(
@@ -447,6 +470,77 @@
     )(*arrays, small.reshape(4, 2, 2, 2, SMALL_ROWS, 128))
 
 
+def update_kernel(
+    num_tokens,
+    fi, fo, fs, fq, all_small,
+    wi, wi_m, wi_v, wo, wo_m, wo_v, kern, kern_m, kern_v, gain, gain_m, gain_v, bias, bias_m, bias_v,
+    norm_o,
+    wi_o, wi_m_o, wi_v_o, wi_low, wo_o, wo_m_o, wo_v_o, wo_low,
+    kern_o, kern_m_o, kern_v_o, kern_low, gain_o, gain_m_o, gain_v_o, gain_low,
+    bias_o, bias_m_o, bias_v_o, bias_low,
+):
+    total = jnp.sum(fq[...], axis=0, keepdims=True)
+    total = jnp.sum(total, axis=1, keepdims=True)
+    kept = kern.shape[1]
+    after_gain = kept + gain.shape[0]
+    after_bias = after_gain + bias.shape[0]
+    lives = jnp.sum(all_small[...].astype(jnp.float32), axis=0)[0:1, after_bias : after_bias + 1]
+    scale = 1.0 / (lives * num_tokens)
+    norm = jnp.sqrt(total) * scale
+    norm_o[...] = norm
+    clip = jnp.minimum(1.0, 1.0 / (norm + 1e-06))
+
+    def update(group, state, outs, where, gradient):
+        news = adamw_update(
+            *(ref[where] for ref in state), gradient * scale, clip, RATES[group], DECAYS[group]
+        )
+        for ref, new in zip(outs, news):
+            ref[where] = new
+
+    def update_in(k, carry):
+        where = (slice(None), pl.ds(pl.multiple_of(k * D, D), D))
+        update(0, (wi, wi_m, wi_v), (wi_o, wi_m_o, wi_v_o, wi_low), where, fi[where])
+        return carry
+
+    lax.fori_loop(0, fi.shape[1] // D, update_in, 0)
+
+    def update_out(k, carry):
+        where = (pl.ds(pl.multiple_of(k * 16, 16), 16), slice(None))
+        update(1, (wo, wo_m, wo_v), (wo_o, wo_m_o, wo_v_o, wo_low), where, fo[where])
+        return carry
+
+    lax.fori_loop(0, fo.shape[0] // 16, update_out, 0)
+    own = kern.shape[0]
+    turned = square_of(fs[...]).T
+    update(2, (kern, kern_m, kern_v), (kern_o, kern_m_o, kern_v_o, kern_low), ..., fs[:, 0:kept])
+    update(
+        3, (gain, gain_m, gain_v), (gain_o, gain_m_o, gain_v_o, gain_low), ...,
+        turned[kept:after_gain, 0:own],
+    )
+    update(
+        4, (bias, bias_m, bias_v), (bias_o, bias_m_o, bias_v_o, bias_low), ...,
+        turned[after_gain:after_bias, 0:own],
+    )
+
+
+def update_all(sums, all_small, state, num_tokens):
+    low, full = jnp.bfloat16, jnp.float32
+    vmem = pl.BlockSpec(memory_space=pltpu.VMEM)
+    return pl.pallas_call(
+        functools.partial(update_kernel, float(num_tokens)),
+        out_shape=(jax.ShapeDtypeStruct((1, 1), full),)
+        + tuple(
+            jax.ShapeDtypeStruct(master.shape, kind)
+            for master in state[::3]
+            for kind in (full, full, full, low)
+        ),
+        in_specs=[vmem] * 20,
+        out_specs=(vmem,) * 21,
+        compiler_params=pltpu.CompilerParams(vmem_limit_bytes=32 << 20),
+        name="update_all",
+    )(*sums, all_small, *state)
+
+
 def cross_rows(left, right):
     return lax.dot_general(
         left, right, (((0,), (0,)), ((), ())), preferred_element_type=jnp.float32
@@ -1005,6 +1099,27 @@
     biases_v,
     special,
 ):
+    if special:
+        all_in, all_out, all_small = gather_all(counts, in_mats, out_mat, kernels.T, gains, biases)
+        block_out, input_grad, factors, grad_small = compute(
+            images,
+            cotangent,
+            counts,
+            all_in.reshape(-1, in_mats.shape[1]),
+            all_out.reshape(-1, out_mat.shape[1]),
+            all_small.reshape(-1, 128),
+        )
+        sums = reduce_all(*factors, grad_small)
+        state = (
+            in_mats, in_mats_m, in_mats_v,
+            out_mat, out_mat_m, out_mat_v,
+            kernels.T, kernels_m.T, kernels_v.T,
+            gains, gains_m, gains_v,
+            biases, biases_m, biases_v,
+        )
+        norm, *news = update_all(sums, all_small, state, images.shape[1])
+        news[8:12] = [part.T for part in news[8:12]]
+        return (block_out, input_grad, norm.reshape(()), *news)
     in_copy = in_mats.astype(jnp.bfloat16)
     out_copy = out_mat.astype(jnp.bfloat16)
     shards = (kernels, gains, biases)
@@ -1013,13 +1128,10 @@
     count_row = jnp.broadcast_to(counts.astype(jnp.float32)[:, None], (1, kernels.shape[1]))
     rows = jnp.concatenate(shards + (count_row,), axis=0)
     small = jnp.pad(rows, ((0, 128 - used - 1), (0, 0))).T.astype(jnp.bfloat16)
-    if special:
-        all_in, all_out, all_small = gather_all(in_copy, out_copy, small)
-    else:
-        all_in, all_out, all_small = (
-            lax.all_gather(part, ("wide", "narrow"), axis=0, tiled=True)
-            for part in (in_copy, out_copy, small)
-        )
+    all_in, all_out, all_small = (
+        lax.all_gather(part, ("wide", "narrow"), axis=0, tiled=True)
+        for part in (in_copy, out_copy, small)
+    )
     all_small = all_small.reshape(-1, small.shape[0], 128)
     live_total = jnp.sum(all_small[:, 0, used].astype(jnp.float32)) * images.shape[1]
     scale_factor = 1.0 / live_total
@@ -1031,25 +1143,18 @@
         all_out.reshape(-1, out_copy.shape[1]),
         all_small.reshape(-1, 128),
     )
-    if special:
-        sum_in, sum_out, sum_small, squares = reduce_all(*factors, grad_small)
-        total_squares = jnp.sum(squares)
-    else:
-        n1, gq, attended, gp, n2, gh, act, gf = factors
-        grad_in = jnp.concatenate(
-            [cross_rows(n1, gq), cross_rows(attended, gp), cross_rows(n2, gh)], axis=1
-        )
-        grad_fc2 = cross_rows(act, gf)
-        sum_in, sum_out, sum_small = (
-            lax.psum_scatter(
-                part.astype(jnp.float32), ("wide", "narrow"), scatter_dimension=0, tiled=True
-            )
-            for part in (grad_in, grad_fc2, grad_small)
-        )
-        total_squares = lax.psum(
-            sum(jnp.sum(part * part) for part in (sum_in, sum_out, sum_small)),
-            ("wide", "narrow"),
-        )
+    n1, gq, attended, gp, n2, gh, act, gf = factors
+    grad_in = jnp.concatenate(
+        [cross_rows(n1, gq), cross_rows(attended, gp), cross_rows(n2, gh)], axis=1
+    )
+    grad_fc2 = cross_rows(act, gf)
+    sum_in, sum_out, sum_small = (
+        lax.psum_scatter(part, ("wide", "narrow"), scatter_dimension=0, tiled=True)
+        for part in (grad_in, grad_fc2, grad_small)
+    )
+    total_squares = lax.psum(
+        sum(jnp.sum(part * part) for part in (sum_in, sum_out, sum_small)), ("wide", "narrow")
+    )
     rows = sum_small.T
     summed = (
         sum_in,

time: 278 us -> 259 us (0.932)
  other arithmetic: 14.2 us -> 0 us
  local copies, waits for them, and re-layouts: 7.35 us -> 3.32 us
    convert_element_type x7 -> x0, other arithmetic: 9.8 us -> none  [the longest x5 6.64 us: adamw_update(): return (master_new, first_new, second_new, master_new.astype(jnp.bfloat16))]
    pallas_call x1 -> x2, Pallas kernels: 40.4 us -> 44 us  [the longest x1 41.2 us: gather_all(): pl.pallas_call(gather_kernel, out_shape=tuple((jax.ShapeDtypeStruct((32,)...]
    unnamed x40, local copies, waits for them, and re-layouts: 6.32 us -> 3.32 us
    reduce_sum x2 -> x0, other arithmetic: 2.84 us -> none  [the longest x1 1.55 us: local(): jnp.sum(all_small[:, 0, used].astype(jnp.float32)) * images.shape[1]]
where the time goes in v5:
time: 259 us; the launch traced here: 258 us
  Pallas kernels  253 us (98%)
  local copies, waits for them, and re-layouts  3.32 us (1%)
    pallas_call x1, Pallas kernels, compute(): forward(counts, images, cotangent, w_in, w_out, small)  87.6 us
    pallas_call x1, Pallas kernels, reduce_all(): pl.pallas_call(reduce_kernel, out_shape=(jax.ShapeDtypeStruct((rows_in, w...  62.9 us
    pallas_call x1, Pallas kernels, compute(): backward(w_in, small, cols, hcols, gx, hat, scale, q, k, v, cv, xt)  59 us
    pallas_call x1, Pallas kernels, gather_all(): pl.pallas_call(gather_kernel, out_shape=tuple((jax.ShapeDtypeStruct((32,)...  41.2 us

profile of v5, /device:TPU:0, one launch (start us, length us, event | category | flops | bytes accessed | tf_op | source)
XLA Modules:
  0.0 258.5 jit_solution(1018856849318941972)
XLA Ops:
  1.3 41.2 %gather_all.1 = (bf16[32,16,4096]{2,1,0:T(8,128)(2,1)}, bf16[32,64,512]{2,1,0:T(8,128)(2,1)}, bf16[32,16,128]{2,1,0:T(8,128)(2,1)}) custom-call(s32[1]{0:T(128)S(6)} %copy.41.counts, f32[16,4096]{1,0:T(8,128)} %wi.1, f32[64,512]{1,0:T(8,128)} %wo.1, f32[16,58]{1,0:T(8,128)} %bitcast.14, f32[2,16]{1,0:T(2,128)} %gain.3, f32[12,16]{1,0:T(8,128)} %bias.3), custom_call_target="tpu_custom_call" | custom-call | tf_op jit(solution)/shard_map/gather_all/pallas_call | solution.py:181
  42.5 87.6 %forward.1 = (bf16[34,50,512]{2,1,0:T(8,128)(2,1)}, bf16[2000,2048]{1,0:T(8,128)(2,1)}, bf16[2000,2048]{1,0:T(8,128)(2,1)}, bf16[2000,512]{1,0:T(8,128)(2,1)}, b...) custom-call(s32[1]{0:T(128)S(6)} %copy.41.counts, ...), custom_call_target="tpu_custom_call" | custom-call | tf_op jit(solution)/shard_map/forward/pallas_call | solution.py:1032
  130.1 59.0 %backward.1 = (f32[34,50,512]{2,1,0:T(8,128)}, bf16[2000,1536]{1,0:T(8,128)(2,1)}, f32[512,128]{1,0:T(8,128)}) custom-call(bf16[512,4096]{1,0:T(8,128)(2,1)} %bitcast.19, bf16[512,128]{1,0:T(8,128)(2,1)} %bitcast.13, f32[4,8,512]{2,1,0:T(8,128)} %get-tuple-element.76.cols_in, f32[8,2048]{1,0:T(8,128)} %get-tuple-element.77.hcols_in, ...), custom_call_target="tpu_custom_call" | custom-call | tf_op jit(solution)/shard_map/backward/pallas_call | solution.py:1065
  189.0 0.0 copy-start
  189.1 0.0 copy-start.1
  189.1 0.0 copy-start.2
  189.1 0.0 copy-start.3
  189.1 0.0 copy-start.4
  189.1 0.0 copy-start.6
  189.1 0.0 copy-start.7
  189.1 0.0 copy-start.9
  189.1 0.0 copy-start.10
  189.1 0.0 copy-start.11
  189.2 0.0 copy-start.12
  189.2 0.0 copy-start.13
  189.2 0.0 copy-start.14
  189.2 0.0 copy-start.17
  189.2 0.0 copy-start.18
  189.2 0.0 copy-start.19
  189.2 62.9 %reduce_all.1 = (f32[16,4096]{1,0:T(8,128)}, f32[64,512]{1,0:T(8,128)}, f32[16,128]{1,0:T(8,128)}, f32[8,128]{1,0:T(8,128)}) custom-call(bf16[2000,512]{1,0:T(8,128)(2,1)} %get-tuple-element.87.n1_h, bf16[2000,1536]{1,0:T(8,128)(2,1)} %get-tuple-element.88.gq_h, bf16[2000,512]{1,0:T(8,128)(2,1)} %get-tuple-element.89.at_h, ...), custom_call_target="tpu_custom_call" | custom-call | tf_op jit(solution)/shard_map/reduce_all/pallas_call | solution.py:455
  252.2 0.0 copy-done
  252.2 0.0 copy-done.1
  252.2 0.0 copy-done.2
  252.2 0.0 copy-done.3
  252.2 0.0 copy-done.4
  252.2 0.0 copy-done.6
  252.2 0.0 copy-done.7
  252.2 0.0 copy-done.9
  252.2 0.0 copy-done.10
  252.2 0.0 copy-done.11
  252.3 0.0 copy-done.12
  252.3 0.0 copy-done.13
  252.3 0.0 copy-done.14
  252.3 0.0 copy-done.17
  252.3 0.0 copy-done.18
  252.3 0.0 copy-done.19
  252.3 0.0 copy-start.5
  252.3 0.9 copy-done.5
  253.3 0.0 copy-start.8
  253.3 0.9 copy-done.8
  254.2 0.0 copy-start.15
  254.2 0.7 copy-done.15
  254.9 0.0 copy-start.16
  254.9 0.7 copy-done.16
  255.5 2.8 %update_all.1 = (f32[1,1]{1,0:T(1,128)}, f32[16,4096]{1,0:T(8,128)}, f32[16,4096]{1,0:T(8,128)}, f32[16,4096]{1,0:T(8,128)}, bf16[16,4096]{1,0:T(8,128)(2,1)}, /...) custom-call(f32[16,4096]{1,0:T(8,128)S(1)} %copy-done.5, ...), custom_call_target="tpu_custom_call" | custom-call | tf_op jit(solution)/shard_map/update_all/pallas_call | solution.py:529
Async XLA Ops:
  189.0 63.1 %copy-start = (bf16[32,16,128]{2,1,0:T(8,128)(2,1)S(1)}, bf16[32,16,128]{2,1,0:T(8,128)(2,1)}, u32[]{:S(2)}) copy-start(bf16[32,16,128]{2,1,0:T(8,128)(2,1)} %get-tuple-element.74.all_small) | copy-start | bytes 393220
  189.1 63.1 %copy-start.1 = (f32[16,4096]{1,0:T(8,128)S(1)}, f32[16,4096]{1,0:T(8,128)}, u32[]{:S(2)}) copy-start(f32[16,4096]{1,0:T(8,128)} %wi.1) | copy-start | bytes 786436
  189.1 63.1 %copy-start.2 = (f32[64,512]{1,0:T(8,128)S(1)}, f32[64,512]{1,0:T(8,128)}, u32[]{:S(2)}) copy-start(f32[64,512]{1,0:T(8,128)} %wo.1) | copy-start | bytes 393220
  189.1 63.1 %copy-start.3 = (f32[16,4096]{1,0:T(8,128)S(1)}, f32[16,4096]{1,0:T(8,128)}, u32[]{:S(2)}) copy-start(f32[16,4096]{1,0:T(8,128)} %wi_m.1) | copy-start | bytes 786436
  189.1 63.1 %copy-start.4 = (f32[16,4096]{1,0:T(8,128)S(1)}, f32[16,4096]{1,0:T(8,128)}, u32[]{:S(2)}) copy-start(f32[16,4096]{1,0:T(8,128)} %wi_v.1) | copy-start | bytes 786436
  189.1 63.1 %copy-start.6 = (f32[64,512]{1,0:T(8,128)S(1)}, f32[64,512]{1,0:T(8,128)}, u32[]{:S(2)}) copy-start(f32[64,512]{1,0:T(8,128)} %wo_m.1) | copy-start | bytes 393220
  189.1 63.1 %copy-start.7 = (f32[64,512]{1,0:T(8,128)S(1)}, f32[64,512]{1,0:T(8,128)}, u32[]{:S(2)}) copy-start(f32[64,512]{1,0:T(8,128)} %wo_v.1) | copy-start | bytes 393220
  189.1 63.1 %copy-start.9 = (f32[58,16]{0,1:T(8,128)S(1)}, f32[58,16]{0,1:T(8,128)}, u32[]{:S(2)}) copy-start(f32[58,16]{0,1:T(8,128)} %param.27) | copy-start | bytes 11140
  189.1 63.1 %copy-start.10 = (f32[12,16]{1,0:T(8,128)S(1)}, f32[12,16]{1,0:T(8,128)}, u32[]{:S(2)}) copy-start(f32[12,16]{1,0:T(8,128)} %bias.3) | copy-start | bytes 2308
  189.1 63.1 %copy-start.11 = (f32[58,16]{0,1:T(8,128)S(1)}, f32[58,16]{0,1:T(8,128)}, u32[]{:S(2)}) copy-start(f32[58,16]{0,1:T(8,128)} %param.28) | copy-start | bytes 11140
  189.2 63.1 %copy-start.12 = (f32[58,16]{0,1:T(8,128)S(1)}, f32[58,16]{0,1:T(8,128)}, u32[]{:S(2)}) copy-start(f32[58,16]{0,1:T(8,128)} %param.29) | copy-start | bytes 11140
  189.2 63.1 %copy-start.13 = (f32[12,16]{1,0:T(8,128)S(1)}, f32[12,16]{1,0:T(8,128)}, u32[]{:S(2)}) copy-start(f32[12,16]{1,0:T(8,128)} %bias_m.1) | copy-start | bytes 2308
  189.2 63.1 %copy-start.14 = (f32[12,16]{1,0:T(8,128)S(1)}, f32[12,16]{1,0:T(8,128)}, u32[]{:S(2)}) copy-start(f32[12,16]{1,0:T(8,128)} %bias_v.1) | copy-start | bytes 2308
  189.2 63.1 %copy-start.17 = (f32[2,16]{1,0:T(2,128)S(1)}, f32[2,16]{1,0:T(2,128)}, u32[]{:S(2)}) copy-start(f32[2,16]{1,0:T(2,128)} %gain.3) | copy-start | bytes 388
  189.2 63.1 %copy-start.18 = (f32[2,16]{1,0:T(2,128)S(1)}, f32[2,16]{1,0:T(2,128)}, u32[]{:S(2)}) copy-start(f32[2,16]{1,0:T(2,128)} %gain_m.1) | copy-start | bytes 388
  189.2 63.1 %copy-start.19 = (f32[2,16]{1,0:T(2,128)S(1)}, f32[2,16]{1,0:T(2,128)}, u32[]{:S(2)}) copy-start(f32[2,16]{1,0:T(2,128)} %gain_v.1) | copy-start | bytes 388
  252.3 1.0 copy-start.5
  253.3 0.9 copy-start.8
  254.2 0.7 copy-start.15
  254.9 0.7 copy-start.16

commit v6 on v5

--- a/solution.py
+++ b/solution.py
@@ -679,7 +679,7 @@
         body(pl.ds(pl.multiple_of(k * CHUNK * SIDE, 16), CHUNK * SIDE))
         return carry
 
-    lax.fori_loop(0, 50 // CHUNK, step, 0)
+    lax.fori_loop(0, 50 // CHUNK, step, 0, unroll=True)
 
 
 def normalise(values):

time: 259 us -> 236 us (0.911)
  Pallas kernels: 253 us -> 231 us
    pallas_call x1, Pallas kernels: 87.6 us -> 67.6 us  [compute(): forward(counts, images, cotangent, w_in, w_out, small)]
    pallas_call x1, Pallas kernels: 59 us -> 56.2 us  [compute(): backward(w_in, small, cols, hcols, gx, hat, scale, q, k, v, cv, xt)]
where the time goes in v6:
time: 236 us
  Pallas kernels  231 us (98%)
  local copies, waits for them, and re-layouts  3.32 us (1%)
    pallas_call x1, Pallas kernels, compute(): forward(counts, images, cotangent, w_in, w_out, small)  67.6 us
    pallas_call x1, Pallas kernels, reduce_all(): pl.pallas_call(reduce_kernel, out_shape=(jax.ShapeDtypeStruct((rows_in, w...  63.2 us
    pallas_call x1, Pallas kernels, compute(): backward(w_in, small, cols, hcols, gx, hat, scale, q, k, v, cv, xt)  56.2 us
    pallas_call x1, Pallas kernels, gather_all(): pl.pallas_call(gather_kernel, out_shape=tuple((jax.ShapeDtypeStruct((32,)...  41.2 us

profile of v6, /device:TPU:0, one launch (start us, length us, event | category | flops | bytes accessed | tf_op | source)
XLA Modules:
  0.0 236.0 jit_solution(11806511853421924907)
XLA Ops:
  1.3 41.2 %gather_all.1 = (bf16[32,16,4096]{2,1,0:T(8,128)(2,1)}, bf16[32,64,512]{2,1,0:T(8,128)(2,1)}, bf16[32,16,128]{2,1,0:T(8,128)(2,1)}) custom-call(s32[1]{0:T(128)S(6)} %copy.41.counts, f32[16,4096]{1,0:T(8,128)} %wi.1, f32[64,512]{1,0:T(8,128)} %wo.1, f32[16,58]{1,0:T(8,128)} %bitcast.14, f32[2,16]{1,0:T(2,128)} %gain.3, f32[12,16]{1,0:T(8,128)} %bias.3), custom_call_target="tpu_custom_call" | custom-call | tf_op jit(solution)/shard_map/gather_all/pallas_call | solution.py:181
  42.5 67.6 %forward.1 = (bf16[34,50,512]{2,1,0:T(8,128)(2,1)}, bf16[2000,2048]{1,0:T(8,128)(2,1)}, bf16[2000,2048]{1,0:T(8,128)(2,1)}, bf16[2000,512]{1,0:T(8,128)(2,1)}, b...) custom-call(s32[1]{0:T(128)S(6)} %copy.41.counts, ...), custom_call_target="tpu_custom_call" | custom-call | tf_op jit(solution)/shard_map/forward/pallas_call | solution.py:1032
  110.2 56.2 %backward.1 = (f32[34,50,512]{2,1,0:T(8,128)}, bf16[2000,1536]{1,0:T(8,128)(2,1)}, f32[512,128]{1,0:T(8,128)}) custom-call(bf16[512,4096]{1,0:T(8,128)(2,1)} %bitcast.19, bf16[512,128]{1,0:T(8,128)(2,1)} %bitcast.13, f32[4,8,512]{2,1,0:T(8,128)} %get-tuple-element.76.cols_in, f32[8,2048]{1,0:T(8,128)} %get-tuple-element.77.hcols_in, ...), custom_call_target="tpu_custom_call" | custom-call | tf_op jit(solution)/shard_map/backward/pallas_call | solution.py:1065
  166.4 0.0 copy-start
  166.4 0.0 copy-start.1
  166.4 0.0 copy-start.2
  166.4 0.0 copy-start.3
  166.4 0.0 copy-start.4
  166.4 0.0 copy-start.6
  166.4 0.0 copy-start.7
  166.4 0.0 copy-start.9
  166.5 0.0 copy-start.10
  166.5 0.0 copy-start.11
  166.5 0.0 copy-start.12
  166.5 0.0 copy-start.13
  166.5 0.0 copy-start.14
  166.5 0.0 copy-start.17
  166.5 0.0 copy-start.18
  166.5 0.0 copy-start.19
  166.6 63.2 %reduce_all.1 = (f32[16,4096]{1,0:T(8,128)}, f32[64,512]{1,0:T(8,128)}, f32[16,128]{1,0:T(8,128)}, f32[8,128]{1,0:T(8,128)}) custom-call(bf16[2000,512]{1,0:T(8,128)(2,1)} %get-tuple-element.87.n1_h, bf16[2000,1536]{1,0:T(8,128)(2,1)} %get-tuple-element.88.gq_h, bf16[2000,512]{1,0:T(8,128)(2,1)} %get-tuple-element.89.at_h, ...), custom_call_target="tpu_custom_call" | custom-call | tf_op jit(solution)/shard_map/reduce_all/pallas_call | solution.py:455
  229.7 0.0 copy-done
  229.7 0.0 copy-done.1
  229.7 0.0 copy-done.2
  229.7 0.0 copy-done.3
  229.8 0.0 copy-done.4
  229.8 0.0 copy-done.6
  229.8 0.0 copy-done.7
  229.8 0.0 copy-done.9
  229.8 0.0 copy-done.10
  229.8 0.0 copy-done.11
  229.8 0.0 copy-done.12
  229.8 0.0 copy-done.13
  229.8 0.0 copy-done.14
  229.8 0.0 copy-done.17
  229.9 0.0 copy-done.18
  229.9 0.0 copy-done.19
  229.9 0.0 copy-start.5
  229.9 0.9 copy-done.5
  230.8 0.0 copy-start.8
  230.8 0.9 copy-done.8
  231.7 0.0 copy-start.15
  231.7 0.7 copy-done.15
  232.4 0.0 copy-start.16
  232.4 0.7 copy-done.16
  233.1 2.8 %update_all.1 = (f32[1,1]{1,0:T(1,128)}, f32[16,4096]{1,0:T(8,128)}, f32[16,4096]{1,0:T(8,128)}, f32[16,4096]{1,0:T(8,128)}, bf16[16,4096]{1,0:T(8,128)(2,1)}, /...) custom-call(f32[16,4096]{1,0:T(8,128)S(1)} %copy-done.5, ...), custom_call_target="tpu_custom_call" | custom-call | tf_op jit(solution)/shard_map/update_all/pallas_call | solution.py:529
Async XLA Ops:
  166.4 63.4 %copy-start = (bf16[32,16,128]{2,1,0:T(8,128)(2,1)S(1)}, bf16[32,16,128]{2,1,0:T(8,128)(2,1)}, u32[]{:S(2)}) copy-start(bf16[32,16,128]{2,1,0:T(8,128)(2,1)} %get-tuple-element.74.all_small) | copy-start | bytes 393220
  166.4 63.4 %copy-start.1 = (f32[16,4096]{1,0:T(8,128)S(1)}, f32[16,4096]{1,0:T(8,128)}, u32[]{:S(2)}) copy-start(f32[16,4096]{1,0:T(8,128)} %wi.1) | copy-start | bytes 786436
  166.4 63.4 %copy-start.2 = (f32[64,512]{1,0:T(8,128)S(1)}, f32[64,512]{1,0:T(8,128)}, u32[]{:S(2)}) copy-start(f32[64,512]{1,0:T(8,128)} %wo.1) | copy-start | bytes 393220
  166.4 63.3 %copy-start.3 = (f32[16,4096]{1,0:T(8,128)S(1)}, f32[16,4096]{1,0:T(8,128)}, u32[]{:S(2)}) copy-start(f32[16,4096]{1,0:T(8,128)} %wi_m.1) | copy-start | bytes 786436
  166.4 63.3 %copy-start.4 = (f32[16,4096]{1,0:T(8,128)S(1)}, f32[16,4096]{1,0:T(8,128)}, u32[]{:S(2)}) copy-start(f32[16,4096]{1,0:T(8,128)} %wi_v.1) | copy-start | bytes 786436
  166.4 63.3 %copy-start.6 = (f32[64,512]{1,0:T(8,128)S(1)}, f32[64,512]{1,0:T(8,128)}, u32[]{:S(2)}) copy-start(f32[64,512]{1,0:T(8,128)} %wo_m.1) | copy-start | bytes 393220
  166.4 63.3 %copy-start.7 = (f32[64,512]{1,0:T(8,128)S(1)}, f32[64,512]{1,0:T(8,128)}, u32[]{:S(2)}) copy-start(f32[64,512]{1,0:T(8,128)} %wo_v.1) | copy-start | bytes 393220
  166.4 63.3 %copy-start.9 = (f32[58,16]{0,1:T(8,128)S(1)}, f32[58,16]{0,1:T(8,128)}, u32[]{:S(2)}) copy-start(f32[58,16]{0,1:T(8,128)} %param.27) | copy-start | bytes 11140
  166.5 63.3 %copy-start.10 = (f32[12,16]{1,0:T(8,128)S(1)}, f32[12,16]{1,0:T(8,128)}, u32[]{:S(2)}) copy-start(f32[12,16]{1,0:T(8,128)} %bias.3) | copy-start | bytes 2308
  166.5 63.3 %copy-start.11 = (f32[58,16]{0,1:T(8,128)S(1)}, f32[58,16]{0,1:T(8,128)}, u32[]{:S(2)}) copy-start(f32[58,16]{0,1:T(8,128)} %param.28) | copy-start | bytes 11140
  166.5 63.3 %copy-start.12 = (f32[58,16]{0,1:T(8,128)S(1)}, f32[58,16]{0,1:T(8,128)}, u32[]{:S(2)}) copy-start(f32[58,16]{0,1:T(8,128)} %param.29) | copy-start | bytes 11140
  166.5 63.3 %copy-start.13 = (f32[12,16]{1,0:T(8,128)S(1)}, f32[12,16]{1,0:T(8,128)}, u32[]{:S(2)}) copy-start(f32[12,16]{1,0:T(8,128)} %bias_m.1) | copy-start | bytes 2308
  166.5 63.3 %copy-start.14 = (f32[12,16]{1,0:T(8,128)S(1)}, f32[12,16]{1,0:T(8,128)}, u32[]{:S(2)}) copy-start(f32[12,16]{1,0:T(8,128)} %bias_v.1) | copy-start | bytes 2308
  166.5 63.3 %copy-start.17 = (f32[2,16]{1,0:T(2,128)S(1)}, f32[2,16]{1,0:T(2,128)}, u32[]{:S(2)}) copy-start(f32[2,16]{1,0:T(2,128)} %gain.3) | copy-start | bytes 388
  166.5 63.3 %copy-start.18 = (f32[2,16]{1,0:T(2,128)S(1)}, f32[2,16]{1,0:T(2,128)}, u32[]{:S(2)}) copy-start(f32[2,16]{1,0:T(2,128)} %gain_m.1) | copy-start | bytes 388
  166.5 63.3 %copy-start.19 = (f32[2,16]{1,0:T(2,128)S(1)}, f32[2,16]{1,0:T(2,128)}, u32[]{:S(2)}) copy-start(f32[2,16]{1,0:T(2,128)} %gain_v.1) | copy-start | bytes 388
  229.9 1.0 copy-start.5
  230.8 0.9 copy-start.8
  231.7 0.7 copy-start.15
  232.4 0.7 copy-start.16
